TPU v7x, 32 devices: a whole 2x2x4 slice. The times are simulated.
32 devices in a mesh: groups: 2 (over x), seq: 16 (over z, y, core).
Axes of the slice: x: 2, y: 2, z: 4, core: 2. Of those that a mesh axis runs over, the one named last changes fastest.
Arguments:
- query_in: bfloat16 [4096, 4096], P(('groups', 'seq')), parts along dimension 0, may hold values from -6 to 6
- key_in: bfloat16 [4096, 4096], P(('groups', 'seq')), parts along dimension 0, may hold values from -6 to 6
- value_in: bfloat16 [4096, 4096], P(('groups', 'seq')), parts along dimension 0, may hold values from -6 to 6
- long_filter: bfloat16 [2048, 4096], P('seq'), may hold values from -0.4 to 0.4
- short_weight: float32 [3, 3, 4096], replicated, may hold values from -3 to 3
- skip_gain: float32 [4096], replicated, may hold values from 0.5 to 1.5
Outputs:
- gated_out: bfloat16 [4096, 4096], P(('groups', 'seq')), parts along dimension 0
There are 2 independent parts, one for each index of `groups`. A program takes and returns all parts, laid end to end along the dimension named above; an argument that names none is the same for every part. Nothing has to cross between parts.
All inputs are finite; a program needn't handle non-finite values.
Results may differ from a plain program's by a relative error of at most 0.0052.
Values may be sent and summed in bfloat16 or wider, within the bound.
No kernel may reach another device: no remote copies, remote signals or barrier semaphores. Data moves between devices by JAX's collectives and lax.ppermute only.
A program may use at most 128 MiB of HBM per device.

v0:
```python
import math

import jax
import jax.numpy as jnp
from jax import lax
from jax.sharding import PartitionSpec as P

PRECISE = lax.Precision.HIGHEST


def from_behind(value, axis, steps):
    count = lax.axis_size(axis)
    initial, last = (max(0, -steps), min(count, count - steps))
    return lax.ppermute(value, axis, [(source, source + steps) for source in range(initial, last)])


def featurize(own_rows, earlier, taps_weight):
    rim_rows = earlier.shape[0]
    row_count = own_rows.shape[0]
    extended = jnp.concatenate([earlier, own_rows], axis=0).astype(jnp.float32)
    result = jnp.zeros(own_rows.shape, jnp.float32)
    for offset in range(rim_rows + 1):
        result = (
            result
            + taps_weight[offset] * extended[rim_rows - offset : rim_rows - offset + row_count]
        )
    return result


def phase_pair(left_index, right_index, modulus):
    product_index = left_index[:, None] * right_index[None, :] % modulus
    angle = product_index.astype(jnp.float32) * (2.0 * math.pi / modulus)
    return (jnp.cos(angle), jnp.sin(angle))


def block_forward(real_blocks):
    blocks = real_blocks.shape[0]
    flat_values = real_blocks.reshape(blocks, -1)
    cosine_table, sine_table = phase_pair(
        jnp.arange(2 * blocks, dtype=jnp.int32), jnp.arange(blocks, dtype=jnp.int32), 2 * blocks
    )
    joint_table = jnp.concatenate([cosine_table, -sine_table], axis=0)
    stacked = jnp.dot(joint_table, flat_values, precision=PRECISE)
    return stacked.reshape((2, 2 * blocks) + real_blocks.shape[1:])


def apply_twiddle(stacked, freq_index, row_index, modulus, direction):
    cosine_table, sine_table = phase_pair(freq_index, row_index, modulus)
    cosine_table = cosine_table[:, :, None]
    sine_table = direction * sine_table[:, :, None]
    out_real = stacked[0] * cosine_table + stacked[1] * sine_table
    out_imaginary = stacked[1] * cosine_table - stacked[0] * sine_table
    return jnp.stack([out_real, out_imaginary])


def row_transform(stacked, direction):
    length = stacked.shape[2]
    row_index = jnp.arange(length, dtype=jnp.int32)
    cosine_table, sine_table = phase_pair(row_index, row_index, length)
    sine_table = direction * sine_table
    upper_table = jnp.stack([cosine_table, sine_table], axis=1)
    lower_table = jnp.stack([-sine_table, cosine_table], axis=1)
    full_table = jnp.stack([upper_table, lower_table])
    return jnp.einsum("ymxn,xknc->ykmc", full_table, stacked, precision=PRECISE)


def block_inverse(stacked, factor):
    double_count = stacked.shape[1]
    blocks = double_count // 2
    cosine_table, sine_table = phase_pair(
        jnp.arange(blocks, dtype=jnp.int32), jnp.arange(double_count, dtype=jnp.int32), double_count
    )
    joint_table = jnp.concatenate([cosine_table, -sine_table], axis=1)
    flat_values = stacked.reshape(2 * double_count, -1)
    result = jnp.dot(joint_table, flat_values, precision=PRECISE) * factor
    return result.reshape((blocks,) + stacked.shape[2:])


def spectral_product(stacked, width):
    spectra = row_transform(stacked, 1.0)
    data_real = spectra[0, ..., :width]
    kernel_real = spectra[0, ..., width:]
    data_imaginary = spectra[1, ..., :width]
    kernel_imaginary = spectra[1, ..., width:]
    joint = jnp.stack(
        [
            data_real * kernel_real - data_imaginary * kernel_imaginary,
            data_real * kernel_imaginary + data_imaginary * kernel_real,
        ]
    )
    return row_transform(joint, -1.0)


def along_rows(product, long_filter):
    blocks = lax.axis_size("seq")
    device_index = lax.axis_index("seq")
    row_count, channels = product.shape
    row_share = row_count // blocks
    full_length = 2 * blocks * row_count
    data_parts, kernel_parts = (
        lax.all_to_all(
            product.reshape(1, row_count, channels), "seq", split_axis=1, concat_axis=0, tiled=True
        ),
        lax.all_to_all(
            long_filter.reshape(1, row_count, channels),
            "seq",
            split_axis=1,
            concat_axis=0,
            tiled=True,
        ),
    )
    joined = jnp.concatenate([data_parts, kernel_parts], axis=2).astype(jnp.float32)
    freq_all = jnp.arange(2 * blocks, dtype=jnp.int32)
    local_rows = device_index * row_share + jnp.arange(row_share, dtype=jnp.int32)
    spectra = apply_twiddle(block_forward(joined), freq_all, local_rows, full_length, 1.0)
    spectra = lax.all_to_all(spectra, "seq", split_axis=1, concat_axis=2, tiled=True)
    joint = spectral_product(spectra, channels)
    own_freq = device_index * 2 + jnp.arange(2, dtype=jnp.int32)
    whole_rows = jnp.arange(row_count, dtype=jnp.int32)
    joint = apply_twiddle(joint, own_freq, whole_rows, full_length, -1.0)
    joint = lax.all_to_all(
        joint.astype(jnp.bfloat16), "seq", split_axis=2, concat_axis=1, tiled=True
    ).astype(joint.dtype)
    convolved = block_inverse(joint, 1.0 / full_length).astype(jnp.bfloat16)
    convolved = lax.all_to_all(convolved, "seq", split_axis=0, concat_axis=1, tiled=True)
    return convolved.reshape(row_count, channels)


def on_device(query_in, key_in, value_in, long_filter, short_weight, skip_gain):
    rim_rows = short_weight.shape[1] - 1
    last_rows = jnp.stack([query_in[-rim_rows:], key_in[-rim_rows:], value_in[-rim_rows:]])
    earlier = from_behind(last_rows, "seq", 1)
    q_short = featurize(query_in, earlier[0], short_weight[0])
    k_short = featurize(key_in, earlier[1], short_weight[1])
    v_short = featurize(value_in, earlier[2], short_weight[2])
    product = (k_short * v_short).astype(jnp.bfloat16)
    product_wide = lax.optimization_barrier(product).astype(jnp.float32)
    convolved = along_rows(product, long_filter)
    gated_out = q_short * (convolved.astype(jnp.float32) + skip_gain * product_wide)
    return gated_out.astype(jnp.bfloat16)


def solution(mesh):
    placed = (
        P(("groups", "seq"), None),
        P(("groups", "seq"), None),
        P(("groups", "seq"), None),
        P("seq", None),
        P(),
        P(),
    )
    return jax.shard_map(
        on_device, mesh=mesh, in_specs=placed, out_specs=P(("groups", "seq"), None), check_vma=False
    )
```

profile of v0, /device:TPU:0, one launch (start us, length us, event | category | flops | bytes accessed | tf_op | source)
XLA Modules:
  0.0 697.5 jit_solution(10720077850557271215)
XLA Ops:
  0.0 0.9 slice_bitcast_fusion.5
  0.9 0.9 slice_bitcast_fusion.3
  1.8 0.1 pad_maximum_fusion.7
  1.9 2.4 collective-permute-start
  4.2 3.6 copy.66
  7.8 0.0 copy-start.2
  7.8 0.5 broadcast.416
  8.4 7.0 %reduce = bf16[128,4096]{1,0:T(8,128)(2,1)S(1)} reduce(bf16[128,1,4096]{2,1,0:T(2,128)(2,1)S(1)} %bitcast.152, bf16[]{:T(256)} %broadcast.416), dimensions={1}, to_apply=%bitcast.138.reduce_sub_computation | reduce | bytes 2097154
  15.4 0.0 copy-start
  15.4 0.0 copy-start.1
  15.4 1.9 reshape.316
  17.3 7.5 %all-to-all-start.1 = ((bf16[16,2,16384]{2,1,0:T(2,128)(2,1)}), bf16[16,2,16384]{2,1,0:T(2,128)(2,1)}, u32[]{:S(2)}, u32[]{:S(2)}) async-start(bf16[16,2,16384]{2,1,0:T(2,128)(2,1)} %reshape.316), calls=%async_computation.1 | async-start | bytes 2097152 | tf_op jit(solution)/shard_map/all_to_all | solution.py:104
  24.8 0.0 copy-done.2
  24.8 0.1 fusion.82
  24.9 0.0 collective-permute-done
  25.0 0.0 copy-done
  25.0 0.3 maximum_convert_fusion.1
  25.3 0.3 maximum_convert_fusion.2
  25.6 1.3 fusion.18
  26.9 2.4 copy.67
  29.3 8.0 %reduce.1 = bf16[128,4096]{1,0:T(8,128)(2,1)} reduce(bf16[128,1,4096]{2,1,0:T(2,128)(2,1)S(1)} %bitcast.154, bf16[]{:T(256)} %broadcast.416), dimensions={1}, to_apply=%bitcast.139.reduce_sub_computation | reduce | bytes 2097154
  37.3 2.9 reshape.318
  40.2 7.5 %all-to-all-done.1 = bf16[16,2,16384]{2,1,0:T(2,128)(2,1)} async-done(((bf16[16,2,16384]{2,1,0:T(2,128)(2,1)}), bf16[16,2,16384]{2,1,0:T(2,128)(2,1)}, u32[]{:S(2)}, u32[]{:S(2)}) %all-to-all-start.1) | async-done | bytes 1048608 | tf_op jit(solution)/shard_map/all_to_all | solution.py:104
  47.8 7.1 %all-to-all-start = ((bf16[16,2,16384]{2,1,0:T(2,128)(2,1)}), bf16[16,2,16384]{2,1,0:T(2,128)(2,1)}, u32[]{:S(2)}, u32[]{:S(2)}) async-start(bf16[16,2,16384]{2,1,0:T(2,128)(2,1)} %reshape.318), calls=%async_computation | async-start | bytes 2097152 | tf_op jit(solution)/shard_map/all_to_all | solution.py:101
  54.9 0.1 sine_negate_fusion
  55.0 0.1 fusion.64
  55.1 4.3 reshape.317
  59.4 2.1 copy.64
  61.5 16.4 %all-to-all-done = bf16[16,2,16384]{2,1,0:T(2,128)(2,1)} async-done(((bf16[16,2,16384]{2,1,0:T(2,128)(2,1)}), bf16[16,2,16384]{2,1,0:T(2,128)(2,1)}, u32[]{:S(2)}, u32[]{:S(2)}) %all-to-all-start) | async-done | bytes 1048608 | tf_op jit(solution)/shard_map/all_to_all | solution.py:101
  77.9 4.3 reshape.319
  82.2 1.1 copy.65
  83.3 1.4 pad_maximum_fusion.2
  84.7 1.2 copy.46
  85.9 6.8 fusion.59
  92.7 6.7 fusion.81
  99.4 8.2 %copy.48 = f32[4,8,8,8192]{3,2,1,0:T(8,128)S(1)} copy(f32[4,8,8,8192]{3,1,2,0:T(8,128)} %bitcast.145) | data formatting | bytes 16777216
  107.6 8.2 %copy.47 = f32[4,8,8,8192]{3,2,1,0:T(8,128)S(1)} copy(f32[4,8,8,8192]{3,1,2,0:T(8,128)} %bitcast.144) | data formatting | bytes 16777216
  115.9 6.9 fusion.8
  122.8 11.5 %pad_maximum_fusion = f32[2,32,8,8192]{3,2,0,1:T(8,128)} fusion(f32[1,32,8,8192]{3,2,0,1:T(8,128)} %get-tuple-element.6, f32[1,32,8,8192]{3,2,0,1:T(8,128)} %get-tuple-element.5), kind=kLoop, calls=%fused_computation.2 | loop fusion | flops 4194304 | bytes 33554432 | tf_op jit(solution)/shard_map/stack | solution.py:53
  134.3 7.1 %all-to-all-start.2 = ((f32[2,32,8,8192]{3,2,0,1:T(8,128)}), f32[2,32,8,8192]{3,2,0,1:T(8,128)}, u32[]{:S(2)}, u32[]{:S(2)}) async-start(f32[2,32,8,8192]{3,2,0,1:T(8,128)} %pad_maximum_fusion), calls=%async_computation.2 | async-start | bytes 33554432 | tf_op jit(solution)/shard_map/all_to_all | solution.py:116
  141.4 0.3 fusion.43
  141.7 0.3 broadcast_multiply_fusion
  141.9 0.3 fusion.41
  142.3 0.1 fusion.76
  142.4 295.8 %all-to-all-done.2 = f32[2,32,8,8192]{3,2,0,1:T(8,128)} async-done(((f32[2,32,8,8192]{3,2,0,1:T(8,128)}), f32[2,32,8,8192]{3,2,0,1:T(8,128)}, u32[]{:S(2)}, u32[]{:S(2)}) %all-to-all-start.2) | async-done | bytes 16777248 | tf_op jit(solution)/shard_map/all_to_all | solution.py:116
  438.1 30.7 %fusion.3 = f32[2,2,128,8192]{2,3,0,1:T(8,128)S(1)} fusion(f32[1,128,2,128]{3,1,2,0:T(8,128)S(1)} %get-tuple-element.24, f32[1,128,2,128]{3,1,2,0:T(8,128)S(1)} %get-tuple-element.25, f32[2,2,16,8,8192]{4,3,0,1,2:T(8,128)} %bitcast.23), kind=kOutput, calls=%fused_computation.6 | convolution fusion | flops 12884967424 | bytes 33816576 | tf_op jit(solution)/shard_map/ymxn,xknc->ykmc/dot_general | solution.py:64
  468.9 1.1 multiply_subtract_fusion
  470.0 6.7 fusion.15
  476.7 1.1 add_convert_fusion
  477.8 2.4 pad_maximum_fusion.1
  480.2 11.2 %copy.34 = bf16[2,2,128,4096]{3,0,1,2:T(2,128)(2,1)} copy(bf16[2,2,128,4096]{2,3,0,1:T(8,128)(2,1)} %pad_maximum_fusion.1) | data formatting | bytes 8388608 | tf_op jit(solution)/shard_map/stack | solution.py:53
  491.4 70.5 %all-to-all-start.3 = ((bf16[2,2,128,4096]{3,0,1,2:T(2,128)(2,1)}), bf16[2,2,128,4096]{3,0,1,2:T(2,128)(2,1)}, u32[]{:S(2)}, u32[]{:S(2)}) async-start(bf16[2,2,128,4096]{3,0,1,2:T(2,128)(2,1)} %copy.34), calls=%async_computation.3 | async-start | bytes 8388608 | tf_op jit(solution)/shard_map/all_to_all | solution.py:121
  561.9 0.1 sine_negate_fusion.1
  562.0 77.6 %all-to-all-done.3 = bf16[2,2,128,4096]{3,0,1,2:T(2,128)(2,1)} async-done(((bf16[2,2,128,4096]{3,0,1,2:T(2,128)(2,1)}), bf16[2,2,128,4096]{3,0,1,2:T(2,128)(2,1)}, u32[]{:S(2)}, u32[]{:S(2)}) %all-to-all-start.3) | async-done | bytes 4194336 | tf_op jit(solution)/shard_map/all_to_all | solution.py:121
  639.6 5.1 copy.63
  644.7 0.5 copy.36
  645.2 2.6 copy.49
  647.8 1.8 fusion
  649.6 0.0 copy-start.3
  649.6 1.5 copy.50
  651.2 19.7 %all-to-all-start.4 = ((bf16[16,8,4096]{2,1,0:T(8,128)(2,1)}), bf16[16,8,4096]{2,1,0:T(8,128)(2,1)}, u32[]{:S(2)}, u32[]{:S(2)}) async-start(bf16[16,8,4096]{2,1,0:T(8,128)(2,1)} %bitcast.63), calls=%async_computation.4 | async-start | bytes 2097152 | tf_op jit(solution)/shard_map/all_to_all | solution.py:125
  670.9 1.5 maximum_convert_fusion
  672.4 21.5 %all-to-all-done.4 = bf16[16,8,4096]{2,1,0:T(8,128)(2,1)} async-done(((bf16[16,8,4096]{2,1,0:T(8,128)(2,1)}), bf16[16,8,4096]{2,1,0:T(8,128)(2,1)}, u32[]{:S(2)}, u32[]{:S(2)}) %all-to-all-start.4) | async-done | bytes 1048608 | tf_op jit(solution)/shard_map/all_to_all | solution.py:125
  693.9 3.2 fusion.24
  (6 shorter events, 0.1 us)
Async XLA Ops:
  1.9 23.0 %collective-permute-start = (bf16[3,2,4096]{2,1,0:T(2,128)(2,1)S(1)}, bf16[3,2,4096]{2,1,0:T(2,128)(2,1)S(1)}, u32[]{:S(2)}, u32[]{:S(2)}) collective-permute-start(bf16[3,2,4096]{2,1,0:T(2,128)(2,1)S(1)} %pad_maximum_fusion.7), channel_id=1, source_target_pairs={{0,1},{1,2},{2,3},{3,4},{4,5},{5,6},{6,7},{7,8},{8,9},{9,10},{10,1... | collective-permute-start | bytes 147464 | tf_op jit(solution)/shard_map/ppermute | solution.py:14
  7.8 17.0 %copy-start.2 = (f32[3,3,4096]{2,1,0:T(4,128)S(1)}, f32[3,3,4096]{2,1,0:T(4,128)}, u32[]{:S(2)}) copy-start(f32[3,3,4096]{2,1,0:T(4,128)} %param.10) | copy-start | bytes 442372
  15.4 9.6 %copy-start = (bf16[128,4096]{1,0:T(8,128)(2,1)S(1)}, bf16[128,4096]{1,0:T(8,128)(2,1)}, u32[]{:S(2)}) copy-start(bf16[128,4096]{1,0:T(8,128)(2,1)} %param.7) | copy-start | bytes 3145732
  15.4 9.9 %copy-start.1 = (bf16[128,4096]{1,0:T(8,128)(2,1)S(1)}, bf16[128,4096]{1,0:T(8,128)(2,1)}, u32[]{:S(2)}) copy-start(bf16[128,4096]{1,0:T(8,128)(2,1)} %param.8) | copy-start | bytes 3145732
  17.3 30.4 %all-to-all-start.1 = ((bf16[16,2,16384]{2,1,0:T(2,128)(2,1)}), bf16[16,2,16384]{2,1,0:T(2,128)(2,1)}, u32[]{:S(2)}, u32[]{:S(2)}) async-start(bf16[16,2,16384]{2,1,0:T(2,128)(2,1)} %reshape.316), calls=%async_computation.1 | async-start | bytes 2097152 | tf_op jit(solution)/shard_map/all_to_all | solution.py:104
  47.8 30.1 %all-to-all-start = ((bf16[16,2,16384]{2,1,0:T(2,128)(2,1)}), bf16[16,2,16384]{2,1,0:T(2,128)(2,1)}, u32[]{:S(2)}, u32[]{:S(2)}) async-start(bf16[16,2,16384]{2,1,0:T(2,128)(2,1)} %reshape.318), calls=%async_computation | async-start | bytes 2097152 | tf_op jit(solution)/shard_map/all_to_all | solution.py:101
  134.3 303.9 %all-to-all-start.2 = ((f32[2,32,8,8192]{3,2,0,1:T(8,128)}), f32[2,32,8,8192]{3,2,0,1:T(8,128)}, u32[]{:S(2)}, u32[]{:S(2)}) async-start(f32[2,32,8,8192]{3,2,0,1:T(8,128)} %pad_maximum_fusion), calls=%async_computation.2 | async-start | bytes 33554432 | tf_op jit(solution)/shard_map/all_to_all | solution.py:116
  491.4 148.2 %all-to-all-start.3 = ((bf16[2,2,128,4096]{3,0,1,2:T(2,128)(2,1)}), bf16[2,2,128,4096]{3,0,1,2:T(2,128)(2,1)}, u32[]{:S(2)}, u32[]{:S(2)}) async-start(bf16[2,2,128,4096]{3,0,1,2:T(2,128)(2,1)} %copy.34), calls=%async_computation.3 | async-start | bytes 8388608 | tf_op jit(solution)/shard_map/all_to_all | solution.py:121
  649.6 44.3 %copy-start.3 = (f32[4096]{0:T(1024)S(1)}, f32[4096]{0:T(1024)}, u32[]{:S(2)}) copy-start(f32[4096]{0:T(1024)} %param.11) | copy-start | bytes 49156
  651.2 42.7 %all-to-all-start.4 = ((bf16[16,8,4096]{2,1,0:T(8,128)(2,1)}), bf16[16,8,4096]{2,1,0:T(8,128)(2,1)}, u32[]{:S(2)}, u32[]{:S(2)}) async-start(bf16[16,8,4096]{2,1,0:T(8,128)(2,1)} %bitcast.63), calls=%async_computation.4 | async-start | bytes 2097152 | tf_op jit(solution)/shard_map/all_to_all | solution.py:125
where the time goes:
time: 707 us; the launch traced here: 697 us
  waiting for transfers between devices  419 us (59%)
  starting transfers between devices  114 us (16%)
  local copies, waits for them, and re-layouts  70.4 us (10%)
  other arithmetic  47.3 us (7%)
  matrix products  46.1 us (7%)
    all_to_all x1, waiting for transfers between devices, along_rows(): lax.all_to_all(spectra, 'seq', split_axis=1, concat_axis=2, tiled=True)  296 us
    all_to_all x1, waiting for transfers between devices, along_rows(): lax.all_to_all(joint.astype(jnp.bfloat16), 'seq', split_axis=2, concat_ax...  77.6 us
    all_to_all x1, starting transfers between devices, along_rows(): lax.all_to_all(joint.astype(jnp.bfloat16), 'seq', split_axis=2, concat_ax...  70.5 us
    unnamed x20, local copies, waits for them, and re-layouts  39.1 us
    dot_general x2, matrix products, row_transform(): return jnp.einsum('ymxn,xknc->ykmc', full_table, stacked, precision=PRECISE)  37.4 us
    all_to_all x1, waiting for transfers between devices, along_rows(): lax.all_to_all(convolved, 'seq', split_axis=0, concat_axis=1, tiled=True)  21.5 us
    all_to_all x1, starting transfers between devices, along_rows(): lax.all_to_all(convolved, 'seq', split_axis=0, concat_axis=1, tiled=True)  19.7 us
    all_to_all x1, waiting for transfers between devices, along_rows(): lax.all_to_all(product.reshape(1, row_count, channels), 'seq', split_axis...  16.4 us
  transfers between devices with their start and end apart: 6, of which 5 were waited for; matrix products, arithmetic and copies ran while one was open for 5% of the time, Pallas kernels for 0%

commit v1 on v0

v1 whole, which is shorter than its diff:
```python
import functools

import jax
import jax.numpy as jnp
import ml_dtypes
import numpy as np
from jax import lax
from jax.experimental import pallas as pl
from jax.experimental.pallas import tpu as pltpu
from jax.sharding import PartitionSpec as P

LANES = 128
BLOCK = 256
UNROLLED = 8
MIB = 1 << 20


def from_behind(value, axis):
    count = lax.axis_size(axis)
    return lax.ppermute(value, axis, [(source, source + 1) for source in range(count - 1)])


def transform_tables(block):
    numbers = np.concatenate([np.arange(0, block, 2), np.arange(1, block, 2)])
    quarter = (2 * numbers[:, None] + 1) * np.arange(block)[None, :] % (4 * block)
    angle = quarter.astype(np.float64) * (2.0 * np.pi / (4 * block))
    table = np.concatenate([np.cos(angle), -np.sin(angle)], axis=0)

    def split(values):
        high = values.astype(ml_dtypes.bfloat16)
        low = (values - high.astype(np.float64)).astype(ml_dtypes.bfloat16)
        return np.concatenate([high, low], axis=0)

    return split(table), split(table.T / block)


def shifted(values, edge, steps):
    rolled = pltpu.roll(values, steps, 0)
    row = lax.broadcasted_iota(jnp.int32, values.shape, 0)
    for place in range(steps):
        source = edge[edge.shape[0] - steps + place : edge.shape[0] - steps + place + 1]
        rolled = jnp.where(row == place, jnp.broadcast_to(source, values.shape), rolled)
    return rolled


def featurize(own, edge, taps):
    own = own.astype(jnp.float32)
    edge = edge.astype(jnp.float32)
    result = taps[0:1] * own
    for offset in range(1, taps.shape[0]):
        result = result + taps[offset : offset + 1] * shifted(own, edge, offset)
    return result


def product_kernel(width, key_ref, value_ref, edge_ref, taps_ref, out_ref):
    for part in range(key_ref.shape[1] // width):
        span = slice(part * width, (part + 1) * width)
        k_short = featurize(key_ref[:, span], edge_ref[1, :, span], taps_ref[1, :, span])
        v_short = featurize(value_ref[:, span], edge_ref[2, :, span], taps_ref[2, :, span])
        out_ref[part] = (k_short * v_short).astype(out_ref.dtype)


def products(key_in, value_in, edges, short_weight, width):
    rows, channels = key_in.shape
    span = max(width, min(channels, 1024))
    taps = short_weight.shape[1]
    return pl.pallas_call(
        functools.partial(product_kernel, width),
        out_shape=jax.ShapeDtypeStruct((channels // width, rows, width), jnp.bfloat16),
        grid=(channels // span,),
        in_specs=[
            pl.BlockSpec((rows, span), lambda i: (0, i)),
            pl.BlockSpec((rows, span), lambda i: (0, i)),
            pl.BlockSpec((3, taps - 1, span), lambda i: (0, 0, i)),
            pl.BlockSpec((3, taps, span), lambda i: (0, 0, i)),
        ],
        out_specs=pl.BlockSpec((span // width, rows, width), lambda i: (i, 0, 0)),
        cost_estimate=pl.CostEstimate(
            flops=12 * rows * channels, bytes_accessed=6 * rows * channels, transcendentals=0
        ),
    )(key_in, value_in, edges, short_weight)


def gate_kernel(width, conv_ref, product_ref, query_ref, edge_ref, taps_ref, gain_ref, out_ref):
    for part in range(query_ref.shape[1] // width):
        span = slice(part * width, (part + 1) * width)
        q_short = featurize(query_ref[:, span], edge_ref[0, :, span], taps_ref[0, :, span])
        mixed = conv_ref[part].astype(jnp.float32) + gain_ref[:, span] * product_ref[part].astype(
            jnp.float32
        )
        out_ref[:, span] = (q_short * mixed).astype(out_ref.dtype)


def gate(convolved, product, query_in, edges, short_weight, skip_gain):
    rows, channels = query_in.shape
    width = product.shape[2]
    span = max(width, min(channels, 1024))
    taps = short_weight.shape[1]
    parts = pl.BlockSpec((span // width, rows, width), lambda i: (i, 0, 0))
    return pl.pallas_call(
        functools.partial(gate_kernel, width),
        out_shape=jax.ShapeDtypeStruct((rows, channels), jnp.bfloat16),
        grid=(channels // span,),
        in_specs=[
            parts,
            parts,
            pl.BlockSpec((rows, span), lambda i: (0, i)),
            pl.BlockSpec((3, taps - 1, span), lambda i: (0, 0, i)),
            pl.BlockSpec((3, taps, span), lambda i: (0, 0, i)),
            pl.BlockSpec((1, span), lambda i: (0, i)),
        ],
        out_specs=pl.BlockSpec((rows, span), lambda i: (0, i)),
        cost_estimate=pl.CostEstimate(
            flops=9 * rows * channels, bytes_accessed=8 * rows * channels, transcendentals=0
        ),
    )(convolved, product, query_in, edges, short_weight, skip_gain.reshape(1, channels))


def spread_kernel(parts, width, group_ref, filter_ref, out_ref, sems):
    group = group_ref[0]
    copies = []
    for place in range(out_ref.shape[0]):
        start = pl.multiple_of((place * parts + group) * width, width)
        copies.append(
            pltpu.make_async_copy(
                filter_ref.at[:, pl.ds(start, width)], out_ref.at[place], sems.at[place]
            )
        )
    for copy in copies:
        copy.start()
    for copy in copies:
        copy.wait()


def spread_filter(long_filter, group, places, parts):
    rows, channels = long_filter.shape
    width = channels // (places * parts)
    return pl.pallas_call(
        functools.partial(spread_kernel, parts, width),
        out_shape=jax.ShapeDtypeStruct((places, rows, width), long_filter.dtype),
        in_specs=[
            pl.BlockSpec(memory_space=pltpu.SMEM),
            pl.BlockSpec(memory_space=pl.ANY),
        ],
        out_specs=pl.BlockSpec(memory_space=pl.ANY),
        scratch_shapes=[pltpu.SemaphoreType.DMA((places,))],
        cost_estimate=pl.CostEstimate(
            flops=0, bytes_accessed=4 * rows * places * width, transcendentals=0
        ),
    )(group.reshape(1), long_filter)


def transform(table, values):
    both = jnp.dot(table, values, preferred_element_type=jnp.float32)
    half = table.shape[0] // 2
    return both[:half] + both[half:]


def over(count, body):
    if count <= UNROLLED:
        for step in range(count):
            body(step)
    else:

        @pl.loop(0, count)
        def _(step):
            body(step)


def filter_kernel(pieces, *refs):
    group_ref, table_ref = refs[:2]
    filter_refs = refs[2 : 2 + pieces]
    out_ref = refs[2 + pieces]
    count, double, _ = out_ref.shape
    block = double // 2

    def body(step):
        start = step * block
        if not isinstance(step, int):
            start = pl.multiple_of(start, block)
        values = [ref[pl.ds(start, block), :] for ref in filter_refs]
        if pieces == 2:
            own, other = values
            first = group_ref[0] == 0
            values = [jnp.where(first, own, other), jnp.where(first, other, own)]
        joined = values[0] if pieces == 1 else jnp.concatenate(values, axis=1)
        out_ref[step] = transform(table_ref[...], joined)

    over(count, body)


def filter_spectra(pieces, group, table):
    length = pieces[0].shape[0]
    width = sum(piece.shape[1] for piece in pieces)
    block = table.shape[1]
    return pl.pallas_call(
        functools.partial(filter_kernel, len(pieces)),
        out_shape=jax.ShapeDtypeStruct((length // block, 2 * block, width), jnp.float32),
        in_specs=[pl.BlockSpec(memory_space=pltpu.SMEM)]
        + [pl.BlockSpec(memory_space=pltpu.VMEM)] * (1 + len(pieces)),
        out_specs=pl.BlockSpec(memory_space=pltpu.VMEM),
        compiler_params=pltpu.CompilerParams(vmem_limit_bytes=40 * MIB),
        cost_estimate=pl.CostEstimate(
            flops=8 * length * block * width, bytes_accessed=10 * length * width, transcendentals=0
        ),
    )(group.reshape(1), table, *pieces)


def conv_kernel(forward_ref, inverse_ref, product_ref, filter_ref, out_ref, data, mixed, last):
    count, double, width = filter_ref.shape
    block = double // 2
    tile = 8

    def piece(step):
        start = step * block
        return pl.ds(start if isinstance(step, int) else pl.multiple_of(start, block), block)

    def forward(step):
        data[step] = transform(forward_ref[...], product_ref[piece(step), :])

    def inverse(slot, step):
        values = mixed[slot]
        high = values.astype(jnp.bfloat16)
        low = (values - high.astype(jnp.float32)).astype(jnp.bfloat16)
        result = transform(inverse_ref[...], high) + jnp.dot(
            inverse_ref[:block], low, preferred_element_type=jnp.float32
        )
        out_ref[piece(step), :] = result.astype(out_ref.dtype)

    over(count, forward)
    lane_step = min(width, LANES)
    strips = [
        (sign, column)
        for sign in (1.0, -1.0)
        for column in range(0, width, lane_step)
    ]
    if count <= UNROLLED:
        for half, (sign, column) in enumerate(strips):
            base = 0 if sign > 0 else block // 2
            lanes = slice(column, column + lane_step)

            @pl.loop(0, block // 2 // tile)
            def _(index):
                real = pl.ds(pl.multiple_of(base + index * tile, tile), tile)
                imag = pl.ds(pl.multiple_of(block + base + index * tile, tile), tile)
                data_parts = [
                    (data[step, real, lanes], data[step, imag, lanes]) for step in range(count)
                ]
                filter_parts = [
                    (filter_ref[step, real, lanes], filter_ref[step, imag, lanes])
                    for step in range(count)
                ]
                before = None
                for total in range(count):
                    sum_real = sum_imag = None
                    for step in range(total + 1):
                        a, b = data_parts[step]
                        c, d = filter_parts[total - step]
                        term_real = a * c - b * d
                        term_imag = a * d + b * c
                        sum_real = term_real if step == 0 else sum_real + term_real
                        sum_imag = term_imag if step == 0 else sum_imag + term_imag
                    if before is None:
                        mixed[total, real, lanes] = sum_real
                        mixed[total, imag, lanes] = sum_imag
                    elif sign > 0:
                        mixed[total, real, lanes] = sum_real - before[1]
                        mixed[total, imag, lanes] = sum_imag + before[0]
                    else:
                        mixed[total, real, lanes] = sum_real + before[1]
                        mixed[total, imag, lanes] = sum_imag - before[0]
                    before = (sum_real, sum_imag)

        for step in range(count):
            inverse(step, step)
    else:
        last[...] = jnp.zeros_like(last)

        @pl.loop(0, count)
        def _(total):
            for sign, column in strips:
                base = 0 if sign > 0 else block // 2
                lanes = slice(column, column + lane_step)

                @pl.loop(0, block // 2 // tile)
                def _(index):
                    real = pl.ds(pl.multiple_of(base + index * tile, tile), tile)
                    imag = pl.ds(pl.multiple_of(block + base + index * tile, tile), tile)

                    def add(step, sums):
                        a, b = data[step, real, lanes], data[step, imag, lanes]
                        c = filter_ref[total - step, real, lanes]
                        d = filter_ref[total - step, imag, lanes]
                        return sums[0] + (a * c - b * d), sums[1] + (a * d + b * c)

                    zero = jnp.zeros((tile, lane_step), jnp.float32)
                    sum_real, sum_imag = lax.fori_loop(0, total + 1, add, (zero, zero))
                    mixed[0, real, lanes] = sum_real - sign * last[imag, lanes]
                    mixed[0, imag, lanes] = sum_imag + sign * last[real, lanes]
                    last[real, lanes] = sum_real
                    last[imag, lanes] = sum_imag

            inverse(0, total)


def convolve(product, spectra, forward_table, inverse_table):
    length, width = product.shape
    count, double, _ = spectra.shape
    small = count <= UNROLLED
    return pl.pallas_call(
        conv_kernel,
        out_shape=jax.ShapeDtypeStruct((length, width), jnp.bfloat16),
        in_specs=[pl.BlockSpec(memory_space=pltpu.VMEM)] * 4,
        out_specs=pl.BlockSpec(memory_space=pltpu.VMEM),
        scratch_shapes=[
            pltpu.VMEM((count, double, width), jnp.float32),
            pltpu.VMEM((count if small else 1, double, width), jnp.float32),
            pltpu.VMEM((8, width) if small else (double, width), jnp.float32),
        ],
        compiler_params=pltpu.CompilerParams(vmem_limit_bytes=(32 if small else 56) * MIB),
        cost_estimate=pl.CostEstimate(
            flops=16 * length * double * width,
            bytes_accessed=12 * length * width,
            transcendentals=0,
        ),
    )(forward_table, inverse_table, product, spectra)


def exchange(value):
    return lax.all_to_all(value, "seq", split_axis=0, concat_axis=0, tiled=True)


def on_device(query_in, key_in, value_in, long_filter, short_weight, skip_gain):
    places = lax.axis_size("seq")
    parts = lax.axis_size("groups")
    group = lax.axis_index("groups").astype(jnp.int32)
    rows, channels = key_in.shape
    width = channels // places
    length = places * rows
    block = BLOCK if length % BLOCK == 0 else rows
    forward_table, inverse_table = transform_tables(block)
    forward_table = jnp.asarray(forward_table)
    inverse_table = jnp.asarray(inverse_table)
    rim = short_weight.shape[1] - 1
    aligned = width % (parts * LANES) == 0 and parts == 2

    if aligned:
        sent = spread_filter(long_filter, group, places, parts)
        own = exchange(sent).reshape(length, width // parts)
        other = lax.ppermute(own, "groups", [(0, 1), (1, 0)])
        filter_pieces = [own, other]
    else:
        sent = long_filter.reshape(rows, places, width).transpose(1, 0, 2)
        filter_pieces = [exchange(sent).reshape(length, width)]

    edges = from_behind(jnp.stack([query_in[-rim:], key_in[-rim:], value_in[-rim:]]), "seq")
    if aligned:
        product = products(key_in, value_in, edges, short_weight, width)
        sent = product
    else:
        product = products(key_in, value_in, edges, short_weight, channels)
        sent = product.reshape(rows, places, width).transpose(1, 0, 2)
    received = exchange(sent).reshape(length, width)
    spectra = filter_spectra(filter_pieces, group, forward_table)
    convolved = convolve(received, spectra, forward_table, inverse_table)
    convolved = exchange(convolved.reshape(places, rows, width))
    if not aligned:
        convolved = convolved.transpose(1, 0, 2).reshape(1, rows, channels)
    return gate(convolved, product, query_in, edges, short_weight, skip_gain)


def solution(mesh):
    placed = (
        P(("groups", "seq"), None),
        P(("groups", "seq"), None),
        P(("groups", "seq"), None),
        P("seq", None),
        P(),
        P(),
    )
    return jax.shard_map(
        on_device, mesh=mesh, in_specs=placed, out_specs=P(("groups", "seq"), None), check_vma=False
    )
```

time: 707 us -> 116 us (0.16); the launches traced: 697 us -> 115 us
  waiting for transfers between devices: 419 us -> 23.5 us
  starting transfers between devices: 114 us -> 20.5 us
  local copies, waits for them, and re-layouts: 70.4 us -> 6.53 us
  other arithmetic: 47.3 us -> 0.08 us
  matrix products: 46.1 us -> 0 us
  Pallas kernels: 0 us -> 33 us
  blocking collectives: 0 us -> 31.6 us
    all_to_all x5 -> x2, waiting for transfers between devices: 419 us -> 10 us  [exchange(): return lax.all_to_all(value, 'seq', split_axis=0, concat_axis=0, tiled=True)]
    all_to_all x5 -> x2, starting transfers between devices: 112 us -> 16.6 us  [exchange(): return lax.all_to_all(value, 'seq', split_axis=0, concat_axis=0, tiled=True)]
    dot_general x4 -> x0, matrix products: 46.1 us -> none  [the longest x2 37.4 us: row_transform(): return jnp.einsum('ymxn,xknc->ykmc', full_table, stacked, precision=PRECISE)]
    unnamed x20 -> x10, local copies, waits for them, and re-layouts: 39.1 us -> 4.76 us
    pallas_call x0 -> x5, Pallas kernels: none -> 33 us  [the longest x1 17.1 us: spread_filter(): pl.pallas_call(functools.partial(spread_kernel, parts, width), out_shape=...]
    all_to_all x0 -> x1, blocking collectives: none -> 31.6 us  [exchange(): return lax.all_to_all(value, 'seq', split_axis=0, concat_axis=0, tiled=True)]
    unnamed x2 -> x0, other arithmetic: 15 us -> none
    another operation x5 -> x1, other arithmetic: 15.1 us -> 0.08 us  [on_device(): jnp.stack([query_in[-rim:], key_in[-rim:], value_in[-rim:]])]
  transfers between devices with their start and end apart: 6 -> 4, of which waited for: 5 -> 4; matrix products, arithmetic and copies ran while one was open for 5% -> 2% of each run, Pallas kernels for 0% -> 5%
where the time goes in v1:
time: 116 us; the launch traced here: 115 us
  Pallas kernels  33 us (28%)
  blocking collectives  31.6 us (27%)
  waiting for transfers between devices  23.5 us (20%)
  starting transfers between devices  20.5 us (18%)
  local copies, waits for them, and re-layouts  6.53 us (6%)
    all_to_all x1, blocking collectives, exchange(): return lax.all_to_all(value, 'seq', split_axis=0, concat_axis=0, tiled=True)  31.6 us
    pallas_call x1, Pallas kernels, spread_filter(): pl.pallas_call(functools.partial(spread_kernel, parts, width), out_shape=...  17.1 us
    all_to_all x2, starting transfers between devices, exchange(): return lax.all_to_all(value, 'seq', split_axis=0, concat_axis=0, tiled=True)  16.6 us
    ppermute x1, waiting for transfers between devices, on_device(): other = lax.ppermute(own, 'groups', [(0, 1), (1, 0)])  12.7 us
    all_to_all x2, waiting for transfers between devices, exchange(): return lax.all_to_all(value, 'seq', split_axis=0, concat_axis=0, tiled=True)  10 us
    pallas_call x1, Pallas kernels, convolve(): pl.pallas_call(conv_kernel, out_shape=jax.ShapeDtypeStruct((length, width...  6.08 us
    unnamed x10, local copies, waits for them, and re-layouts  4.76 us
    pallas_call x1, Pallas kernels, products(): pl.pallas_call(functools.partial(product_kernel, width), out_shape=jax.Sh...  4.28 us
  transfers between devices with their start and end apart: 4, of which 4 were waited for; matrix products, arithmetic and copies ran while one was open for 2% of the time, Pallas kernels for 5%

profile of v1, /device:TPU:0, one launch (start us, length us, event | category | flops | bytes accessed | tf_op | source)
XLA Modules:
  0.0 115.3 jit_solution(13100662021974649520)
XLA Ops:
  0.0 0.0 copy-start.2
  0.0 17.1 %shard_map.83 = bf16[16,128,128]{2,1,0:T(8,128)(2,1)} custom-call(s32[1]{0:T(128)} %bitcast.4.group_ref.refs_0_, bf16[128,4096]{1,0:T(8,128)(2,1)} %filter_ref.1), custom_call_target="tpu_custom_call" | custom-call | bytes 1048576 | tf_op jit(solution)/shard_map/pallas_call | solution.py:138
  17.1 7.4 %all-to-all-start.1 = ((bf16[16,128,128]{2,1,0:T(8,128)(2,1)}), bf16[16,128,128]{2,1,0:T(8,128)(2,1)S(1)}, u32[]{:S(2)}, u32[]{:S(2)}) async-start(bf16[16,128,128]{2,1,0:T(8,128)(2,1)} %shard_map.83), calls=%async_computation.1 | async-start | bytes 1048576 | tf_op jit(solution)/shard_map/all_to_all | solution.py:330
  24.5 0.9 slice_bitcast_fusion
  25.5 0.9 slice_bitcast_fusion.2
  26.3 0.1 pad_maximum_fusion
  26.4 2.3 %collective-permute-start = (bf16[3,2,4096]{2,1,0:T(2,128)(2,1)S(1)}, bf16[3,2,4096]{2,1,0:T(2,128)(2,1)S(1)}, u32[]{:S(2)}, u32[]{:S(2)}) collective-permute-start(bf16[3,2,4096]{2,1,0:T(2,128)(2,1)S(1)} %pad_maximum_fusion), channel_id=1, source_target_pairs={{0,1},{1,2},{2,3},{3,4},{4,5},{5,6},{6,7},{7,8},{8,9},{9,10},{10,1... | collective-permute-start | bytes 147464 | tf_op jit(solution)/shard_map/ppermute | solution.py:20
  28.7 0.9 collective-permute-done.edge_ref
  29.6 0.0 copy-start.4
  29.6 0.6 copy-done.4
  30.2 4.3 %shard_map.82.product_ref = bf16[16,128,256]{2,1,0:T(8,128)(2,1)} custom-call(bf16[128,4096]{1,0:T(8,128)(2,1)} %key_ref.1, bf16[128,4096]{1,0:T(8,128)(2,1)} %value_ref.1, bf16[3,2,4096]{2,1,0:T(2,128)(2,1)} %copy-done.4, f32[3,3,4096]{2,1,0:T(4,128)} %taps_ref.3), custom_call_target="tpu_custom_call" | custom-call | flops 6291456 | bytes 3145728 | tf_op jit(solution)/shard_map/pallas_call | solution.py:67
  34.5 0.0 copy-start.3
  34.5 4.5 %all-to-all-done.1 = bf16[16,128,128]{2,1,0:T(8,128)(2,1)S(1)} async-done(((bf16[16,128,128]{2,1,0:T(8,128)(2,1)}), bf16[16,128,128]{2,1,0:T(8,128)(2,1)S(1)}, u32[]{:S(2)}, u32[]{:S(2)}) %all-to-all-start.1) | async-done | bytes 524320 | tf_op jit(solution)/shard_map/all_to_all | solution.py:330
  39.0 9.2 %all-to-all-start = ((bf16[16,128,256]{2,1,0:T(8,128)(2,1)}), bf16[16,128,256]{2,1,0:T(8,128)(2,1)S(1)}, u32[]{:S(2)}, u32[]{:S(2)}) async-start(bf16[16,128,256]{2,1,0:T(8,128)(2,1)} %shard_map.82.product_ref), calls=%async_computation | async-start | bytes 2097152 | tf_op jit(solution)/shard_map/all_to_all | solution.py:330
  48.2 1.6 %collective-permute-start.1 = (bf16[2048,128]{1,0:T(8,128)(2,1)S(1)}, bf16[2048,128]{1,0:T(8,128)(2,1)S(1)}, u32[]{:S(2)}, u32[]{:S(2)}) collective-permute-start(bf16[2048,128]{1,0:T(8,128)(2,1)S(1)} %bitcast.11), channel_id=1, source_target_pairs={{0,16},{16,0},{1,17},{17,1},{2,18},{18,2},{3,19},{19,3},{4,20},{20... | collective-permute-start | bytes 1572872 | tf_op jit(solution)/shard_map/ppermute | solution.py:350
  49.8 12.7 %collective-permute-done.1.refs_3_ = bf16[2048,128]{1,0:T(8,128)(2,1)S(1)} collective-permute-done((bf16[2048,128]{1,0:T(8,128)(2,1)S(1)}, bf16[2048,128]{1,0:T(8,128)(2,1)S(1)}, u32[]{:S(2)}, u32[]{:S(2)}) %collective-permute-start.1) | collective-permute-done | bytes 524320 | tf_op jit(solution)/shard_map/ppermute | solution.py:350
  62.5 0.0 copy-done.2
  62.5 1.3 %shard_map.84.filter_ref = f32[8,512,256]{2,1,0:T(8,128)S(1)} custom-call(s32[1]{0:T(128)} %bitcast.4.group_ref.refs_0_, bf16[1024,256]{1,0:T(8,128)(2,1)S(1)} %copy-done.2, bf16[2048,128]{1,0:T(8,128)(2,1)S(1)} %bitcast.12, bf16[2048,128]{1,0:T(8,128)(2,1)S(1)} %collective-permute-done.1.refs_3_), custom_call_target="tpu_custom_call" | custom-call | flops 1073741824 | bytes 5242880 | tf_op jit(solution)/shard_map/pallas_call | solution.py:196
  63.7 0.0 copy-start
  63.7 1.9 %copy-done = f32[8,512,256]{2,1,0:T(8,128)} copy-done((f32[8,512,256]{2,1,0:T(8,128)}, f32[8,512,256]{2,1,0:T(8,128)S(1)}, u32[]{:S(2)}) %copy-start) | copy-done | bytes 4194328
  65.7 5.5 %all-to-all-done = bf16[16,128,256]{2,1,0:T(8,128)(2,1)S(1)} async-done(((bf16[16,128,256]{2,1,0:T(8,128)(2,1)}), bf16[16,128,256]{2,1,0:T(8,128)(2,1)S(1)}, u32[]{:S(2)}, u32[]{:S(2)}) %all-to-all-start) | async-done | bytes 1048608 | tf_op jit(solution)/shard_map/all_to_all | solution.py:330
  71.2 0.0 copy-done.3
  71.2 0.0 copy-start.1
  71.2 2.2 %copy-done.1 = f32[8,512,256]{2,1,0:T(8,128)S(1)} copy-done((f32[8,512,256]{2,1,0:T(8,128)S(1)}, f32[8,512,256]{2,1,0:T(8,128)}, u32[]{:S(2)}) %copy-start.1) | copy-done | bytes 4194328
  73.4 6.1 %shard_map.85 = bf16[2048,256]{1,0:T(8,128)(2,1)S(1)} custom-call(bf16[1024,256]{1,0:T(8,128)(2,1)S(1)} %copy-done.2, bf16[512,512]{1,0:T(8,128)(2,1)S(1)} %copy-done.3, bf16[2048,256]{1,0:T(8,128)(2,1)S(1)} %bitcast.13, f32[8,512,256]{2,1,0:T(8,128)S(1)} %copy-done.1), custom_call_target="tpu_custom_call" | custom-call | flops 4294967296 | bytes 6291456 | tf_op jit(solution)/shard_map/pallas_call | solution.py:310
  79.4 31.6 %all_to_all.15.conv_ref = bf16[16,128,256]{2,1,0:T(8,128)(2,1)} all-to-all(bf16[16,128,256]{2,1,0:T(8,128)(2,1)S(1)} %bitcast.14), channel_id=1, replica_groups=mesh['groups'=2,'seq'=16] {'seq'}, dimensions={0} | all-to-all | bytes 2097152 | tf_op jit(solution)/shard_map/all_to_all | solution.py:330
  111.1 4.3 %shard_map.86 = bf16[128,4096]{1,0:T(8,128)(2,1)} custom-call(bf16[16,128,256]{2,1,0:T(8,128)(2,1)} %all_to_all.15.conv_ref, bf16[16,128,256]{2,1,0:T(8,128)(2,1)} %shard_map.82.product_ref, bf16[128,4096]{1,0:T(8,128)(2,1)} %query_ref.1, bf16[3,2,4096]{2,1,0:T(2,128)(2,1)} %copy-done.4, f32[3,3,4096]{2,1,0:T(4,128)} %taps_ref.3, f32[1,4096]{1,0:T(1,128)} %bitcast.15), custom_call_target="tpu_custom_call" | custom-call | flops 4718592 | bytes 4194304 | tf_op jit(solution)/shard_map/pallas_call | solution.py:100
Async XLA Ops:
  0.0 62.5 %copy-start.2 = (bf16[1024,256]{1,0:T(8,128)(2,1)S(1)}, bf16[1024,256]{1,0:T(8,128)(2,1)}, u32[]{:S(2)}) copy-start(bf16[1024,256]{1,0:T(8,128)(2,1)} %constant.10.clone.refs_1_.forward_ref) | copy-start | bytes 1572868
  17.1 21.9 %all-to-all-start.1 = ((bf16[16,128,128]{2,1,0:T(8,128)(2,1)}), bf16[16,128,128]{2,1,0:T(8,128)(2,1)S(1)}, u32[]{:S(2)}, u32[]{:S(2)}) async-start(bf16[16,128,128]{2,1,0:T(8,128)(2,1)} %shard_map.83), calls=%async_computation.1 | async-start | bytes 1048576 | tf_op jit(solution)/shard_map/all_to_all | solution.py:330
  26.4 3.2 %collective-permute-start = (bf16[3,2,4096]{2,1,0:T(2,128)(2,1)S(1)}, bf16[3,2,4096]{2,1,0:T(2,128)(2,1)S(1)}, u32[]{:S(2)}, u32[]{:S(2)}) collective-permute-start(bf16[3,2,4096]{2,1,0:T(2,128)(2,1)S(1)} %pad_maximum_fusion), channel_id=1, source_target_pairs={{0,1},{1,2},{2,3},{3,4},{4,5},{5,6},{6,7},{7,8},{8,9},{9,10},{10,1... | collective-permute-start | bytes 147464 | tf_op jit(solution)/shard_map/ppermute | solution.py:20
  29.6 0.6 copy-start.4
  34.5 36.7 %copy-start.3 = (bf16[512,512]{1,0:T(8,128)(2,1)S(1)}, bf16[512,512]{1,0:T(8,128)(2,1)}, u32[]{:S(2)}) copy-start(bf16[512,512]{1,0:T(8,128)(2,1)} %constant.11.clone.inverse_ref) | copy-start | bytes 1572868
  39.0 32.2 %all-to-all-start = ((bf16[16,128,256]{2,1,0:T(8,128)(2,1)}), bf16[16,128,256]{2,1,0:T(8,128)(2,1)S(1)}, u32[]{:S(2)}, u32[]{:S(2)}) async-start(bf16[16,128,256]{2,1,0:T(8,128)(2,1)} %shard_map.82.product_ref), calls=%async_computation | async-start | bytes 2097152 | tf_op jit(solution)/shard_map/all_to_all | solution.py:330
  48.2 14.2 %collective-permute-start.1 = (bf16[2048,128]{1,0:T(8,128)(2,1)S(1)}, bf16[2048,128]{1,0:T(8,128)(2,1)S(1)}, u32[]{:S(2)}, u32[]{:S(2)}) collective-permute-start(bf16[2048,128]{1,0:T(8,128)(2,1)S(1)} %bitcast.11), channel_id=1, source_target_pairs={{0,16},{16,0},{1,17},{17,1},{2,18},{18,2},{3,19},{19,3},{4,20},{20... | collective-permute-start | bytes 1572872 | tf_op jit(solution)/shard_map/ppermute | solution.py:350
  63.7 2.0 %copy-start = (f32[8,512,256]{2,1,0:T(8,128)}, f32[8,512,256]{2,1,0:T(8,128)S(1)}, u32[]{:S(2)}) copy-start(f32[8,512,256]{2,1,0:T(8,128)S(1)} %shard_map.84.filter_ref) | copy-start | bytes 12582916
  71.2 2.2 %copy-start.1 = (f32[8,512,256]{2,1,0:T(8,128)S(1)}, f32[8,512,256]{2,1,0:T(8,128)}, u32[]{:S(2)}) copy-start(f32[8,512,256]{2,1,0:T(8,128)} %copy-done) | copy-start | bytes 12582916

commit v2 on v1

v2 whole, which is shorter than its diff:
```python
import functools

import jax
import jax.numpy as jnp
import ml_dtypes
import numpy as np
from jax import lax
from jax.experimental import pallas as pl
from jax.experimental.pallas import tpu as pltpu
from jax.sharding import PartitionSpec as P

LANES = 128
SUBLANES = 8
BLOCK = 256
UNROLLED = 8
MIB = 1 << 20


def from_behind(value, axis):
    count = lax.axis_size(axis)
    return lax.ppermute(value, axis, [(source, source + 1) for source in range(count - 1)])


def transform_tables(block):
    numbers = np.concatenate([np.arange(0, block, 2), np.arange(1, block, 2)])
    quarter = (2 * numbers[:, None] + 1) * np.arange(block)[None, :] % (4 * block)
    angle = quarter.astype(np.float64) * (2.0 * np.pi / (4 * block))
    table = np.concatenate([np.cos(angle), -np.sin(angle)], axis=0)

    def split(values):
        high = values.astype(ml_dtypes.bfloat16)
        low = (values - high.astype(np.float64)).astype(ml_dtypes.bfloat16)
        return np.concatenate([high, low], axis=0)

    return split(table), split(table.T / block)


def shifted(values, edge, steps):
    rolled = pltpu.roll(values, steps, 0)
    row = lax.broadcasted_iota(jnp.int32, values.shape, 0)
    for place in range(steps):
        source = edge[edge.shape[0] - steps + place : edge.shape[0] - steps + place + 1]
        rolled = jnp.where(row == place, jnp.broadcast_to(source, values.shape), rolled)
    return rolled


def featurize_inside(own, taps):
    result = taps[0:1] * own
    for offset in range(1, taps.shape[0]):
        result = result + taps[offset : offset + 1] * pltpu.roll(own, offset, 0)
    return result


def featurize(own, edge, taps):
    own = own.astype(jnp.float32)
    edge = edge.astype(jnp.float32)
    top = own[:SUBLANES]
    first = taps[0:1] * top
    for offset in range(1, taps.shape[0]):
        first = first + taps[offset : offset + 1] * shifted(top, edge, offset)
    return jnp.concatenate([first, featurize_inside(own, taps)[SUBLANES:]], axis=0)


def product_kernel(key_ref, value_ref, edge_ref, taps_ref, out_ref):
    for start in range(0, key_ref.shape[1], LANES):
        span = slice(start, start + LANES)
        k_short = featurize(key_ref[:, span], edge_ref[1, :, span], taps_ref[1, :, span])
        v_short = featurize(value_ref[:, span], edge_ref[2, :, span], taps_ref[2, :, span])
        out_ref[:, span] = (k_short * v_short).astype(out_ref.dtype)


def products(key_in, value_in, edges, short_weight):
    rows, channels = key_in.shape
    span = min(channels, 1024)
    taps = short_weight.shape[1]
    return pl.pallas_call(
        product_kernel,
        out_shape=jax.ShapeDtypeStruct((rows, channels), jnp.bfloat16),
        grid=(channels // span,),
        in_specs=[
            pl.BlockSpec((rows, span), lambda i: (0, i)),
            pl.BlockSpec((rows, span), lambda i: (0, i)),
            pl.BlockSpec((3, taps - 1, span), lambda i: (0, 0, i)),
            pl.BlockSpec((3, taps, span), lambda i: (0, 0, i)),
        ],
        out_specs=pl.BlockSpec((rows, span), lambda i: (0, i)),
        cost_estimate=pl.CostEstimate(
            flops=12 * rows * channels, bytes_accessed=6 * rows * channels, transcendentals=0
        ),
    )(key_in, value_in, edges, short_weight)


def gate_kernel(conv_ref, product_ref, query_ref, edge_ref, taps_ref, gain_ref, out_ref):
    for part in range(conv_ref.shape[0]):
        span = slice(part * LANES, (part + 1) * LANES)
        q_short = featurize(query_ref[:, span], edge_ref[0, :, span], taps_ref[0, :, span])
        mixed = conv_ref[part].astype(jnp.float32) + gain_ref[:, span] * product_ref[
            :, span
        ].astype(jnp.float32)
        out_ref[:, span] = (q_short * mixed).astype(out_ref.dtype)


def gate(convolved, product, query_in, edges, short_weight, skip_gain):
    rows, channels = query_in.shape
    span = min(channels, 1024)
    taps = short_weight.shape[1]
    across = pl.BlockSpec((rows, span), lambda i: (0, i))
    return pl.pallas_call(
        gate_kernel,
        out_shape=jax.ShapeDtypeStruct((rows, channels), jnp.bfloat16),
        grid=(channels // span,),
        in_specs=[
            pl.BlockSpec((span // LANES, rows, LANES), lambda i: (i, 0, 0)),
            across,
            across,
            pl.BlockSpec((3, taps - 1, span), lambda i: (0, 0, i)),
            pl.BlockSpec((3, taps, span), lambda i: (0, 0, i)),
            pl.BlockSpec((1, span), lambda i: (0, i)),
        ],
        out_specs=across,
        cost_estimate=pl.CostEstimate(
            flops=9 * rows * channels, bytes_accessed=8 * rows * channels, transcendentals=0
        ),
    )(convolved, product, query_in, edges, short_weight, skip_gain.reshape(1, channels))


def pack_kernel(group_ref, key_ref, value_ref, filter_ref, taps_ref, out_ref):
    del group_ref
    rows = key_ref.shape[0]
    share = filter_ref.shape[0]
    row = lax.broadcasted_iota(jnp.int32, (SUBLANES, LANES), 0)
    for part in range(out_ref.shape[0]):
        span = slice(part * LANES, (part + 1) * LANES)
        key = key_ref[:, span].astype(jnp.float32)
        value = value_ref[:, span].astype(jnp.float32)
        k_short = featurize_inside(key, taps_ref[1, :, span])
        v_short = featurize_inside(value, taps_ref[2, :, span])
        out_ref[part, :rows] = (k_short * v_short).astype(out_ref.dtype)
        out_ref[part, rows : rows + share] = filter_ref[:, span]
        key_tile = jnp.where(
            row < 2,
            pltpu.roll(key[rows - SUBLANES :], 2, 0),
            pltpu.roll(key[:SUBLANES], 2, 0),
        )
        value_tile = jnp.where(
            row < 6,
            pltpu.roll(value[rows - SUBLANES :], 6, 0),
            pltpu.roll(value[:SUBLANES], 6, 0),
        )
        edge = jnp.where(row < 4, key_tile, value_tile)
        out_ref[part, rows + share :] = edge.astype(out_ref.dtype)


def pack(key_in, value_in, long_filter, short_weight, group, owners, parts):
    rows, channels = key_in.shape
    span = min(channels, 1024)
    taps = short_weight.shape[1]
    height = rows + rows // parts + SUBLANES
    return pl.pallas_call(
        pack_kernel,
        out_shape=jax.ShapeDtypeStruct((owners, height, LANES), jnp.bfloat16),
        grid_spec=pltpu.PrefetchScalarGridSpec(
            num_scalar_prefetch=1,
            grid=(channels // span,),
            in_specs=[
                pl.BlockSpec((rows, span), lambda i, g: (0, i)),
                pl.BlockSpec((rows, span), lambda i, g: (0, i)),
                pl.BlockSpec((rows // parts, span), lambda i, g: (g[0], i)),
                pl.BlockSpec((3, taps, span), lambda i, g: (0, 0, i)),
            ],
            out_specs=pl.BlockSpec((span // LANES, height, LANES), lambda i, g: (i, 0, 0)),
        ),
        cost_estimate=pl.CostEstimate(
            flops=12 * rows * channels, bytes_accessed=8 * rows * channels, transcendentals=0
        ),
    )(group.reshape(1), key_in, value_in, long_filter, short_weight)


def transform(table, values):
    both = jnp.dot(table, values, preferred_element_type=jnp.float32)
    half = table.shape[0] // 2
    return both[:half] + both[half:]


def over(count, body):
    if count <= UNROLLED:
        for step in range(count):
            body(step)
    else:

        @pl.loop(0, count)
        def _(step):
            body(step)


def filter_kernel(table_ref, filter_ref, out_ref):
    count, double, _ = out_ref.shape
    block = double // 2

    def body(step):
        start = step * block
        if not isinstance(step, int):
            start = pl.multiple_of(start, block)
        out_ref[step] = transform(table_ref[...], filter_ref[pl.ds(start, block), :])

    over(count, body)


def filter_spectra(long_filter, table):
    length, width = long_filter.shape
    block = table.shape[1]
    return pl.pallas_call(
        filter_kernel,
        out_shape=jax.ShapeDtypeStruct((length // block, 2 * block, width), jnp.float32),
        in_specs=[pl.BlockSpec(memory_space=pltpu.VMEM)] * 2,
        out_specs=pl.BlockSpec(memory_space=pltpu.VMEM),
        compiler_params=pltpu.CompilerParams(vmem_limit_bytes=40 * MIB),
        cost_estimate=pl.CostEstimate(
            flops=8 * length * block * width, bytes_accessed=10 * length * width, transcendentals=0
        ),
    )(table, long_filter)


def inverse(table_ref, values, block):
    high = values.astype(jnp.bfloat16)
    low = (values - high.astype(jnp.float32)).astype(jnp.bfloat16)
    return transform(table_ref[...], high) + jnp.dot(
        table_ref[:block], low, preferred_element_type=jnp.float32
    )


def conv_kernel(forward_ref, inverse_ref, product_ref, filter_ref, out_ref, data, mixed, last):
    count, double, width = filter_ref.shape
    block = double // 2
    lane_step = min(width, LANES)

    def piece(step):
        start = step * block
        return pl.ds(start if isinstance(step, int) else pl.multiple_of(start, block), block)

    def forward(step):
        data[step] = transform(forward_ref[...], product_ref[piece(step), :])

    over(count, forward)
    last[...] = jnp.zeros_like(last)

    @pl.loop(0, count)
    def _(total):
        for sign, base in ((1.0, 0), (-1.0, block // 2)):
            for column in range(0, width, lane_step):
                lanes = slice(column, column + lane_step)

                @pl.loop(0, block // 2 // SUBLANES)
                def _(index):
                    start = pl.multiple_of(base + index * SUBLANES, SUBLANES)
                    real = pl.ds(start, SUBLANES)
                    imag = pl.ds(pl.multiple_of(block + start, SUBLANES), SUBLANES)

                    def add(step, sums):
                        a, b = data[step, real, lanes], data[step, imag, lanes]
                        c = filter_ref[total - step, real, lanes]
                        d = filter_ref[total - step, imag, lanes]
                        return sums[0] + (a * c - b * d), sums[1] + (a * d + b * c)

                    zero = jnp.zeros((SUBLANES, lane_step), jnp.float32)
                    sum_real, sum_imag = lax.fori_loop(0, total + 1, add, (zero, zero))
                    mixed[real, lanes] = sum_real - sign * last[imag, lanes]
                    mixed[imag, lanes] = sum_imag + sign * last[real, lanes]
                    last[real, lanes] = sum_real
                    last[imag, lanes] = sum_imag

        out_ref[piece(total), :] = inverse(inverse_ref, mixed[...], block).astype(out_ref.dtype)


def convolve(product, spectra, forward_table, inverse_table):
    length, width = product.shape
    count, double, _ = spectra.shape
    return pl.pallas_call(
        conv_kernel,
        out_shape=jax.ShapeDtypeStruct((length, width), jnp.bfloat16),
        in_specs=[pl.BlockSpec(memory_space=pltpu.VMEM)] * 4,
        out_specs=pl.BlockSpec(memory_space=pltpu.VMEM),
        scratch_shapes=[
            pltpu.VMEM((count, double, width), jnp.float32),
            pltpu.VMEM((double, width), jnp.float32),
            pltpu.VMEM((double, width), jnp.float32),
        ],
        compiler_params=pltpu.CompilerParams(vmem_limit_bytes=56 * MIB),
        cost_estimate=pl.CostEstimate(
            flops=16 * length * double * width,
            bytes_accessed=12 * length * width,
            transcendentals=0,
        ),
    )(forward_table, inverse_table, product, spectra)


def whole_kernel(
    owner_ref, forward_ref, inverse_ref, taps_ref, sent_ref, out_ref,
    arrived, product, filters, data, mixed, ready, in_sems, out_sems,
):
    del owner_ref
    senders, height, _ = sent_ref.shape
    _, rows, _ = out_ref.shape
    places = senders // 2
    share = rows // 2
    count, double, _ = data.shape
    block = double // 2
    near = block // rows

    copies = []
    for step in range(count):
        for part in range(2):
            span = pl.ds(part * places + step * near, near)
            copies.append(
                pltpu.make_async_copy(sent_ref.at[span], arrived.at[span], in_sems.at[step, part])
            )
    for copy in copies:
        copy.start()

    row = lax.broadcasted_iota(jnp.int32, (SUBLANES, LANES), 0)
    weights = [
        jnp.where(row < 4, taps_ref[1, tap : tap + 1], taps_ref[2, tap : tap + 1])
        for tap in range(taps_ref.shape[1])
    ]
    own_rows = (row % 4) >= 2
    behind = [jnp.zeros((SUBLANES, LANES), jnp.float32)] * 2
    for step in range(count):
        for part in range(2):
            copies[2 * step + part].wait()
            lanes = slice(part * LANES, (part + 1) * LANES)
            for offset in range(near):
                sender = part * places + step * near + offset
                edge = arrived[sender, rows + share :].astype(jnp.float32)
                joined = jnp.where(own_rows, edge, behind[part])
                behind[part] = edge
                short = weights[0] * joined
                for tap in range(1, len(weights)):
                    short = short + weights[tap] * pltpu.roll(joined, tap, 0)
                first = pltpu.roll(short * pltpu.roll(short, 4, 0), 6, 0)
                values = arrived[sender, :rows].astype(jnp.float32)
                top = jnp.where(row < 2, first, values[:SUBLANES])
                values = jnp.concatenate([top, values[SUBLANES:]], axis=0)
                product[step, offset * rows : (offset + 1) * rows, lanes] = values.astype(
                    product.dtype
                )
                start = offset * rows + part * share
                half = (step % 2) * LANES
                filters[start : start + share, half : half + LANES] = arrived[
                    sender, rows : rows + share
                ]
        data[step, :, : 2 * LANES] = transform(forward_ref[...], product[step])
        if step % 2:
            both = transform(forward_ref[...], filters[...])
            data[step - 1, :, 2 * LANES :] = both[:, :LANES]
            data[step, :, 2 * LANES :] = both[:, LANES:]

    for sign, base in ((1, 0), (-1, block // 2)):

        @pl.loop(0, block // 2 // SUBLANES)
        def _(index):
            start = pl.multiple_of(base + index * SUBLANES, SUBLANES)
            real = pl.ds(start, SUBLANES)
            imag = pl.ds(pl.multiple_of(block + start, SUBLANES), SUBLANES)
            third = slice(2 * LANES, 3 * LANES)
            filter_parts = [
                (data[step, real, third], data[step, imag, third]) for step in range(count)
            ]
            for part in range(2):
                lanes = slice(part * LANES, (part + 1) * LANES)
                data_parts = [
                    (data[step, real, lanes], data[step, imag, lanes]) for step in range(count)
                ]
                before = None
                for total in range(count):
                    sums = None
                    for step in range(total + 1):
                        a, b = data_parts[step]
                        c, d = filter_parts[total - step]
                        term = (a * c - b * d, a * d + b * c)
                        sums = term if sums is None else (sums[0] + term[0], sums[1] + term[1])
                    if before is None:
                        both = sums
                    elif sign > 0:
                        both = (sums[0] - before[1], sums[1] + before[0])
                    else:
                        both = (sums[0] + before[1], sums[1] - before[0])
                    mixed[total, real, lanes] = both[0]
                    mixed[total, imag, lanes] = both[1]
                    before = sums

    copies = []
    for step in range(count):
        result = inverse(inverse_ref, mixed[step], block).astype(ready.dtype)
        for part in range(2):
            for offset in range(near):
                ready[part * places + step * near + offset] = result[
                    offset * rows : (offset + 1) * rows, part * LANES : (part + 1) * LANES
                ]
            span = pl.ds(part * places + step * near, near)
            copies.append(
                pltpu.make_async_copy(ready.at[span], out_ref.at[span], out_sems.at[step, part])
            )
            copies[-1].start()
    for copy in copies:
        copy.wait()


def convolve_whole(sent, short_weight, owner, rows, forward_table, inverse_table):
    senders, height, _ = sent.shape
    block = forward_table.shape[1]
    length = senders // 2 * rows
    count = length // block
    taps = short_weight.shape[1]
    whole = pl.BlockSpec(memory_space=pltpu.HBM)
    return pl.pallas_call(
        whole_kernel,
        out_shape=jax.ShapeDtypeStruct((senders, rows, LANES), jnp.bfloat16),
        grid_spec=pltpu.PrefetchScalarGridSpec(
            num_scalar_prefetch=1,
            grid=(1,),
            in_specs=[
                pl.BlockSpec(memory_space=pltpu.VMEM),
                pl.BlockSpec(memory_space=pltpu.VMEM),
                pl.BlockSpec((3, taps, LANES), lambda i, owner: (0, 0, owner[0])),
                whole,
            ],
            out_specs=whole,
            scratch_shapes=[
                pltpu.VMEM((senders, height, LANES), jnp.bfloat16),
                pltpu.VMEM((count, block, 2 * LANES), jnp.bfloat16),
                pltpu.VMEM((block, 2 * LANES), jnp.bfloat16),
                pltpu.VMEM((count, 2 * block, 3 * LANES), jnp.float32),
                pltpu.VMEM((count, 2 * block, 2 * LANES), jnp.float32),
                pltpu.VMEM((senders, rows, LANES), jnp.bfloat16),
                pltpu.SemaphoreType.DMA((count, 2)),
                pltpu.SemaphoreType.DMA((count, 2)),
            ],
        ),
        compiler_params=pltpu.CompilerParams(vmem_limit_bytes=32 * MIB),
        cost_estimate=pl.CostEstimate(
            flops=40 * length * block * LANES,
            bytes_accessed=2 * senders * (height + rows) * LANES,
            transcendentals=0,
        ),
    )(owner.reshape(1), forward_table, inverse_table, short_weight, sent)


def exchange(value, axes):
    return lax.all_to_all(value, axes, split_axis=0, concat_axis=0, tiled=True)


def on_device(query_in, key_in, value_in, long_filter, short_weight, skip_gain):
    places = lax.axis_size("seq")
    parts = lax.axis_size("groups")
    group = lax.axis_index("groups").astype(jnp.int32)
    place = lax.axis_index("seq").astype(jnp.int32)
    rows, channels = key_in.shape
    length = places * rows
    block = BLOCK if length % BLOCK == 0 else rows
    forward_table, inverse_table = transform_tables(block)
    forward_table = jnp.asarray(forward_table)
    inverse_table = jnp.asarray(inverse_table)
    rim = short_weight.shape[1] - 1
    owners = parts * places
    count = length // block
    aligned = (
        parts == 2
        and rim == 2
        and channels == owners * LANES
        and rows % 32 == 0
        and block % rows == 0
        and count % 2 == 0
        and count <= UNROLLED
    )
    edges = jnp.stack([query_in[-rim:], key_in[-rim:], value_in[-rim:]])

    if aligned:
        sent = pack(key_in, value_in, long_filter, short_weight, group, owners, parts)
        edges, sent = lax.optimization_barrier((edges, sent))
        received = exchange(sent, ("groups", "seq"))
        edges = from_behind(edges, "seq")
        product = products(key_in, value_in, edges, short_weight)
        owner = group * places + place
        convolved = convolve_whole(
            received, short_weight, owner, rows, forward_table, inverse_table
        )
        convolved = exchange(convolved, ("groups", "seq"))
    else:
        width = channels // places
        sent = long_filter.reshape(rows, places, width).transpose(1, 0, 2)
        spectra = filter_spectra(exchange(sent, "seq").reshape(length, width), forward_table)
        edges = from_behind(edges, "seq")
        product = products(key_in, value_in, edges, short_weight)
        sent = product.reshape(rows, places, width).transpose(1, 0, 2)
        received = exchange(sent, "seq").reshape(length, width)
        convolved = convolve(received, spectra, forward_table, inverse_table)
        convolved = exchange(convolved.reshape(places, rows, width), "seq")
        convolved = convolved.transpose(1, 0, 2).reshape(rows, channels // LANES, LANES)
        convolved = convolved.transpose(1, 0, 2)
    return gate(convolved, product, query_in, edges, short_weight, skip_gain)


def solution(mesh):
    placed = (
        P(("groups", "seq"), None),
        P(("groups", "seq"), None),
        P(("groups", "seq"), None),
        P("seq", None),
        P(),
        P(),
    )
    return jax.shard_map(
        on_device, mesh=mesh, in_specs=placed, out_specs=P(("groups", "seq"), None), check_vma=False
    )
```

time: 116 us -> 103 us (0.89)
  the two profiles are of different devices: /device:TPU:0 before, /device:TPU:16 now
where the time goes in v2:
time: 103 us; the launch traced here: 102 us
  waiting for transfers between devices  59.9 us (58%)
  Pallas kernels  24.5 us (24%)
  starting transfers between devices  14.2 us (14%)
  local copies, waits for them, and re-layouts  3.38 us (3%)
    all_to_all x2, waiting for transfers between devices, exchange(): return lax.all_to_all(value, axes, split_axis=0, concat_axis=0, tiled=True)  36.5 us
    ppermute x1, waiting for transfers between devices, from_behind(): lax.ppermute(value, axis, [(source, source + 1) for source in range(count...  23.4 us
    all_to_all x2, starting transfers between devices, exchange(): return lax.all_to_all(value, axes, split_axis=0, concat_axis=0, tiled=True)  12.1 us
    pallas_call x1, Pallas kernels, convolve_whole(): pl.pallas_call(whole_kernel, out_shape=jax.ShapeDtypeStruct((senders, row...  11.4 us
    pallas_call x1, Pallas kernels, pack(): pl.pallas_call(pack_kernel, out_shape=jax.ShapeDtypeStruct((owners, heigh...  4.48 us
    pallas_call x1, Pallas kernels, products(): pl.pallas_call(product_kernel, out_shape=jax.ShapeDtypeStruct((rows, chan...  4.31 us
    pallas_call x1, Pallas kernels, gate(): pl.pallas_call(gate_kernel, out_shape=jax.ShapeDtypeStruct((rows, channel...  4.29 us
  transfers between devices with their start and end apart: 3, of which 2 were waited for; matrix products, arithmetic and copies ran while one was open for 0% of the time, Pallas kernels for 4%

profile of v2, /device:TPU:16, one launch (start us, length us, event | category | flops | bytes accessed | tf_op | source)
XLA Modules:
  0.0 102.1 jit_solution(7273247351202245516)
XLA Ops:
  0.0 0.9 slice_bitcast_fusion.2
  0.9 0.9 slice_bitcast_fusion
  1.8 0.1 pad_maximum_fusion
  1.9 4.5 %shard_map.82 = bf16[32,200,128]{2,1,0:T(8,128)(2,1)} custom-call(s32[1]{0:T(128)} %bitcast.4.group_ref, bf16[128,4096]{1,0:T(8,128)(2,1)} %key_ref.3, bf16[128,4096]{1,0:T(8,128)(2,1)} %value_ref.3, bf16[128,4096]{1,0:T(8,128)(2,1)} %filter_ref.1, f32[3,3,4096]{2,1,0:T(4,128)} %taps_ref.7), custom_call_target="tpu_custom_call" | custom-call | flops 6291456 | bytes 4194304 | tf_op jit(solution)/shard_map/pallas_call | solution.py:159
  6.3 0.0 copy-start
  6.3 0.0 copy-start.1
  6.3 0.0 copy-start.2
  6.4 5.9 %all-to-all-start = ((bf16[32,200,128]{2,1,0:T(8,128)(2,1)}), bf16[32,200,128]{2,1,0:T(8,128)(2,1)S(1)}, u32[]{:S(2)}, u32[]{:S(2)}) async-start(bf16[32,200,128]{2,1,0:T(8,128)(2,1)} %shard_map.82), calls=%async_computation | async-start | bytes 3276800 | tf_op jit(solution)/shard_map/all_to_all | solution.py:449
  12.3 36.5 %all-to-all-done.sent_ref = bf16[32,200,128]{2,1,0:T(8,128)(2,1)S(1)} async-done(((bf16[32,200,128]{2,1,0:T(8,128)(2,1)}), bf16[32,200,128]{2,1,0:T(8,128)(2,1)S(1)}, u32[]{:S(2)}, u32[]{:S(2)}) %all-to-all-start) | async-done | bytes 1638432 | tf_op jit(solution)/shard_map/all_to_all | solution.py:449
  48.9 0.0 copy-done
  48.9 0.0 copy-done.1
  48.9 0.0 copy-done.2
  48.9 11.4 %shard_map.83 = bf16[32,128,128]{2,1,0:T(8,128)(2,1)} custom-call(s32[1]{0:T(128)} %bitcast.owner_ref, bf16[1024,256]{1,0:T(8,128)(2,1)S(1)} %copy-done.2, bf16[512,512]{1,0:T(8,128)(2,1)S(1)} %copy-done.1, f32[3,3,4096]{2,1,0:T(4,128)S(1)} %copy-done, bf16[32,200,128]{2,1,0:T(8,128)(2,1)S(1)} %all-to-all-done.sent_ref), custom_call_target="tpu_custom_call" | custom-call | flops 2684354560 | bytes 2686976 | tf_op jit(solution)/shard_map/pallas_call | solution.py:415
  60.3 6.2 %all-to-all-start.1 = ((bf16[32,128,128]{2,1,0:T(8,128)(2,1)}), bf16[32,128,128]{2,1,0:T(8,128)(2,1)S(1)}, u32[]{:S(2)}, u32[]{:S(2)}) async-start(bf16[32,128,128]{2,1,0:T(8,128)(2,1)} %shard_map.83), calls=%async_computation.1 | async-start | bytes 2097152 | tf_op jit(solution)/shard_map/all_to_all | solution.py:449
  66.4 2.1 %collective-permute-start = (bf16[3,2,4096]{2,1,0:T(2,128)(2,1)S(1)}, bf16[3,2,4096]{2,1,0:T(2,128)(2,1)S(1)}, u32[]{:S(2)}, u32[]{:S(2)}) collective-permute-start(bf16[3,2,4096]{2,1,0:T(2,128)(2,1)S(1)} %pad_maximum_fusion), channel_id=1, source_target_pairs={{0,1},{1,2},{2,3},{3,4},{4,5},{5,6},{6,7},{7,8},{8,9},{9,10},{10,1... | collective-permute-start | bytes 147464 | tf_op jit(solution)/shard_map/ppermute | solution.py:21
  68.5 23.4 %collective-permute-done.edge_ref = bf16[3,2,4096]{2,1,0:T(2,128)(2,1)S(1)} collective-permute-done((bf16[3,2,4096]{2,1,0:T(2,128)(2,1)S(1)}, bf16[3,2,4096]{2,1,0:T(2,128)(2,1)S(1)}, u32[]{:S(2)}, u32[]{:S(2)}) %collective-permute-start) | collective-permute-done | bytes 49184 | tf_op jit(solution)/shard_map/ppermute | solution.py:21
  91.9 0.0 copy-start.4
  91.9 0.6 copy-done.4
  92.5 4.3 %shard_map.84.product_ref = bf16[128,4096]{1,0:T(8,128)(2,1)} custom-call(bf16[128,4096]{1,0:T(8,128)(2,1)} %key_ref.3, bf16[128,4096]{1,0:T(8,128)(2,1)} %value_ref.3, bf16[3,2,4096]{2,1,0:T(2,128)(2,1)} %copy-done.4, f32[3,3,4096]{2,1,0:T(4,128)} %taps_ref.7), custom_call_target="tpu_custom_call" | custom-call | flops 6291456 | bytes 3145728 | tf_op jit(solution)/shard_map/pallas_call | solution.py:76
  96.8 0.0 all-to-all-done.1.conv_ref
  96.8 0.0 copy-start.3
  96.8 1.0 copy-done.3
  97.8 4.3 %shard_map.85 = bf16[128,4096]{1,0:T(8,128)(2,1)} custom-call(bf16[32,128,128]{2,1,0:T(8,128)(2,1)} %copy-done.3, bf16[128,4096]{1,0:T(8,128)(2,1)} %shard_map.84.product_ref, bf16[128,4096]{1,0:T(8,128)(2,1)} %query_ref.1, bf16[3,2,4096]{2,1,0:T(2,128)(2,1)} %copy-done.4, f32[3,3,4096]{2,1,0:T(4,128)} %taps_ref.7, f32[1,4096]{1,0:T(1,128)} %bitcast.9), custom_call_target="tpu_custom_call" | custom-call | flops 4718592 | bytes 4194304 | tf_op jit(solution)/shard_map/pallas_call | solution.py:108
Async XLA Ops:
  6.3 42.5 %copy-start = (f32[3,3,4096]{2,1,0:T(4,128)S(1)}, f32[3,3,4096]{2,1,0:T(4,128)}, u32[]{:S(2)}) copy-start(f32[3,3,4096]{2,1,0:T(4,128)} %taps_ref.7) | copy-start | bytes 442372
  6.3 42.5 %copy-start.1 = (bf16[512,512]{1,0:T(8,128)(2,1)S(1)}, bf16[512,512]{1,0:T(8,128)(2,1)}, u32[]{:S(2)}) copy-start(bf16[512,512]{1,0:T(8,128)(2,1)} %constant.16.clone.inverse_ref) | copy-start | bytes 1572868
  6.3 42.5 %copy-start.2 = (bf16[1024,256]{1,0:T(8,128)(2,1)S(1)}, bf16[1024,256]{1,0:T(8,128)(2,1)}, u32[]{:S(2)}) copy-start(bf16[1024,256]{1,0:T(8,128)(2,1)} %constant.15.clone.forward_ref) | copy-start | bytes 1572868
  6.4 42.5 %all-to-all-start = ((bf16[32,200,128]{2,1,0:T(8,128)(2,1)}), bf16[32,200,128]{2,1,0:T(8,128)(2,1)S(1)}, u32[]{:S(2)}, u32[]{:S(2)}) async-start(bf16[32,200,128]{2,1,0:T(8,128)(2,1)} %shard_map.82), calls=%async_computation | async-start | bytes 3276800 | tf_op jit(solution)/shard_map/all_to_all | solution.py:449
  60.3 36.6 %all-to-all-start.1 = ((bf16[32,128,128]{2,1,0:T(8,128)(2,1)}), bf16[32,128,128]{2,1,0:T(8,128)(2,1)S(1)}, u32[]{:S(2)}, u32[]{:S(2)}) async-start(bf16[32,128,128]{2,1,0:T(8,128)(2,1)} %shard_map.83), calls=%async_computation.1 | async-start | bytes 2097152 | tf_op jit(solution)/shard_map/all_to_all | solution.py:449
  66.4 25.5 %collective-permute-start = (bf16[3,2,4096]{2,1,0:T(2,128)(2,1)S(1)}, bf16[3,2,4096]{2,1,0:T(2,128)(2,1)S(1)}, u32[]{:S(2)}, u32[]{:S(2)}) collective-permute-start(bf16[3,2,4096]{2,1,0:T(2,128)(2,1)S(1)} %pad_maximum_fusion), channel_id=1, source_target_pairs={{0,1},{1,2},{2,3},{3,4},{4,5},{5,6},{6,7},{7,8},{8,9},{9,10},{10,1... | collective-permute-start | bytes 147464 | tf_op jit(solution)/shard_map/ppermute | solution.py:21
  91.9 0.6 copy-start.4
  96.8 1.0 copy-start.3

commit v3 on v2

--- a/solution.py
+++ b/solution.py
@@ -124,56 +124,160 @@
     )(convolved, product, query_in, edges, short_weight, skip_gain.reshape(1, channels))
 
 
-def pack_kernel(group_ref, key_ref, value_ref, filter_ref, taps_ref, out_ref):
-    del group_ref
-    rows = key_ref.shape[0]
-    share = filter_ref.shape[0]
+def finish_kernel(
+    conv_ref, product_ref, query_ref, edge_ref, taps_ref, gain_ref, out_ref, ready, sems
+):
+    channels = ready.shape[1]
+    chunks = sems.shape[0]
+    span = channels // chunks
+    near = span // LANES
+
+    def departure(chunk):
+        columns = pl.ds(pl.multiple_of(chunk * span, span), span)
+        return pltpu.make_async_copy(ready.at[:, columns], out_ref.at[:, columns], sems.at[chunk])
+
+    @pl.loop(0, chunks)
+    def _(chunk):
+        for part in range(near):
+            lanes = pl.ds(pl.multiple_of(chunk * span + part * LANES, LANES), LANES)
+            q_short = featurize(query_ref[:, lanes], edge_ref[0, :, lanes], taps_ref[0, :, lanes])
+            mixed = conv_ref[chunk * near + part].astype(jnp.float32) + gain_ref[
+                :, lanes
+            ] * product_ref[:, lanes].astype(jnp.float32)
+            ready[:, lanes] = (q_short * mixed).astype(ready.dtype)
+        departure(chunk).start()
+
+    for chunk in range(chunks):
+        departure(chunk).wait()
+
+
+def finish(convolved, product, query_in, edges, short_weight, skip_gain):
+    rows, channels = query_in.shape
+    chunks = max(1, channels // 512)
+    here = pl.BlockSpec(memory_space=pltpu.VMEM)
+    return pl.pallas_call(
+        finish_kernel,
+        out_shape=jax.ShapeDtypeStruct((rows, channels), jnp.bfloat16),
+        in_specs=[here] * 6,
+        out_specs=pl.BlockSpec(memory_space=pltpu.HBM),
+        scratch_shapes=[
+            pltpu.VMEM((rows, channels), jnp.bfloat16),
+            pltpu.SemaphoreType.DMA((chunks,)),
+        ],
+        compiler_params=pltpu.CompilerParams(vmem_limit_bytes=8 * MIB),
+        cost_estimate=pl.CostEstimate(
+            flops=9 * rows * channels, bytes_accessed=8 * rows * channels, transcendentals=0
+        ),
+    )(convolved, product, query_in, edges, short_weight, skip_gain.reshape(1, channels))
+
+
+def pack_kernel(
+    group_ref, query_ref, key_ref, value_ref, filter_ref, taps_ref, out_ref, edges_ref,
+    query, key, value, filters, taps, packed, edges, in_sems, one_sems, out_sems,
+):
+    rows, channels = key.shape
+    share = filters.shape[0]
+    rim = edges.shape[1]
+    chunks = out_sems.shape[0]
+    span = channels // chunks
+    near = span // LANES
+    start = pl.multiple_of(group_ref[0] * share, share)
+    whole = [
+        pltpu.make_async_copy(taps_ref, taps, one_sems.at[0]),
+        pltpu.make_async_copy(query_ref.at[pl.ds(rows - SUBLANES, SUBLANES)], query, one_sems.at[1]),
+    ]
+
+    def arrivals(chunk):
+        columns = pl.ds(pl.multiple_of(chunk * span, span), span)
+        return [
+            pltpu.make_async_copy(key_ref.at[:, columns], key.at[:, columns], in_sems.at[0, chunk]),
+            pltpu.make_async_copy(
+                value_ref.at[:, columns], value.at[:, columns], in_sems.at[1, chunk]
+            ),
+            pltpu.make_async_copy(
+                filter_ref.at[pl.ds(start, share), columns],
+                filters.at[:, columns],
+                in_sems.at[2, chunk],
+            ),
+        ]
+
+    def departure(chunk):
+        owners = pl.ds(chunk * near, near)
+        return pltpu.make_async_copy(packed.at[owners], out_ref.at[owners], out_sems.at[chunk])
+
+    for copy in whole:
+        copy.start()
+    for chunk in range(chunks):
+        for copy in arrivals(chunk):
+            copy.start()
+    for copy in whole:
+        copy.wait()
     row = lax.broadcasted_iota(jnp.int32, (SUBLANES, LANES), 0)
-    for part in range(out_ref.shape[0]):
-        span = slice(part * LANES, (part + 1) * LANES)
-        key = key_ref[:, span].astype(jnp.float32)
-        value = value_ref[:, span].astype(jnp.float32)
-        k_short = featurize_inside(key, taps_ref[1, :, span])
-        v_short = featurize_inside(value, taps_ref[2, :, span])
-        out_ref[part, :rows] = (k_short * v_short).astype(out_ref.dtype)
-        out_ref[part, rows : rows + share] = filter_ref[:, span]
-        key_tile = jnp.where(
-            row < 2,
-            pltpu.roll(key[rows - SUBLANES :], 2, 0),
-            pltpu.roll(key[:SUBLANES], 2, 0),
-        )
-        value_tile = jnp.where(
-            row < 6,
-            pltpu.roll(value[rows - SUBLANES :], 6, 0),
-            pltpu.roll(value[:SUBLANES], 6, 0),
-        )
-        edge = jnp.where(row < 4, key_tile, value_tile)
-        out_ref[part, rows + share :] = edge.astype(out_ref.dtype)
-
-
-def pack(key_in, value_in, long_filter, short_weight, group, owners, parts):
+
+    @pl.loop(0, chunks)
+    def _(chunk):
+        for copy in arrivals(chunk):
+            copy.wait()
+        for part in range(near):
+            span_here = pl.ds(pl.multiple_of(chunk * span + part * LANES, LANES), LANES)
+            owner = chunk * near + part
+            key_here = key[:, span_here].astype(jnp.float32)
+            value_here = value[:, span_here].astype(jnp.float32)
+            k_short = featurize_inside(key_here, taps[1, :, span_here])
+            v_short = featurize_inside(value_here, taps[2, :, span_here])
+            packed[owner, :rows] = (k_short * v_short).astype(packed.dtype)
+            packed[owner, rows : rows + share] = filters[:, span_here]
+            query_last = pltpu.roll(query[:, span_here].astype(jnp.float32), rim, 0)
+            key_last = pltpu.roll(key_here[rows - SUBLANES :], rim, 0)
+            value_last = pltpu.roll(value_here[rows - SUBLANES :], rim, 0)
+            key_tile = jnp.where(row < 2, key_last, pltpu.roll(key_here[:SUBLANES], 2, 0))
+            value_tile = jnp.where(
+                row < 6, pltpu.roll(value_last, 4, 0), pltpu.roll(value_here[:SUBLANES], 6, 0)
+            )
+            edge = jnp.where(row < 4, key_tile, value_tile)
+            packed[owner, rows + share :] = edge.astype(packed.dtype)
+            for stream, last in enumerate((query_last, key_last, value_last)):
+                edges[stream, :, span_here] = last[:rim].astype(edges.dtype)
+        departure(chunk).start()
+
+    last = pltpu.make_async_copy(edges, edges_ref, one_sems.at[0])
+    last.start()
+    for chunk in range(chunks):
+        departure(chunk).wait()
+    last.wait()
+
+
+def pack(query_in, key_in, value_in, long_filter, short_weight, group, owners, parts):
     rows, channels = key_in.shape
-    span = min(channels, 1024)
+    chunks = max(1, channels // 512)
     taps = short_weight.shape[1]
-    height = rows + rows // parts + SUBLANES
+    share = rows // parts
+    height = rows + share + SUBLANES
+    here = pl.BlockSpec(memory_space=pltpu.HBM)
     return pl.pallas_call(
         pack_kernel,
-        out_shape=jax.ShapeDtypeStruct((owners, height, LANES), jnp.bfloat16),
-        grid_spec=pltpu.PrefetchScalarGridSpec(
-            num_scalar_prefetch=1,
-            grid=(channels // span,),
-            in_specs=[
-                pl.BlockSpec((rows, span), lambda i, g: (0, i)),
-                pl.BlockSpec((rows, span), lambda i, g: (0, i)),
-                pl.BlockSpec((rows // parts, span), lambda i, g: (g[0], i)),
-                pl.BlockSpec((3, taps, span), lambda i, g: (0, 0, i)),
-            ],
-            out_specs=pl.BlockSpec((span // LANES, height, LANES), lambda i, g: (i, 0, 0)),
-        ),
+        out_shape=(
+            jax.ShapeDtypeStruct((owners, height, LANES), jnp.bfloat16),
+            jax.ShapeDtypeStruct((3, taps - 1, channels), jnp.bfloat16),
+        ),
+        in_specs=[pl.BlockSpec(memory_space=pltpu.SMEM)] + [here] * 5,
+        out_specs=(here, here),
+        scratch_shapes=[
+            pltpu.VMEM((SUBLANES, channels), jnp.bfloat16),
+            pltpu.VMEM((rows, channels), jnp.bfloat16),
+            pltpu.VMEM((rows, channels), jnp.bfloat16),
+            pltpu.VMEM((share, channels), jnp.bfloat16),
+            pltpu.VMEM((3, taps, channels), jnp.float32),
+            pltpu.VMEM((owners, height, LANES), jnp.bfloat16),
+            pltpu.VMEM((3, taps - 1, channels), jnp.bfloat16),
+            pltpu.SemaphoreType.DMA((3, chunks)),
+            pltpu.SemaphoreType.DMA((2,)),
+            pltpu.SemaphoreType.DMA((chunks,)),
+        ],
         cost_estimate=pl.CostEstimate(
             flops=12 * rows * channels, bytes_accessed=8 * rows * channels, transcendentals=0
         ),
-    )(group.reshape(1), key_in, value_in, long_filter, short_weight)
+    )(group.reshape(1), query_in, key_in, value_in, long_filter, short_weight)
 
 
 def transform(table, values):
@@ -295,27 +399,16 @@
 
 
 def whole_kernel(
-    owner_ref, forward_ref, inverse_ref, taps_ref, sent_ref, out_ref,
-    arrived, product, filters, data, mixed, ready, in_sems, out_sems,
+    owner_ref, forward_ref, inverse_ref, taps_ref, arrived, out_ref,
+    product, filters, data, mixed, ready, out_sems,
 ):
     del owner_ref
-    senders, height, _ = sent_ref.shape
-    _, rows, _ = out_ref.shape
+    senders, rows, _ = ready.shape
     places = senders // 2
     share = rows // 2
     count, double, _ = data.shape
     block = double // 2
     near = block // rows
-
-    copies = []
-    for step in range(count):
-        for part in range(2):
-            span = pl.ds(part * places + step * near, near)
-            copies.append(
-                pltpu.make_async_copy(sent_ref.at[span], arrived.at[span], in_sems.at[step, part])
-            )
-    for copy in copies:
-        copy.start()
 
     row = lax.broadcasted_iota(jnp.int32, (SUBLANES, LANES), 0)
     weights = [
@@ -326,7 +419,6 @@
     behind = [jnp.zeros((SUBLANES, LANES), jnp.float32)] * 2
     for step in range(count):
         for part in range(2):
-            copies[2 * step + part].wait()
             lanes = slice(part * LANES, (part + 1) * LANES)
             for offset in range(near):
                 sender = part * places + step * near + offset
@@ -411,7 +503,6 @@
     length = senders // 2 * rows
     count = length // block
     taps = short_weight.shape[1]
-    whole = pl.BlockSpec(memory_space=pltpu.HBM)
     return pl.pallas_call(
         whole_kernel,
         out_shape=jax.ShapeDtypeStruct((senders, rows, LANES), jnp.bfloat16),
@@ -422,17 +513,15 @@
                 pl.BlockSpec(memory_space=pltpu.VMEM),
                 pl.BlockSpec(memory_space=pltpu.VMEM),
                 pl.BlockSpec((3, taps, LANES), lambda i, owner: (0, 0, owner[0])),
-                whole,
+                pl.BlockSpec(memory_space=pltpu.VMEM),
             ],
-            out_specs=whole,
+            out_specs=pl.BlockSpec(memory_space=pltpu.HBM),
             scratch_shapes=[
-                pltpu.VMEM((senders, height, LANES), jnp.bfloat16),
                 pltpu.VMEM((count, block, 2 * LANES), jnp.bfloat16),
                 pltpu.VMEM((block, 2 * LANES), jnp.bfloat16),
                 pltpu.VMEM((count, 2 * block, 3 * LANES), jnp.float32),
                 pltpu.VMEM((count, 2 * block, 2 * LANES), jnp.float32),
                 pltpu.VMEM((senders, rows, LANES), jnp.bfloat16),
-                pltpu.SemaphoreType.DMA((count, 2)),
                 pltpu.SemaphoreType.DMA((count, 2)),
             ],
         ),
@@ -472,21 +561,23 @@
         and count % 2 == 0
         and count <= UNROLLED
     )
-    edges = jnp.stack([query_in[-rim:], key_in[-rim:], value_in[-rim:]])
-
     if aligned:
-        sent = pack(key_in, value_in, long_filter, short_weight, group, owners, parts)
-        edges, sent = lax.optimization_barrier((edges, sent))
+        sent, edges = pack(
+            query_in, key_in, value_in, long_filter, short_weight, group, owners, parts
+        )
         received = exchange(sent, ("groups", "seq"))
         edges = from_behind(edges, "seq")
         product = products(key_in, value_in, edges, short_weight)
+        received, product, edges = lax.optimization_barrier((received, product, edges))
         owner = group * places + place
         convolved = convolve_whole(
             received, short_weight, owner, rows, forward_table, inverse_table
         )
         convolved = exchange(convolved, ("groups", "seq"))
+        return finish(convolved, product, query_in, edges, short_weight, skip_gain)
     else:
         width = channels // places
+        edges = jnp.stack([query_in[-rim:], key_in[-rim:], value_in[-rim:]])
         sent = long_filter.reshape(rows, places, width).transpose(1, 0, 2)
         spectra = filter_spectra(exchange(sent, "seq").reshape(length, width), forward_table)
         edges = from_behind(edges, "seq")
@@ -497,7 +588,7 @@
         convolved = exchange(convolved.reshape(places, rows, width), "seq")
         convolved = convolved.transpose(1, 0, 2).reshape(rows, channels // LANES, LANES)
         convolved = convolved.transpose(1, 0, 2)
-    return gate(convolved, product, query_in, edges, short_weight, skip_gain)
+        return gate(convolved, product, query_in, edges, short_weight, skip_gain)
 
 
 def solution(mesh):

time: 103 us -> 99 us (0.961)
  the two profiles are of different devices: /device:TPU:16 before, /device:TPU:0 now
where the time goes in v3:
time: 99 us; the launch traced here: 98.6 us
  blocking collectives  34 us (34%)
  waiting for transfers between devices  32.9 us (33%)
  Pallas kernels  21.4 us (22%)
  starting transfers between devices  9.46 us (10%)
    all_to_all x1, blocking collectives, exchange(): return lax.all_to_all(value, axes, split_axis=0, concat_axis=0, tiled=True)  34 us
    all_to_all x1, waiting for transfers between devices, exchange(): return lax.all_to_all(value, axes, split_axis=0, concat_axis=0, tiled=True)  32.1 us
    pallas_call x1, Pallas kernels, convolve_whole(): pl.pallas_call(whole_kernel, out_shape=jax.ShapeDtypeStruct((senders, row...  10.6 us
    all_to_all x1, starting transfers between devices, exchange(): return lax.all_to_all(value, axes, split_axis=0, concat_axis=0, tiled=True)  7.3 us
    pallas_call x1, Pallas kernels, pack(): pl.pallas_call(pack_kernel, out_shape=(jax.ShapeDtypeStruct((owners, heig...  4.38 us
    pallas_call x1, Pallas kernels, products(): pl.pallas_call(product_kernel, out_shape=jax.ShapeDtypeStruct((rows, chan...  4.29 us
    ppermute x1, starting transfers between devices, from_behind(): lax.ppermute(value, axis, [(source, source + 1) for source in range(count...  2.16 us
    pallas_call x1, Pallas kernels, finish(): pl.pallas_call(finish_kernel, out_shape=jax.ShapeDtypeStruct((rows, chann...  2.09 us
  transfers between devices with their start and end apart: 2, of which 2 were waited for; matrix products, arithmetic and copies ran while one was open for 0% of the time, Pallas kernels for 4%

profile of v3, /device:TPU:0, one launch (start us, length us, event | category | flops | bytes accessed | tf_op | source)
XLA Modules:
  0.0 98.6 jit_solution(9649357943504108813)
XLA Ops:
  0.0 4.4 %shard_map.82 = (bf16[32,200,128]{2,1,0:T(8,128)(2,1)}, bf16[3,2,4096]{2,1,0:T(2,128)(2,1)}) custom-call(s32[1]{0:T(128)} %bitcast.1.group_ref, bf16[128,4096]{1,0:T(8,128)(2,1)} %query_ref.3, bf16[128,4096]{1,0:T(8,128)(2,1)} %key_ref.3, bf16[128,4096]{1,0:T(8,128)(2,1)} %value_ref.3, bf16[128,4096]{1,0:T(8,128)(2,1)} %filter_ref.1, f32[3,3,4096]{2,1,0:T(4,128)} %taps_ref.7), custom_call_target="tpu_custom_call" | custom-call | flops 6291456 | bytes 4194304 | tf_op jit(solution)/shard_map/pallas_call | solution.py:257
  4.4 0.0 copy-start.8
  4.4 7.3 %all-to-all-start = ((bf16[32,200,128]{2,1,0:T(8,128)(2,1)}), bf16[32,200,128]{2,1,0:T(8,128)(2,1)S(1)}, u32[]{:S(2)}, u32[]{:S(2)}) async-start(bf16[32,200,128]{2,1,0:T(8,128)(2,1)} %get-tuple-element.10), calls=%async_computation | async-start | bytes 3276800 | tf_op jit(solution)/shard_map/all_to_all | solution.py:538
  11.7 0.0 copy-done.8
  11.7 2.2 %collective-permute-start = (bf16[3,2,4096]{2,1,0:T(2,128)(2,1)S(1)}, bf16[3,2,4096]{2,1,0:T(2,128)(2,1)S(1)}, u32[]{:S(2)}, u32[]{:S(2)}) collective-permute-start(bf16[3,2,4096]{2,1,0:T(2,128)(2,1)S(1)} %copy-done.8), channel_id=1, source_target_pairs={{0,1},{1,2},{2,3},{3,4},{4,5},{5,6},{6,7},{7,8},{8,9},{9,10},{10,1... | collective-permute-start | bytes 147464 | tf_op jit(solution)/shard_map/ppermute | solution.py:21
  13.9 0.0 copy-start.2
  13.9 0.0 copy-start.6
  13.9 0.0 copy-start.7
  13.9 0.8 collective-permute-done.edge_ref
  14.7 0.0 copy-start.3
  14.8 0.6 copy-done.3
  15.4 4.3 %shard_map.83.product_ref = bf16[128,4096]{1,0:T(8,128)(2,1)} custom-call(bf16[128,4096]{1,0:T(8,128)(2,1)} %key_ref.3, bf16[128,4096]{1,0:T(8,128)(2,1)} %value_ref.3, bf16[3,2,4096]{2,1,0:T(2,128)(2,1)} %copy-done.3, f32[3,3,4096]{2,1,0:T(4,128)} %taps_ref.7), custom_call_target="tpu_custom_call" | custom-call | flops 6291456 | bytes 3145728 | tf_op jit(solution)/shard_map/pallas_call | solution.py:76
  19.7 32.1 %all-to-all-done.arrived = bf16[32,200,128]{2,1,0:T(8,128)(2,1)S(1)} async-done(((bf16[32,200,128]{2,1,0:T(8,128)(2,1)}), bf16[32,200,128]{2,1,0:T(8,128)(2,1)S(1)}, u32[]{:S(2)}, u32[]{:S(2)}) %all-to-all-start) | async-done | bytes 1638432 | tf_op jit(solution)/shard_map/all_to_all | solution.py:538
  51.8 0.0 copy-done.2
  51.8 0.0 copy-done.6
  51.8 0.0 copy-done.7
  51.8 0.0 copy-start.4
  51.8 0.0 copy-start.5
  51.8 10.6 %shard_map.84 = bf16[32,128,128]{2,1,0:T(8,128)(2,1)S(1)} custom-call(s32[1]{0:T(128)} %bitcast.owner_ref, bf16[1024,256]{1,0:T(8,128)(2,1)S(1)} %copy-done.7, bf16[512,512]{1,0:T(8,128)(2,1)S(1)} %copy-done.6, f32[3,3,4096]{2,1,0:T(4,128)S(1)} %copy-done.2, bf16[32,200,128]{2,1,0:T(8,128)(2,1)S(1)} %all-to-all-done.arrived), custom_call_target="tpu_custom_call" | custom-call | flops 2684354560 | bytes 2686976 | tf_op jit(solution)/shard_map/pallas_call | solution.py:506
  62.5 0.0 copy-start
  62.5 0.0 copy-start.1
  62.5 34.0 %all_to_all.10.conv_ref = bf16[32,128,128]{2,1,0:T(8,128)(2,1)S(1)} all-to-all(bf16[32,128,128]{2,1,0:T(8,128)(2,1)S(1)} %shard_map.84), channel_id=1, replica_groups=mesh['groups'=2,'seq'=16] {'groups','seq'}, dimensions={0} | all-to-all | bytes 2097152 | tf_op jit(solution)/shard_map/all_to_all | solution.py:538
  96.5 0.0 copy-done.4
  96.5 0.0 copy-done.5
  96.5 0.0 copy-done
  96.5 0.0 copy-done.1
  96.5 2.1 %shard_map.85 = bf16[128,4096]{1,0:T(8,128)(2,1)} custom-call(bf16[32,128,128]{2,1,0:T(8,128)(2,1)S(1)} %all_to_all.10.conv_ref, bf16[128,4096]{1,0:T(8,128)(2,1)S(1)} %copy-done.1, bf16[128,4096]{1,0:T(8,128)(2,1)S(1)} %copy-done, bf16[3,2,4096]{2,1,0:T(2,128)(2,1)S(1)} %copy-done.4, f32[3,3,4096]{2,1,0:T(4,128)S(1)} %copy-done.2, f32[1,4096]{1,0:T(1,128)S(1)} %bitcast.3), custom_call_target="tpu_custom_call" | custom-call | flops 4718592 | bytes 4194304 | tf_op jit(solution)/shard_map/pallas_call | solution.py:158
Async XLA Ops:
  4.4 7.3 %copy-start.8 = (bf16[3,2,4096]{2,1,0:T(2,128)(2,1)S(1)}, bf16[3,2,4096]{2,1,0:T(2,128)(2,1)}, u32[]{:S(2)}) copy-start(bf16[3,2,4096]{2,1,0:T(2,128)(2,1)} %get-tuple-element.11) | copy-start | bytes 147460
  4.4 47.4 %all-to-all-start = ((bf16[32,200,128]{2,1,0:T(8,128)(2,1)}), bf16[32,200,128]{2,1,0:T(8,128)(2,1)S(1)}, u32[]{:S(2)}, u32[]{:S(2)}) async-start(bf16[32,200,128]{2,1,0:T(8,128)(2,1)} %get-tuple-element.10), calls=%async_computation | async-start | bytes 3276800 | tf_op jit(solution)/shard_map/all_to_all | solution.py:538
  11.7 3.0 %collective-permute-start = (bf16[3,2,4096]{2,1,0:T(2,128)(2,1)S(1)}, bf16[3,2,4096]{2,1,0:T(2,128)(2,1)S(1)}, u32[]{:S(2)}, u32[]{:S(2)}) collective-permute-start(bf16[3,2,4096]{2,1,0:T(2,128)(2,1)S(1)} %copy-done.8), channel_id=1, source_target_pairs={{0,1},{1,2},{2,3},{3,4},{4,5},{5,6},{6,7},{7,8},{8,9},{9,10},{10,1... | collective-permute-start | bytes 147464 | tf_op jit(solution)/shard_map/ppermute | solution.py:21
  13.9 37.9 %copy-start.2 = (f32[3,3,4096]{2,1,0:T(4,128)S(1)}, f32[3,3,4096]{2,1,0:T(4,128)}, u32[]{:S(2)}) copy-start(f32[3,3,4096]{2,1,0:T(4,128)} %taps_ref.7) | copy-start | bytes 442372
  13.9 37.9 %copy-start.6 = (bf16[512,512]{1,0:T(8,128)(2,1)S(1)}, bf16[512,512]{1,0:T(8,128)(2,1)}, u32[]{:S(2)}) copy-start(bf16[512,512]{1,0:T(8,128)(2,1)} %constant.16.clone.inverse_ref) | copy-start | bytes 1572868
  13.9 37.9 %copy-start.7 = (bf16[1024,256]{1,0:T(8,128)(2,1)S(1)}, bf16[1024,256]{1,0:T(8,128)(2,1)}, u32[]{:S(2)}) copy-start(bf16[1024,256]{1,0:T(8,128)(2,1)} %constant.15.clone.forward_ref) | copy-start | bytes 1572868
  14.7 0.6 copy-start.3
  51.8 44.7 %copy-start.4 = (bf16[3,2,4096]{2,1,0:T(2,128)(2,1)S(1)}, bf16[3,2,4096]{2,1,0:T(2,128)(2,1)}, u32[]{:S(2)}) copy-start(bf16[3,2,4096]{2,1,0:T(2,128)(2,1)} %copy-done.3) | copy-start | bytes 147460
  51.8 44.7 %copy-start.5 = (f32[4096]{0:T(1024)S(1)}, f32[4096]{0:T(1024)}, u32[]{:S(2)}) copy-start(f32[4096]{0:T(1024)} %param.13) | copy-start | bytes 49156
  62.5 34.0 %copy-start = (bf16[128,4096]{1,0:T(8,128)(2,1)S(1)}, bf16[128,4096]{1,0:T(8,128)(2,1)}, u32[]{:S(2)}) copy-start(bf16[128,4096]{1,0:T(8,128)(2,1)} %query_ref.3) | copy-start | bytes 3145732
  62.5 34.0 %copy-start.1 = (bf16[128,4096]{1,0:T(8,128)(2,1)S(1)}, bf16[128,4096]{1,0:T(8,128)(2,1)}, u32[]{:S(2)}) copy-start(bf16[128,4096]{1,0:T(8,128)(2,1)} %shard_map.83.product_ref) | copy-start | bytes 3145732

commit v4 on v3

--- a/solution.py
+++ b/solution.py
@@ -125,12 +125,14 @@
 
 
 def finish_kernel(
-    conv_ref, product_ref, query_ref, edge_ref, taps_ref, gain_ref, out_ref, ready, sems
+    conv_ref, sent_ref, query_ref, edge_ref, taps_ref, gain_ref, out_ref, ready, sems
 ):
-    channels = ready.shape[1]
+    rows, channels = ready.shape
+    tail = sent_ref.shape[1] - SUBLANES
     chunks = sems.shape[0]
     span = channels // chunks
     near = span // LANES
+    row = lax.broadcasted_iota(jnp.int32, (SUBLANES, LANES), 0)
 
     def departure(chunk):
         columns = pl.ds(pl.multiple_of(chunk * span, span), span)
@@ -139,11 +141,26 @@
     @pl.loop(0, chunks)
     def _(chunk):
         for part in range(near):
-            lanes = pl.ds(pl.multiple_of(chunk * span + part * LANES, LANES), LANES)
-            q_short = featurize(query_ref[:, lanes], edge_ref[0, :, lanes], taps_ref[0, :, lanes])
-            mixed = conv_ref[chunk * near + part].astype(jnp.float32) + gain_ref[
-                :, lanes
-            ] * product_ref[:, lanes].astype(jnp.float32)
+            owner = chunk * near + part
+            lanes = pl.ds(pl.multiple_of(owner * LANES, LANES), LANES)
+            behind = edge_ref[:, lanes].astype(jnp.float32)
+            own = sent_ref[owner, tail:].astype(jnp.float32)
+            first = first_products(own, behind, tap_tiles(taps_ref, lanes))
+            first = first.astype(jnp.bfloat16).astype(jnp.float32)
+            product = sent_ref[owner, :rows].astype(jnp.float32)
+            top = jnp.where(row < 2, first, product[:SUBLANES])
+            product = jnp.concatenate([top, product[SUBLANES:]], axis=0)
+
+            query = query_ref[:, lanes].astype(jnp.float32)
+            weights = taps_ref[0, :, lanes]
+            top = query[:SUBLANES]
+            one = jnp.where(row < 1, pltpu.roll(behind, 5, 0), pltpu.roll(top, 1, 0))
+            two = jnp.where(row < 2, pltpu.roll(behind, 6, 0), pltpu.roll(top, 2, 0))
+            top = weights[0:1] * top + weights[1:2] * one + weights[2:3] * two
+            inside = featurize_inside(query, weights)
+            q_short = jnp.concatenate([top, inside[SUBLANES:]], axis=0)
+
+            mixed = conv_ref[owner].astype(jnp.float32) + gain_ref[:, lanes] * product
             ready[:, lanes] = (q_short * mixed).astype(ready.dtype)
         departure(chunk).start()
 
@@ -151,7 +168,7 @@
         departure(chunk).wait()
 
 
-def finish(convolved, product, query_in, edges, short_weight, skip_gain):
+def finish(convolved, sent, query_in, edges, short_weight, skip_gain):
     rows, channels = query_in.shape
     chunks = max(1, channels // 512)
     here = pl.BlockSpec(memory_space=pltpu.VMEM)
@@ -168,7 +185,24 @@
         cost_estimate=pl.CostEstimate(
             flops=9 * rows * channels, bytes_accessed=8 * rows * channels, transcendentals=0
         ),
-    )(convolved, product, query_in, edges, short_weight, skip_gain.reshape(1, channels))
+    )(convolved, sent, query_in, edges, short_weight, skip_gain.reshape(1, channels))
+
+
+def tap_tiles(taps_ref, lanes):
+    row = lax.broadcasted_iota(jnp.int32, (SUBLANES, LANES), 0)
+    return [
+        jnp.where(row < 4, taps_ref[1, tap : tap + 1, lanes], taps_ref[2, tap : tap + 1, lanes])
+        for tap in range(taps_ref.shape[1])
+    ]
+
+
+def first_products(tile, behind, weights):
+    row = lax.broadcasted_iota(jnp.int32, (SUBLANES, LANES), 0)
+    joined = jnp.where(row % 4 >= 2, tile, behind)
+    short = weights[0] * joined
+    for tap in range(1, len(weights)):
+        short = short + weights[tap] * pltpu.roll(joined, tap, 0)
+    return pltpu.roll(short * pltpu.roll(short, 4, 0), 6, 0)
 
 
 def pack_kernel(
@@ -177,7 +211,6 @@
 ):
     rows, channels = key.shape
     share = filters.shape[0]
-    rim = edges.shape[1]
     chunks = out_sems.shape[0]
     span = channels // chunks
     near = span // LANES
@@ -227,17 +260,21 @@
             v_short = featurize_inside(value_here, taps[2, :, span_here])
             packed[owner, :rows] = (k_short * v_short).astype(packed.dtype)
             packed[owner, rows : rows + share] = filters[:, span_here]
-            query_last = pltpu.roll(query[:, span_here].astype(jnp.float32), rim, 0)
-            key_last = pltpu.roll(key_here[rows - SUBLANES :], rim, 0)
-            value_last = pltpu.roll(value_here[rows - SUBLANES :], rim, 0)
-            key_tile = jnp.where(row < 2, key_last, pltpu.roll(key_here[:SUBLANES], 2, 0))
+            query_last = pltpu.roll(query[:, span_here].astype(jnp.float32), 4, 0)
+            key_tile = jnp.where(
+                row < 2,
+                pltpu.roll(key_here[rows - SUBLANES :], 2, 0),
+                pltpu.roll(key_here[:SUBLANES], 2, 0),
+            )
             value_tile = jnp.where(
-                row < 6, pltpu.roll(value_last, 4, 0), pltpu.roll(value_here[:SUBLANES], 6, 0)
+                row < 6,
+                pltpu.roll(value_here[rows - SUBLANES :], 6, 0),
+                pltpu.roll(value_here[:SUBLANES], 6, 0),
             )
             edge = jnp.where(row < 4, key_tile, value_tile)
             packed[owner, rows + share :] = edge.astype(packed.dtype)
-            for stream, last in enumerate((query_last, key_last, value_last)):
-                edges[stream, :, span_here] = last[:rim].astype(edges.dtype)
+            edge = jnp.where((row == 2) | (row == 3), query_last, edge)
+            edges[:, span_here] = edge.astype(edges.dtype)
         departure(chunk).start()
 
     last = pltpu.make_async_copy(edges, edges_ref, one_sems.at[0])
@@ -258,7 +295,7 @@
         pack_kernel,
         out_shape=(
             jax.ShapeDtypeStruct((owners, height, LANES), jnp.bfloat16),
-            jax.ShapeDtypeStruct((3, taps - 1, channels), jnp.bfloat16),
+            jax.ShapeDtypeStruct((SUBLANES, channels), jnp.bfloat16),
         ),
         in_specs=[pl.BlockSpec(memory_space=pltpu.SMEM)] + [here] * 5,
         out_specs=(here, here),
@@ -269,7 +306,7 @@
             pltpu.VMEM((share, channels), jnp.bfloat16),
             pltpu.VMEM((3, taps, channels), jnp.float32),
             pltpu.VMEM((owners, height, LANES), jnp.bfloat16),
-            pltpu.VMEM((3, taps - 1, channels), jnp.bfloat16),
+            pltpu.VMEM((SUBLANES, channels), jnp.bfloat16),
             pltpu.SemaphoreType.DMA((3, chunks)),
             pltpu.SemaphoreType.DMA((2,)),
             pltpu.SemaphoreType.DMA((chunks,)),
@@ -399,8 +436,8 @@
 
 
 def whole_kernel(
-    owner_ref, forward_ref, inverse_ref, taps_ref, arrived, out_ref,
-    product, filters, data, mixed, ready, out_sems,
+    owner_ref, forward_ref, inverse_ref, taps_ref, arrived, ready,
+    product, filters, data, mixed,
 ):
     del owner_ref
     senders, rows, _ = ready.shape
@@ -411,11 +448,7 @@
     near = block // rows
 
     row = lax.broadcasted_iota(jnp.int32, (SUBLANES, LANES), 0)
-    weights = [
-        jnp.where(row < 4, taps_ref[1, tap : tap + 1], taps_ref[2, tap : tap + 1])
-        for tap in range(taps_ref.shape[1])
-    ]
-    own_rows = (row % 4) >= 2
+    weights = tap_tiles(taps_ref, slice(None))
     behind = [jnp.zeros((SUBLANES, LANES), jnp.float32)] * 2
     for step in range(count):
         for part in range(2):
@@ -423,12 +456,8 @@
             for offset in range(near):
                 sender = part * places + step * near + offset
                 edge = arrived[sender, rows + share :].astype(jnp.float32)
-                joined = jnp.where(own_rows, edge, behind[part])
+                first = first_products(edge, behind[part], weights)
                 behind[part] = edge
-                short = weights[0] * joined
-                for tap in range(1, len(weights)):
-                    short = short + weights[tap] * pltpu.roll(joined, tap, 0)
-                first = pltpu.roll(short * pltpu.roll(short, 4, 0), 6, 0)
                 values = arrived[sender, :rows].astype(jnp.float32)
                 top = jnp.where(row < 2, first, values[:SUBLANES])
                 values = jnp.concatenate([top, values[SUBLANES:]], axis=0)
@@ -480,7 +509,6 @@
                     mixed[total, imag, lanes] = both[1]
                     before = sums
 
-    copies = []
     for step in range(count):
         result = inverse(inverse_ref, mixed[step], block).astype(ready.dtype)
         for part in range(2):
@@ -488,13 +516,6 @@
                 ready[part * places + step * near + offset] = result[
                     offset * rows : (offset + 1) * rows, part * LANES : (part + 1) * LANES
                 ]
-            span = pl.ds(part * places + step * near, near)
-            copies.append(
-                pltpu.make_async_copy(ready.at[span], out_ref.at[span], out_sems.at[step, part])
-            )
-            copies[-1].start()
-    for copy in copies:
-        copy.wait()
 
 
 def convolve_whole(sent, short_weight, owner, rows, forward_table, inverse_table):
@@ -515,14 +536,12 @@
                 pl.BlockSpec((3, taps, LANES), lambda i, owner: (0, 0, owner[0])),
                 pl.BlockSpec(memory_space=pltpu.VMEM),
             ],
-            out_specs=pl.BlockSpec(memory_space=pltpu.HBM),
+            out_specs=pl.BlockSpec(memory_space=pltpu.VMEM),
             scratch_shapes=[
                 pltpu.VMEM((count, block, 2 * LANES), jnp.bfloat16),
                 pltpu.VMEM((block, 2 * LANES), jnp.bfloat16),
                 pltpu.VMEM((count, 2 * block, 3 * LANES), jnp.float32),
                 pltpu.VMEM((count, 2 * block, 2 * LANES), jnp.float32),
-                pltpu.VMEM((senders, rows, LANES), jnp.bfloat16),
-                pltpu.SemaphoreType.DMA((count, 2)),
             ],
         ),
         compiler_params=pltpu.CompilerParams(vmem_limit_bytes=32 * MIB),
@@ -567,14 +586,13 @@
         )
         received = exchange(sent, ("groups", "seq"))
         edges = from_behind(edges, "seq")
-        product = products(key_in, value_in, edges, short_weight)
-        received, product, edges = lax.optimization_barrier((received, product, edges))
+        received, edges = lax.optimization_barrier((received, edges))
         owner = group * places + place
         convolved = convolve_whole(
             received, short_weight, owner, rows, forward_table, inverse_table
         )
         convolved = exchange(convolved, ("groups", "seq"))
-        return finish(convolved, product, query_in, edges, short_weight, skip_gain)
+        return finish(convolved, sent, query_in, edges, short_weight, skip_gain)
     else:
         width = channels // places
         edges = jnp.stack([query_in[-rim:], key_in[-rim:], value_in[-rim:]])

time: 99 us -> 90.1 us (0.910)
  Pallas kernels: 21.4 us -> 13.1 us
  waiting for transfers between devices: 32.9 us -> 37.9 us
  blocking collectives: 34 us -> 29.3 us
    all_to_all x1, waiting for transfers between devices: 32.1 us -> 37 us  [exchange(): return lax.all_to_all(value, axes, split_axis=0, concat_axis=0, tiled=True)]
    all_to_all x1, blocking collectives: 34 us -> 29.3 us  [exchange(): return lax.all_to_all(value, axes, split_axis=0, concat_axis=0, tiled=True)]
    pallas_call x1 -> x0, Pallas kernels: 4.29 us -> none  [products(): pl.pallas_call(product_kernel, out_shape=jax.ShapeDtypeStruct((rows, chan...]
    pallas_call x1, Pallas kernels: 10.6 us -> 6.53 us  [convolve_whole(): pl.pallas_call(whole_kernel, out_shape=jax.ShapeDtypeStruct((senders, row...]
  transfers between devices with their start and end apart: 2 -> 2, of which waited for: 2 -> 2; matrix products, arithmetic and copies ran while one was open for 0% -> 0% of each run, Pallas kernels for 4% -> 0%
where the time goes in v4:
time: 90.1 us; the launch traced here: 89.8 us
  waiting for transfers between devices  37.9 us (42%)
  blocking collectives  29.3 us (33%)
  Pallas kernels  13.1 us (15%)
  starting transfers between devices  9.46 us (10%)
    all_to_all x1, waiting for transfers between devices, exchange(): return lax.all_to_all(value, axes, split_axis=0, concat_axis=0, tiled=True)  37 us
    all_to_all x1, blocking collectives, exchange(): return lax.all_to_all(value, axes, split_axis=0, concat_axis=0, tiled=True)  29.3 us
    all_to_all x1, starting transfers between devices, exchange(): return lax.all_to_all(value, axes, split_axis=0, concat_axis=0, tiled=True)  7.3 us
    pallas_call x1, Pallas kernels, convolve_whole(): pl.pallas_call(whole_kernel, out_shape=jax.ShapeDtypeStruct((senders, row...  6.53 us
    pallas_call x1, Pallas kernels, pack(): pl.pallas_call(pack_kernel, out_shape=(jax.ShapeDtypeStruct((owners, heig...  4.36 us
    pallas_call x1, Pallas kernels, finish(): pl.pallas_call(finish_kernel, out_shape=jax.ShapeDtypeStruct((rows, chann...  2.18 us
    ppermute x1, starting transfers between devices, from_behind(): lax.ppermute(value, axis, [(source, source + 1) for source in range(count...  2.16 us
  transfers between devices with their start and end apart: 2, of which 2 were waited for; matrix products, arithmetic and copies ran while one was open for 0% of the time, Pallas kernels for 0%

profile of v4, /device:TPU:0, one launch (start us, length us, event | category | flops | bytes accessed | tf_op | source)
XLA Modules:
  0.0 89.8 jit_solution(11040145888681579591)
XLA Ops:
  0.0 4.4 %shard_map.82 = (bf16[32,200,128]{2,1,0:T(8,128)(2,1)}, bf16[8,4096]{1,0:T(8,128)(2,1)}) custom-call(s32[1]{0:T(128)} %bitcast.1.group_ref, bf16[128,4096]{1,0:T(8,128)(2,1)} %query_ref.3, bf16[128,4096]{1,0:T(8,128)(2,1)} %key_ref.1, bf16[128,4096]{1,0:T(8,128)(2,1)} %value_ref.1, bf16[128,4096]{1,0:T(8,128)(2,1)} %filter_ref.1, f32[3,3,4096]{2,1,0:T(4,128)} %taps_ref.5), custom_call_target="tpu_custom_call" | custom-call | flops 6291456 | bytes 4194304 | tf_op jit(solution)/shard_map/pallas_call | solution.py:294
  4.4 0.0 copy-start.6
  4.4 0.0 copy-start.2
  4.4 0.0 copy-start.4
  4.4 0.0 copy-start.5
  4.4 7.3 %all-to-all-start = ((bf16[32,200,128]{2,1,0:T(8,128)(2,1)}), bf16[32,200,128]{2,1,0:T(8,128)(2,1)S(1)}, u32[]{:S(2)}, u32[]{:S(2)}) async-start(bf16[32,200,128]{2,1,0:T(8,128)(2,1)} %get-tuple-element.9.sent_ref), calls=%async_computation | async-start | bytes 3276800 | tf_op jit(solution)/shard_map/all_to_all | solution.py:557
  11.7 0.0 copy-done.6
  11.7 2.2 %collective-permute-start = (bf16[8,4096]{1,0:T(8,128)(2,1)S(1)}, bf16[8,4096]{1,0:T(8,128)(2,1)S(1)}, u32[]{:S(2)}, u32[]{:S(2)}) collective-permute-start(bf16[8,4096]{1,0:T(8,128)(2,1)S(1)} %copy-done.6), channel_id=1, source_target_pairs={{0,1},{1,2},{2,3},{3,4},{4,5},{5,6},{6,7},{7,8},{8,9},{9,10},{10,1... | collective-permute-start | bytes 196616 | tf_op jit(solution)/shard_map/ppermute | solution.py:21
  13.9 0.9 collective-permute-done.edge_ref
  14.8 37.0 %all-to-all-done.arrived = bf16[32,200,128]{2,1,0:T(8,128)(2,1)S(1)} async-done(((bf16[32,200,128]{2,1,0:T(8,128)(2,1)}), bf16[32,200,128]{2,1,0:T(8,128)(2,1)S(1)}, u32[]{:S(2)}, u32[]{:S(2)}) %all-to-all-start) | async-done | bytes 1638432 | tf_op jit(solution)/shard_map/all_to_all | solution.py:557
  51.8 0.0 copy-done.2
  51.8 0.0 copy-done.4
  51.8 0.0 copy-done.5
  51.8 0.0 copy-start.1
  51.8 6.5 %shard_map.83 = bf16[32,128,128]{2,1,0:T(8,128)(2,1)S(1)} custom-call(s32[1]{0:T(128)} %bitcast.owner_ref, bf16[1024,256]{1,0:T(8,128)(2,1)S(1)} %copy-done.5, bf16[512,512]{1,0:T(8,128)(2,1)S(1)} %copy-done.4, f32[3,3,4096]{2,1,0:T(4,128)S(1)} %copy-done.2, bf16[32,200,128]{2,1,0:T(8,128)(2,1)S(1)} %all-to-all-done.arrived), custom_call_target="tpu_custom_call" | custom-call | flops 2684354560 | bytes 2686976 | tf_op jit(solution)/shard_map/pallas_call | solution.py:527
  58.4 0.0 copy-start
  58.4 0.0 copy-start.3
  58.4 29.3 %all_to_all.10.conv_ref = bf16[32,128,128]{2,1,0:T(8,128)(2,1)S(1)} all-to-all(bf16[32,128,128]{2,1,0:T(8,128)(2,1)S(1)} %shard_map.83), channel_id=1, replica_groups=mesh['groups'=2,'seq'=16] {'groups','seq'}, dimensions={0} | all-to-all | bytes 2097152 | tf_op jit(solution)/shard_map/all_to_all | solution.py:557
  87.7 0.0 copy-done.1
  87.7 0.0 copy-done
  87.7 0.0 copy-done.3
  87.7 2.2 %shard_map.84 = bf16[128,4096]{1,0:T(8,128)(2,1)} custom-call(bf16[32,128,128]{2,1,0:T(8,128)(2,1)S(1)} %all_to_all.10.conv_ref, bf16[32,200,128]{2,1,0:T(8,128)(2,1)S(1)} %copy-done, bf16[128,4096]{1,0:T(8,128)(2,1)S(1)} %copy-done.1, bf16[8,4096]{1,0:T(8,128)(2,1)S(1)} %collective-permute-done.edge_ref, f32[3,3,4096]{2,1,0:T(4,128)S(1)} %copy-done.2, ...), custom_call_target="tpu_custom_call" | custom-call | flops 4718592 | bytes 4194304 | tf_op jit(solution)/shard_map/pallas_call | solution.py:175
Async XLA Ops:
  4.4 7.4 %copy-start.6 = (bf16[8,4096]{1,0:T(8,128)(2,1)S(1)}, bf16[8,4096]{1,0:T(8,128)(2,1)}, u32[]{:S(2)}) copy-start(bf16[8,4096]{1,0:T(8,128)(2,1)} %get-tuple-element.10) | copy-start | bytes 196612
  4.4 47.4 %copy-start.2 = (f32[3,3,4096]{2,1,0:T(4,128)S(1)}, f32[3,3,4096]{2,1,0:T(4,128)}, u32[]{:S(2)}) copy-start(f32[3,3,4096]{2,1,0:T(4,128)} %taps_ref.5) | copy-start | bytes 442372
  4.4 47.4 %copy-start.4 = (bf16[512,512]{1,0:T(8,128)(2,1)S(1)}, bf16[512,512]{1,0:T(8,128)(2,1)}, u32[]{:S(2)}) copy-start(bf16[512,512]{1,0:T(8,128)(2,1)} %constant.16.clone.inverse_ref) | copy-start | bytes 1572868
  4.4 47.4 %copy-start.5 = (bf16[1024,256]{1,0:T(8,128)(2,1)S(1)}, bf16[1024,256]{1,0:T(8,128)(2,1)}, u32[]{:S(2)}) copy-start(bf16[1024,256]{1,0:T(8,128)(2,1)} %constant.15.clone.forward_ref) | copy-start | bytes 1572868
  4.4 47.4 %all-to-all-start = ((bf16[32,200,128]{2,1,0:T(8,128)(2,1)}), bf16[32,200,128]{2,1,0:T(8,128)(2,1)S(1)}, u32[]{:S(2)}, u32[]{:S(2)}) async-start(bf16[32,200,128]{2,1,0:T(8,128)(2,1)} %get-tuple-element.9.sent_ref), calls=%async_computation | async-start | bytes 3276800 | tf_op jit(solution)/shard_map/all_to_all | solution.py:557
  11.7 3.0 %collective-permute-start = (bf16[8,4096]{1,0:T(8,128)(2,1)S(1)}, bf16[8,4096]{1,0:T(8,128)(2,1)S(1)}, u32[]{:S(2)}, u32[]{:S(2)}) collective-permute-start(bf16[8,4096]{1,0:T(8,128)(2,1)S(1)} %copy-done.6), channel_id=1, source_target_pairs={{0,1},{1,2},{2,3},{3,4},{4,5},{5,6},{6,7},{7,8},{8,9},{9,10},{10,1... | collective-permute-start | bytes 196616 | tf_op jit(solution)/shard_map/ppermute | solution.py:21
  51.8 35.8 %copy-start.1 = (bf16[128,4096]{1,0:T(8,128)(2,1)S(1)}, bf16[128,4096]{1,0:T(8,128)(2,1)}, u32[]{:S(2)}) copy-start(bf16[128,4096]{1,0:T(8,128)(2,1)} %query_ref.3) | copy-start | bytes 3145732
  58.4 29.3 %copy-start = (bf16[32,200,128]{2,1,0:T(8,128)(2,1)S(1)}, bf16[32,200,128]{2,1,0:T(8,128)(2,1)}, u32[]{:S(2)}) copy-start(bf16[32,200,128]{2,1,0:T(8,128)(2,1)} %get-tuple-element.9.sent_ref) | copy-start | bytes 4915204
  58.4 29.3 %copy-start.3 = (f32[4096]{0:T(1024)S(1)}, f32[4096]{0:T(1024)}, u32[]{:S(2)}) copy-start(f32[4096]{0:T(1024)} %param.13) | copy-start | bytes 49156

commit v5 on v4

--- a/solution.py
+++ b/solution.py
@@ -33,6 +33,16 @@
         return np.concatenate([high, low], axis=0)
 
     return split(table), split(table.T / block)
+
+
+def half_tables(block):
+    forward, inverse = transform_tables(block)
+    half = block // 2
+    rows = np.arange(2 * block).reshape(2, 2, half).transpose(1, 0, 2).reshape(2, block)
+    forward = forward.reshape(2, 2 * block, block)
+    forward = np.stack([forward[:, rows[side]].reshape(2 * block, block) for side in range(2)])
+    inverse = np.stack([inverse[:, rows[side]] for side in range(2)])
+    return forward, inverse
 
 
 def shifted(values, edge, steps):
@@ -286,7 +296,7 @@
 
 def pack(query_in, key_in, value_in, long_filter, short_weight, group, owners, parts):
     rows, channels = key_in.shape
-    chunks = max(1, channels // 512)
+    chunks = max(1, channels // 1024)
     taps = short_weight.shape[1]
     share = rows // parts
     height = rows + share + SUBLANES
@@ -437,18 +447,57 @@
 
 def whole_kernel(
     owner_ref, forward_ref, inverse_ref, taps_ref, arrived, ready,
-    product, filters, data, mixed,
+    product, filters, data, known, mixed, partly,
 ):
     del owner_ref
     senders, rows, _ = ready.shape
     places = senders // 2
     share = rows // 2
-    count, double, _ = data.shape
-    block = double // 2
+    _, count, block, _ = data.shape
+    half = block // 2
     near = block // rows
-
+    tiles = half // SUBLANES // count
     row = lax.broadcasted_iota(jnp.int32, (SUBLANES, LANES), 0)
     weights = tap_tiles(taps_ref, slice(None))
+
+    def forward(side, values):
+        return transform(forward_ref[side], values)
+
+    def backward(side, step):
+        return inverse(inverse_ref.at[side], mixed[side, step], block)
+
+    def multiply(side, tile):
+        start = tile * SUBLANES
+        real = slice(start, start + SUBLANES)
+        imag = slice(half + start, half + start + SUBLANES)
+        filter_parts = []
+        for step in range(count):
+            c, d = known[side, step, real], known[side, step, imag]
+            filter_parts.append((c, d - c, c + d))
+        for part in range(2):
+            lanes = slice(part * LANES, (part + 1) * LANES)
+            data_parts = []
+            for step in range(count):
+                a, b = data[side, step, real, lanes], data[side, step, imag, lanes]
+                data_parts.append((a + b, a, b))
+            before = None
+            for total in range(count):
+                sums = None
+                for step in range(total + 1):
+                    pairs = zip(data_parts[step], filter_parts[total - step])
+                    terms = [x * y for x, y in pairs]
+                    sums = terms if sums is None else [x + y for x, y in zip(sums, terms)]
+                both = (sums[0] - sums[2], sums[0] + sums[1])
+                if before is None:
+                    out = both
+                elif side == 0:
+                    out = (both[0] - before[1], both[1] + before[0])
+                else:
+                    out = (both[0] + before[1], both[1] - before[0])
+                mixed[side, total, real, lanes] = out[0]
+                mixed[side, total, imag, lanes] = out[1]
+                before = both
+
     behind = [jnp.zeros((SUBLANES, LANES), jnp.float32)] * 2
     for step in range(count):
         for part in range(2):
@@ -458,59 +507,38 @@
                 edge = arrived[sender, rows + share :].astype(jnp.float32)
                 first = first_products(edge, behind[part], weights)
                 behind[part] = edge
-                values = arrived[sender, :rows].astype(jnp.float32)
+                values = arrived[sender, : 2 * SUBLANES].astype(jnp.float32)
                 top = jnp.where(row < 2, first, values[:SUBLANES])
                 values = jnp.concatenate([top, values[SUBLANES:]], axis=0)
-                product[step, offset * rows : (offset + 1) * rows, lanes] = values.astype(
-                    product.dtype
-                )
+                start = offset * rows
+                product[step, start : start + 2 * SUBLANES, lanes] = values.astype(product.dtype)
+                product[step, start + 2 * SUBLANES : start + rows, lanes] = arrived[
+                    sender, 2 * SUBLANES : rows
+                ]
                 start = offset * rows + part * share
-                half = (step % 2) * LANES
-                filters[start : start + share, half : half + LANES] = arrived[
+                place = (step % 2) * LANES
+                filters[step // 2, start : start + share, place : place + LANES] = arrived[
                     sender, rows : rows + share
                 ]
-        data[step, :, : 2 * LANES] = transform(forward_ref[...], product[step])
+        data[0, step] = forward(0, product[step])
         if step % 2:
-            both = transform(forward_ref[...], filters[...])
-            data[step - 1, :, 2 * LANES :] = both[:, :LANES]
-            data[step, :, 2 * LANES :] = both[:, LANES:]
-
-    for sign, base in ((1, 0), (-1, block // 2)):
-
-        @pl.loop(0, block // 2 // SUBLANES)
-        def _(index):
-            start = pl.multiple_of(base + index * SUBLANES, SUBLANES)
-            real = pl.ds(start, SUBLANES)
-            imag = pl.ds(pl.multiple_of(block + start, SUBLANES), SUBLANES)
-            third = slice(2 * LANES, 3 * LANES)
-            filter_parts = [
-                (data[step, real, third], data[step, imag, third]) for step in range(count)
-            ]
-            for part in range(2):
-                lanes = slice(part * LANES, (part + 1) * LANES)
-                data_parts = [
-                    (data[step, real, lanes], data[step, imag, lanes]) for step in range(count)
-                ]
-                before = None
-                for total in range(count):
-                    sums = None
-                    for step in range(total + 1):
-                        a, b = data_parts[step]
-                        c, d = filter_parts[total - step]
-                        term = (a * c - b * d, a * d + b * c)
-                        sums = term if sums is None else (sums[0] + term[0], sums[1] + term[1])
-                    if before is None:
-                        both = sums
-                    elif sign > 0:
-                        both = (sums[0] - before[1], sums[1] + before[0])
-                    else:
-                        both = (sums[0] + before[1], sums[1] - before[0])
-                    mixed[total, real, lanes] = both[0]
-                    mixed[total, imag, lanes] = both[1]
-                    before = sums
+            for side in range(2):
+                both = forward(side, filters[step // 2])
+                known[side, step - 1] = both[:, :LANES]
+                known[side, step] = both[:, LANES:]
 
     for step in range(count):
-        result = inverse(inverse_ref, mixed[step], block).astype(ready.dtype)
+        for tile in range(tiles):
+            multiply(0, step * tiles + tile)
+        data[1, step] = forward(1, product[step])
+
+    for step in range(count):
+        for tile in range(tiles):
+            multiply(1, step * tiles + tile)
+        partly[step] = backward(0, step)
+
+    for step in range(count):
+        result = (partly[step] + backward(1, step)).astype(ready.dtype)
         for part in range(2):
             for offset in range(near):
                 ready[part * places + step * near + offset] = result[
@@ -520,7 +548,7 @@
 
 def convolve_whole(sent, short_weight, owner, rows, forward_table, inverse_table):
     senders, height, _ = sent.shape
-    block = forward_table.shape[1]
+    block = forward_table.shape[2]
     length = senders // 2 * rows
     count = length // block
     taps = short_weight.shape[1]
@@ -539,9 +567,11 @@
             out_specs=pl.BlockSpec(memory_space=pltpu.VMEM),
             scratch_shapes=[
                 pltpu.VMEM((count, block, 2 * LANES), jnp.bfloat16),
-                pltpu.VMEM((block, 2 * LANES), jnp.bfloat16),
-                pltpu.VMEM((count, 2 * block, 3 * LANES), jnp.float32),
-                pltpu.VMEM((count, 2 * block, 2 * LANES), jnp.float32),
+                pltpu.VMEM((count // 2, block, 2 * LANES), jnp.bfloat16),
+                pltpu.VMEM((2, count, block, 2 * LANES), jnp.float32),
+                pltpu.VMEM((2, count, block, LANES), jnp.float32),
+                pltpu.VMEM((2, count, block, 2 * LANES), jnp.float32),
+                pltpu.VMEM((count, block, 2 * LANES), jnp.float32),
             ],
         ),
         compiler_params=pltpu.CompilerParams(vmem_limit_bytes=32 * MIB),
@@ -565,9 +595,6 @@
     rows, channels = key_in.shape
     length = places * rows
     block = BLOCK if length % BLOCK == 0 else rows
-    forward_table, inverse_table = transform_tables(block)
-    forward_table = jnp.asarray(forward_table)
-    inverse_table = jnp.asarray(inverse_table)
     rim = short_weight.shape[1] - 1
     owners = parts * places
     count = length // block
@@ -577,9 +604,12 @@
         and channels == owners * LANES
         and rows % 32 == 0
         and block % rows == 0
-        and count % 2 == 0
-        and count <= UNROLLED
+        and block == BLOCK
+        and count in (2, 4, 8)
     )
+    forward_table, inverse_table = half_tables(block) if aligned else transform_tables(block)
+    forward_table = jnp.asarray(forward_table)
+    inverse_table = jnp.asarray(inverse_table)
     if aligned:
         sent, edges = pack(
             query_in, key_in, value_in, long_filter, short_weight, group, owners, parts

time: 90.1 us -> 88.3 us (0.980)
  Pallas kernels: 13.1 us -> 11.2 us
    pallas_call x1, Pallas kernels: 6.53 us -> 4.91 us  [convolve_whole(): pl.pallas_call(whole_kernel, out_shape=jax.ShapeDtypeStruct((senders, row...]
where the time goes in v5:
time: 88.3 us; the launch traced here: 88 us
  waiting for transfers between devices  37.9 us (43%)
  blocking collectives  29.3 us (33%)
  Pallas kernels  11.2 us (13%)
  starting transfers between devices  9.46 us (11%)
    all_to_all x1, waiting for transfers between devices, exchange(): return lax.all_to_all(value, axes, split_axis=0, concat_axis=0, tiled=True)  37 us
    all_to_all x1, blocking collectives, exchange(): return lax.all_to_all(value, axes, split_axis=0, concat_axis=0, tiled=True)  29.3 us
    all_to_all x1, starting transfers between devices, exchange(): return lax.all_to_all(value, axes, split_axis=0, concat_axis=0, tiled=True)  7.3 us
    pallas_call x1, Pallas kernels, convolve_whole(): pl.pallas_call(whole_kernel, out_shape=jax.ShapeDtypeStruct((senders, row...  4.91 us
    pallas_call x1, Pallas kernels, pack(): pl.pallas_call(pack_kernel, out_shape=(jax.ShapeDtypeStruct((owners, heig...  4.16 us
    pallas_call x1, Pallas kernels, finish(): pl.pallas_call(finish_kernel, out_shape=jax.ShapeDtypeStruct((rows, chann...  2.18 us
    ppermute x1, starting transfers between devices, from_behind(): lax.ppermute(value, axis, [(source, source + 1) for source in range(count...  2.16 us
  transfers between devices with their start and end apart: 2, of which 2 were waited for; matrix products, arithmetic and copies ran while one was open for 0% of the time, Pallas kernels for 0%

profile of v5, /device:TPU:0, one launch (start us, length us, event | category | flops | bytes accessed | tf_op | source)
XLA Modules:
  0.0 88.0 jit_solution(191688477879694240)
XLA Ops:
  0.0 4.2 %shard_map.82 = (bf16[32,200,128]{2,1,0:T(8,128)(2,1)}, bf16[8,4096]{1,0:T(8,128)(2,1)}) custom-call(s32[1]{0:T(128)} %bitcast.1.group_ref, bf16[128,4096]{1,0:T(8,128)(2,1)} %query_ref.3, bf16[128,4096]{1,0:T(8,128)(2,1)} %key_ref.1, bf16[128,4096]{1,0:T(8,128)(2,1)} %value_ref.1, bf16[128,4096]{1,0:T(8,128)(2,1)} %filter_ref.1, f32[3,3,4096]{2,1,0:T(4,128)} %taps_ref.5), custom_call_target="tpu_custom_call" | custom-call | flops 6291456 | bytes 4194304 | tf_op jit(solution)/shard_map/pallas_call | solution.py:304
  4.2 0.0 copy-start.6
  4.2 0.0 copy-start.2
  4.2 0.0 copy-start.4
  4.2 0.0 copy-start.5
  4.2 7.3 %all-to-all-start = ((bf16[32,200,128]{2,1,0:T(8,128)(2,1)}), bf16[32,200,128]{2,1,0:T(8,128)(2,1)S(1)}, u32[]{:S(2)}, u32[]{:S(2)}) async-start(bf16[32,200,128]{2,1,0:T(8,128)(2,1)} %get-tuple-element.9.sent_ref), calls=%async_computation | async-start | bytes 3276800 | tf_op jit(solution)/shard_map/all_to_all | solution.py:587
  11.5 0.0 copy-done.6
  11.5 2.2 %collective-permute-start = (bf16[8,4096]{1,0:T(8,128)(2,1)S(1)}, bf16[8,4096]{1,0:T(8,128)(2,1)S(1)}, u32[]{:S(2)}, u32[]{:S(2)}) collective-permute-start(bf16[8,4096]{1,0:T(8,128)(2,1)S(1)} %copy-done.6), channel_id=1, source_target_pairs={{0,1},{1,2},{2,3},{3,4},{4,5},{5,6},{6,7},{7,8},{8,9},{9,10},{10,1... | collective-permute-start | bytes 196616 | tf_op jit(solution)/shard_map/ppermute | solution.py:21
  13.7 0.9 collective-permute-done.edge_ref
  14.6 37.0 %all-to-all-done.arrived = bf16[32,200,128]{2,1,0:T(8,128)(2,1)S(1)} async-done(((bf16[32,200,128]{2,1,0:T(8,128)(2,1)}), bf16[32,200,128]{2,1,0:T(8,128)(2,1)S(1)}, u32[]{:S(2)}, u32[]{:S(2)}) %all-to-all-start) | async-done | bytes 1638432 | tf_op jit(solution)/shard_map/all_to_all | solution.py:587
  51.6 0.0 copy-done.2
  51.6 0.0 copy-done.4
  51.6 0.0 copy-done.5
  51.6 0.0 copy-start.1
  51.6 4.9 %shard_map.83 = bf16[32,128,128]{2,1,0:T(8,128)(2,1)S(1)} custom-call(s32[1]{0:T(128)} %bitcast.owner_ref, bf16[2,512,256]{2,1,0:T(8,128)(2,1)S(1)} %copy-done.5, bf16[2,512,256]{2,1,0:T(8,128)(2,1)S(1)} %copy-done.4, f32[3,3,4096]{2,1,0:T(4,128)S(1)} %copy-done.2, bf16[32,200,128]{2,1,0:T(8,128)(2,1)S(1)} %all-to-all-done.arrived), custom_call_target="tpu_custom_call" | custom-call | flops 2684354560 | bytes 2686976 | tf_op jit(solution)/shard_map/pallas_call | solution.py:555
  56.5 0.0 copy-start
  56.5 0.0 copy-start.3
  56.6 29.3 %all_to_all.10.conv_ref = bf16[32,128,128]{2,1,0:T(8,128)(2,1)S(1)} all-to-all(bf16[32,128,128]{2,1,0:T(8,128)(2,1)S(1)} %shard_map.83), channel_id=1, replica_groups=mesh['groups'=2,'seq'=16] {'groups','seq'}, dimensions={0} | all-to-all | bytes 2097152 | tf_op jit(solution)/shard_map/all_to_all | solution.py:587
  85.8 0.0 copy-done.1
  85.8 0.0 copy-done
  85.8 0.0 copy-done.3
  85.8 2.2 %shard_map.84 = bf16[128,4096]{1,0:T(8,128)(2,1)} custom-call(bf16[32,128,128]{2,1,0:T(8,128)(2,1)S(1)} %all_to_all.10.conv_ref, bf16[32,200,128]{2,1,0:T(8,128)(2,1)S(1)} %copy-done, bf16[128,4096]{1,0:T(8,128)(2,1)S(1)} %copy-done.1, bf16[8,4096]{1,0:T(8,128)(2,1)S(1)} %collective-permute-done.edge_ref, f32[3,3,4096]{2,1,0:T(4,128)S(1)} %copy-done.2, ...), custom_call_target="tpu_custom_call" | custom-call | flops 4718592 | bytes 4194304 | tf_op jit(solution)/shard_map/pallas_call | solution.py:185
Async XLA Ops:
  4.2 7.4 %copy-start.6 = (bf16[8,4096]{1,0:T(8,128)(2,1)S(1)}, bf16[8,4096]{1,0:T(8,128)(2,1)}, u32[]{:S(2)}) copy-start(bf16[8,4096]{1,0:T(8,128)(2,1)} %get-tuple-element.10) | copy-start | bytes 196612
  4.2 47.4 %copy-start.2 = (f32[3,3,4096]{2,1,0:T(4,128)S(1)}, f32[3,3,4096]{2,1,0:T(4,128)}, u32[]{:S(2)}) copy-start(f32[3,3,4096]{2,1,0:T(4,128)} %taps_ref.5) | copy-start | bytes 442372
  4.2 47.4 %copy-start.4 = (bf16[2,512,256]{2,1,0:T(8,128)(2,1)S(1)}, bf16[2,512,256]{2,1,0:T(8,128)(2,1)}, u32[]{:S(2)}) copy-start(bf16[2,512,256]{2,1,0:T(8,128)(2,1)} %constant.16.clone.inverse_ref) | copy-start | bytes 1572868
  4.2 47.4 %copy-start.5 = (bf16[2,512,256]{2,1,0:T(8,128)(2,1)S(1)}, bf16[2,512,256]{2,1,0:T(8,128)(2,1)}, u32[]{:S(2)}) copy-start(bf16[2,512,256]{2,1,0:T(8,128)(2,1)} %constant.15.clone.forward_ref) | copy-start | bytes 1572868
  4.2 47.4 %all-to-all-start = ((bf16[32,200,128]{2,1,0:T(8,128)(2,1)}), bf16[32,200,128]{2,1,0:T(8,128)(2,1)S(1)}, u32[]{:S(2)}, u32[]{:S(2)}) async-start(bf16[32,200,128]{2,1,0:T(8,128)(2,1)} %get-tuple-element.9.sent_ref), calls=%async_computation | async-start | bytes 3276800 | tf_op jit(solution)/shard_map/all_to_all | solution.py:587
  11.5 3.0 %collective-permute-start = (bf16[8,4096]{1,0:T(8,128)(2,1)S(1)}, bf16[8,4096]{1,0:T(8,128)(2,1)S(1)}, u32[]{:S(2)}, u32[]{:S(2)}) collective-permute-start(bf16[8,4096]{1,0:T(8,128)(2,1)S(1)} %copy-done.6), channel_id=1, source_target_pairs={{0,1},{1,2},{2,3},{3,4},{4,5},{5,6},{6,7},{7,8},{8,9},{9,10},{10,1... | collective-permute-start | bytes 196616 | tf_op jit(solution)/shard_map/ppermute | solution.py:21
  51.6 34.2 %copy-start.1 = (bf16[128,4096]{1,0:T(8,128)(2,1)S(1)}, bf16[128,4096]{1,0:T(8,128)(2,1)}, u32[]{:S(2)}) copy-start(bf16[128,4096]{1,0:T(8,128)(2,1)} %query_ref.3) | copy-start | bytes 3145732
  56.5 29.3 %copy-start = (bf16[32,200,128]{2,1,0:T(8,128)(2,1)S(1)}, bf16[32,200,128]{2,1,0:T(8,128)(2,1)}, u32[]{:S(2)}) copy-start(bf16[32,200,128]{2,1,0:T(8,128)(2,1)} %get-tuple-element.9.sent_ref) | copy-start | bytes 4915204
  56.5 29.3 %copy-start.3 = (f32[4096]{0:T(1024)S(1)}, f32[4096]{0:T(1024)}, u32[]{:S(2)}) copy-start(f32[4096]{0:T(1024)} %param.13) | copy-start | bytes 49156

commit v6 on v5

--- a/solution.py
+++ b/solution.py
@@ -134,8 +134,43 @@
     )(convolved, product, query_in, edges, short_weight, skip_gain.reshape(1, channels))
 
 
+def prepare_kernel(sent_ref, query_ref, taps_ref, gain_ref, short_ref, direct_ref):
+    owners, rows, _ = short_ref.shape
+    for owner in range(owners):
+        lanes = slice(owner * LANES, (owner + 1) * LANES)
+        q_short = featurize_inside(query_ref[:, lanes].astype(jnp.float32), taps_ref[0, :, lanes])
+        product = sent_ref[owner, :rows].astype(jnp.float32)
+        short_ref[owner] = q_short
+        direct_ref[owner] = q_short * (gain_ref[:, lanes] * product)
+
+
+def prepare(sent, query_in, short_weight, skip_gain):
+    rows, channels = query_in.shape
+    owners, height, _ = sent.shape
+    near = min(owners, 8)
+    span = near * LANES
+    taps = short_weight.shape[1]
+    out = pl.BlockSpec((near, rows, LANES), lambda i: (i, 0, 0))
+    return pl.pallas_call(
+        prepare_kernel,
+        out_shape=(jax.ShapeDtypeStruct((owners, rows, LANES), jnp.float32),) * 2,
+        grid=(owners // near,),
+        in_specs=[
+            pl.BlockSpec((near, height, LANES), lambda i: (i, 0, 0)),
+            pl.BlockSpec((rows, span), lambda i: (0, i)),
+            pl.BlockSpec((3, taps, span), lambda i: (0, 0, i)),
+            pl.BlockSpec((1, span), lambda i: (0, i)),
+        ],
+        out_specs=(out, out),
+        cost_estimate=pl.CostEstimate(
+            flops=8 * rows * channels, bytes_accessed=12 * rows * channels, transcendentals=0
+        ),
+    )(sent, query_in, short_weight, skip_gain.reshape(1, channels))
+
+
 def finish_kernel(
-    conv_ref, sent_ref, query_ref, edge_ref, taps_ref, gain_ref, out_ref, ready, sems
+    conv_ref, short_ref, direct_ref, sent_ref, query_ref, edge_ref, taps_ref, gain_ref, out_ref,
+    ready, sems,
 ):
     rows, channels = ready.shape
     tail = sent_ref.shape[1] - SUBLANES
@@ -157,35 +192,34 @@
             own = sent_ref[owner, tail:].astype(jnp.float32)
             first = first_products(own, behind, tap_tiles(taps_ref, lanes))
             first = first.astype(jnp.bfloat16).astype(jnp.float32)
-            product = sent_ref[owner, :rows].astype(jnp.float32)
-            top = jnp.where(row < 2, first, product[:SUBLANES])
-            product = jnp.concatenate([top, product[SUBLANES:]], axis=0)
-
-            query = query_ref[:, lanes].astype(jnp.float32)
+            product = sent_ref[owner, :SUBLANES].astype(jnp.float32)
+            product = jnp.where(row < 2, first, product)
+
             weights = taps_ref[0, :, lanes]
-            top = query[:SUBLANES]
+            top = query_ref[:SUBLANES, lanes].astype(jnp.float32)
             one = jnp.where(row < 1, pltpu.roll(behind, 5, 0), pltpu.roll(top, 1, 0))
             two = jnp.where(row < 2, pltpu.roll(behind, 6, 0), pltpu.roll(top, 2, 0))
             top = weights[0:1] * top + weights[1:2] * one + weights[2:3] * two
-            inside = featurize_inside(query, weights)
-            q_short = jnp.concatenate([top, inside[SUBLANES:]], axis=0)
-
-            mixed = conv_ref[owner].astype(jnp.float32) + gain_ref[:, lanes] * product
-            ready[:, lanes] = (q_short * mixed).astype(ready.dtype)
+
+            convolved = conv_ref[owner].astype(jnp.float32)
+            top = top * convolved[:SUBLANES] + top * (gain_ref[:, lanes] * product)
+            result = short_ref[owner] * convolved + direct_ref[owner]
+            result = jnp.concatenate([top, result[SUBLANES:]], axis=0)
+            ready[:, lanes] = result.astype(ready.dtype)
         departure(chunk).start()
 
     for chunk in range(chunks):
         departure(chunk).wait()
 
 
-def finish(convolved, sent, query_in, edges, short_weight, skip_gain):
+def finish(convolved, prepared, sent, query_in, edges, short_weight, skip_gain):
     rows, channels = query_in.shape
     chunks = max(1, channels // 512)
     here = pl.BlockSpec(memory_space=pltpu.VMEM)
     return pl.pallas_call(
         finish_kernel,
         out_shape=jax.ShapeDtypeStruct((rows, channels), jnp.bfloat16),
-        in_specs=[here] * 6,
+        in_specs=[here] * 8,
         out_specs=pl.BlockSpec(memory_space=pltpu.HBM),
         scratch_shapes=[
             pltpu.VMEM((rows, channels), jnp.bfloat16),
@@ -193,9 +227,11 @@
         ],
         compiler_params=pltpu.CompilerParams(vmem_limit_bytes=8 * MIB),
         cost_estimate=pl.CostEstimate(
-            flops=9 * rows * channels, bytes_accessed=8 * rows * channels, transcendentals=0
-        ),
-    )(convolved, sent, query_in, edges, short_weight, skip_gain.reshape(1, channels))
+            flops=3 * rows * channels, bytes_accessed=12 * rows * channels, transcendentals=0
+        ),
+    )(
+        convolved, *prepared, sent, query_in, edges, short_weight, skip_gain.reshape(1, channels)
+    )
 
 
 def tap_tiles(taps_ref, lanes):
@@ -616,13 +652,16 @@
         )
         received = exchange(sent, ("groups", "seq"))
         edges = from_behind(edges, "seq")
-        received, edges = lax.optimization_barrier((received, edges))
+        prepared = prepare(sent, query_in, short_weight, skip_gain)
+        received, edges, prepared = lax.optimization_barrier((received, edges, prepared))
         owner = group * places + place
         convolved = convolve_whole(
             received, short_weight, owner, rows, forward_table, inverse_table
         )
         convolved = exchange(convolved, ("groups", "seq"))
-        return finish(convolved, sent, query_in, edges, short_weight, skip_gain)
+        return finish(
+            convolved, prepared, sent, query_in, edges, short_weight, skip_gain
+        )
     else:
         width = channels // places
         edges = jnp.stack([query_in[-rim:], key_in[-rim:], value_in[-rim:]])

time: 88.3 us -> 87.5 us (level)
  waiting for transfers between devices: 37.9 us -> 33 us
  Pallas kernels: 11.2 us -> 15 us
    pallas_call x0 -> x1, Pallas kernels: none -> 4.68 us  [prepare(): pl.pallas_call(prepare_kernel, out_shape=(jax.ShapeDtypeStruct((owners, r...]
    all_to_all x1, waiting for transfers between devices: 37 us -> 33 us  [exchange(): return lax.all_to_all(value, axes, split_axis=0, concat_axis=0, tiled=True)]
    pallas_call x1, Pallas kernels: 2.18 us -> 1.26 us  [finish(): pl.pallas_call(finish_kernel, out_shape=jax.ShapeDtypeStruct((rows, chann...]
  transfers between devices with their start and end apart: 2 -> 2, of which waited for: 2 -> 1; matrix products, arithmetic and copies ran while one was open for 0% -> 0% of each run, Pallas kernels for 0% -> 5%
where the time goes in v6:
time: 87.5 us; the launch traced here: 87.1 us
  waiting for transfers between devices  33 us (38%)
  blocking collectives  29.3 us (33%)
  Pallas kernels  15 us (17%)
  starting transfers between devices  9.59 us (11%)
    all_to_all x1, waiting for transfers between devices, exchange(): return lax.all_to_all(value, axes, split_axis=0, concat_axis=0, tiled=True)  33 us
    all_to_all x1, blocking collectives, exchange(): return lax.all_to_all(value, axes, split_axis=0, concat_axis=0, tiled=True)  29.3 us
    all_to_all x1, starting transfers between devices, exchange(): return lax.all_to_all(value, axes, split_axis=0, concat_axis=0, tiled=True)  7.3 us
    pallas_call x1, Pallas kernels, convolve_whole(): pl.pallas_call(whole_kernel, out_shape=jax.ShapeDtypeStruct((senders, row...  4.91 us
    pallas_call x1, Pallas kernels, prepare(): pl.pallas_call(prepare_kernel, out_shape=(jax.ShapeDtypeStruct((owners, r...  4.68 us
    pallas_call x1, Pallas kernels, pack(): pl.pallas_call(pack_kernel, out_shape=(jax.ShapeDtypeStruct((owners, heig...  4.14 us
    ppermute x1, starting transfers between devices, from_behind(): lax.ppermute(value, axis, [(source, source + 1) for source in range(count...  2.29 us
  transfers between devices with their start and end apart: 2, of which 1 were waited for; matrix products, arithmetic and copies ran while one was open for 0% of the time, Pallas kernels for 5%

profile of v6, /device:TPU:0, one launch (start us, length us, event | category | flops | bytes accessed | tf_op | source)
XLA Modules:
  0.0 87.1 jit_solution(1841074992191307775)
XLA Ops:
  0.0 4.1 %shard_map.82 = (bf16[32,200,128]{2,1,0:T(8,128)(2,1)}, bf16[8,4096]{1,0:T(8,128)(2,1)}) custom-call(s32[1]{0:T(128)} %bitcast.1.group_ref, bf16[128,4096]{1,0:T(8,128)(2,1)} %query_ref.5, bf16[128,4096]{1,0:T(8,128)(2,1)} %key_ref.1, bf16[128,4096]{1,0:T(8,128)(2,1)} %value_ref.1, bf16[128,4096]{1,0:T(8,128)(2,1)} %filter_ref.1, f32[3,3,4096]{2,1,0:T(4,128)} %taps_ref.7), custom_call_target="tpu_custom_call" | custom-call | flops 6291456 | bytes 4194304 | tf_op jit(solution)/shard_map/pallas_call | solution.py:340
  4.2 0.0 copy-start.8
  4.2 7.3 %all-to-all-start = ((bf16[32,200,128]{2,1,0:T(8,128)(2,1)}), bf16[32,200,128]{2,1,0:T(8,128)(2,1)S(1)}, u32[]{:S(2)}, u32[]{:S(2)}) async-start(bf16[32,200,128]{2,1,0:T(8,128)(2,1)} %get-tuple-element.13.sent_ref), calls=%async_computation | async-start | bytes 3276800 | tf_op jit(solution)/shard_map/all_to_all | solution.py:623
  11.5 0.0 copy-start.4
  11.5 0.0 copy-start.6
  11.5 0.0 copy-start.7
  11.5 0.0 copy-done.8
  11.5 2.3 %collective-permute-start = (bf16[8,4096]{1,0:T(8,128)(2,1)S(1)}, bf16[8,4096]{1,0:T(8,128)(2,1)S(1)}, u32[]{:S(2)}, u32[]{:S(2)}) collective-permute-start(bf16[8,4096]{1,0:T(8,128)(2,1)S(1)} %copy-done.8), channel_id=1, source_target_pairs={{0,1},{1,2},{2,3},{3,4},{4,5},{5,6},{6,7},{7,8},{8,9},{9,10},{10,1... | collective-permute-start | bytes 196616 | tf_op jit(solution)/shard_map/ppermute | solution.py:21
  13.8 4.7 %shard_map.83 = (f32[32,128,128]{2,1,0:T(8,128)}, f32[32,128,128]{2,1,0:T(8,128)}) custom-call(bf16[32,200,128]{2,1,0:T(8,128)(2,1)} %get-tuple-element.13.sent_ref, bf16[128,4096]{1,0:T(8,128)(2,1)} %query_ref.5, f32[3,3,4096]{2,1,0:T(4,128)} %taps_ref.7, f32[1,4096]{1,0:T(1,128)} %bitcast.3), custom_call_target="tpu_custom_call" | custom-call | flops 4194304 | bytes 6291456 | tf_op jit(solution)/shard_map/pallas_call | solution.py:154
  18.5 0.0 collective-permute-done.edge_ref
  18.5 33.0 %all-to-all-done.arrived = bf16[32,200,128]{2,1,0:T(8,128)(2,1)S(1)} async-done(((bf16[32,200,128]{2,1,0:T(8,128)(2,1)}), bf16[32,200,128]{2,1,0:T(8,128)(2,1)S(1)}, u32[]{:S(2)}, u32[]{:S(2)}) %all-to-all-start) | async-done | bytes 1638432 | tf_op jit(solution)/shard_map/all_to_all | solution.py:623
  51.5 0.0 copy-done.4
  51.5 0.0 copy-done.6
  51.6 0.0 copy-done.7
  51.6 0.0 copy-start.1
  51.6 0.0 copy-start.2
  51.6 0.0 copy-start.3
  51.6 4.9 %shard_map.84 = bf16[32,128,128]{2,1,0:T(8,128)(2,1)S(1)} custom-call(s32[1]{0:T(128)} %bitcast.owner_ref, bf16[2,512,256]{2,1,0:T(8,128)(2,1)S(1)} %copy-done.7, bf16[2,512,256]{2,1,0:T(8,128)(2,1)S(1)} %copy-done.6, f32[3,3,4096]{2,1,0:T(4,128)S(1)} %copy-done.4, bf16[32,200,128]{2,1,0:T(8,128)(2,1)S(1)} %all-to-all-done.arrived), custom_call_target="tpu_custom_call" | custom-call | flops 2684354560 | bytes 2686976 | tf_op jit(solution)/shard_map/pallas_call | solution.py:591
  56.5 0.0 copy-start
  56.5 0.0 copy-start.5
  56.5 29.3 %all_to_all.10.conv_ref = bf16[32,128,128]{2,1,0:T(8,128)(2,1)S(1)} all-to-all(bf16[32,128,128]{2,1,0:T(8,128)(2,1)S(1)} %shard_map.84), channel_id=1, replica_groups=mesh['groups'=2,'seq'=16] {'groups','seq'}, dimensions={0} | all-to-all | bytes 2097152 | tf_op jit(solution)/shard_map/all_to_all | solution.py:623
  85.8 0.0 copy-done.1
  85.8 0.0 copy-done.2
  85.8 0.0 copy-done.3
  85.8 0.0 copy-done
  85.8 0.0 copy-done.5
  85.8 1.3 %shard_map.85 = bf16[128,4096]{1,0:T(8,128)(2,1)} custom-call(bf16[32,128,128]{2,1,0:T(8,128)(2,1)S(1)} %all_to_all.10.conv_ref, f32[32,128,128]{2,1,0:T(8,128)S(1)} %copy-done.2, f32[32,128,128]{2,1,0:T(8,128)S(1)} %copy-done.3, bf16[32,200,128]{2,1,0:T(8,128)(2,1)S(1)} %copy-done, bf16[128,4096]{1,0:T(8,128)(2,1)S(1)} %copy-done.1, ...), custom_call_target="tpu_custom_call" | custom-call | flops 1572864 | bytes 6291456 | tf_op jit(solution)/shard_map/pallas_call | solution.py:219
Async XLA Ops:
  4.2 7.4 %copy-start.8 = (bf16[8,4096]{1,0:T(8,128)(2,1)S(1)}, bf16[8,4096]{1,0:T(8,128)(2,1)}, u32[]{:S(2)}) copy-start(bf16[8,4096]{1,0:T(8,128)(2,1)} %get-tuple-element.14) | copy-start | bytes 196612
  4.2 47.4 %all-to-all-start = ((bf16[32,200,128]{2,1,0:T(8,128)(2,1)}), bf16[32,200,128]{2,1,0:T(8,128)(2,1)S(1)}, u32[]{:S(2)}, u32[]{:S(2)}) async-start(bf16[32,200,128]{2,1,0:T(8,128)(2,1)} %get-tuple-element.13.sent_ref), calls=%async_computation | async-start | bytes 3276800 | tf_op jit(solution)/shard_map/all_to_all | solution.py:623
  11.5 40.1 %copy-start.4 = (f32[3,3,4096]{2,1,0:T(4,128)S(1)}, f32[3,3,4096]{2,1,0:T(4,128)}, u32[]{:S(2)}) copy-start(f32[3,3,4096]{2,1,0:T(4,128)} %taps_ref.7) | copy-start | bytes 442372
  11.5 40.1 %copy-start.6 = (bf16[2,512,256]{2,1,0:T(8,128)(2,1)S(1)}, bf16[2,512,256]{2,1,0:T(8,128)(2,1)}, u32[]{:S(2)}) copy-start(bf16[2,512,256]{2,1,0:T(8,128)(2,1)} %constant.16.clone.inverse_ref) | copy-start | bytes 1572868
  11.5 40.1 %copy-start.7 = (bf16[2,512,256]{2,1,0:T(8,128)(2,1)S(1)}, bf16[2,512,256]{2,1,0:T(8,128)(2,1)}, u32[]{:S(2)}) copy-start(bf16[2,512,256]{2,1,0:T(8,128)(2,1)} %constant.15.clone.forward_ref) | copy-start | bytes 1572868
  11.5 7.0 %collective-permute-start = (bf16[8,4096]{1,0:T(8,128)(2,1)S(1)}, bf16[8,4096]{1,0:T(8,128)(2,1)S(1)}, u32[]{:S(2)}, u32[]{:S(2)}) collective-permute-start(bf16[8,4096]{1,0:T(8,128)(2,1)S(1)} %copy-done.8), channel_id=1, source_target_pairs={{0,1},{1,2},{2,3},{3,4},{4,5},{5,6},{6,7},{7,8},{8,9},{9,10},{10,1... | collective-permute-start | bytes 196616 | tf_op jit(solution)/shard_map/ppermute | solution.py:21
  51.6 34.3 %copy-start.1 = (bf16[128,4096]{1,0:T(8,128)(2,1)S(1)}, bf16[128,4096]{1,0:T(8,128)(2,1)}, u32[]{:S(2)}) copy-start(bf16[128,4096]{1,0:T(8,128)(2,1)} %query_ref.5) | copy-start | bytes 3145732
  51.6 34.2 %copy-start.2 = (f32[32,128,128]{2,1,0:T(8,128)S(1)}, f32[32,128,128]{2,1,0:T(8,128)}, u32[]{:S(2)}) copy-start(f32[32,128,128]{2,1,0:T(8,128)} %get-tuple-element.18.short_ref) | copy-start | bytes 6291460
  51.6 34.2 %copy-start.3 = (f32[32,128,128]{2,1,0:T(8,128)S(1)}, f32[32,128,128]{2,1,0:T(8,128)}, u32[]{:S(2)}) copy-start(f32[32,128,128]{2,1,0:T(8,128)} %get-tuple-element.19.direct_ref) | copy-start | bytes 6291460
  56.5 29.3 %copy-start = (bf16[32,200,128]{2,1,0:T(8,128)(2,1)S(1)}, bf16[32,200,128]{2,1,0:T(8,128)(2,1)}, u32[]{:S(2)}) copy-start(bf16[32,200,128]{2,1,0:T(8,128)(2,1)} %get-tuple-element.13.sent_ref) | copy-start | bytes 4915204
  56.5 29.3 %copy-start.5 = (f32[4096]{0:T(1024)S(1)}, f32[4096]{0:T(1024)}, u32[]{:S(2)}) copy-start(f32[4096]{0:T(1024)} %param.13) | copy-start | bytes 49156

commit v7 on v6

--- a/solution.py
+++ b/solution.py
@@ -288,7 +288,7 @@
         copy.start()
     for chunk in range(chunks):
         for copy in arrivals(chunk):
-            copy.start()
+            copy.start(priority=1)
     for copy in whole:
         copy.wait()
     row = lax.broadcasted_iota(jnp.int32, (SUBLANES, LANES), 0)

time: 87.5 us -> 87 us (level)
  no operation moved by 1% of the time
where the time goes in v7:
time: 87 us; the launch traced here: 86.6 us
  waiting for transfers between devices  33 us (38%)
  blocking collectives  29.3 us (34%)
  Pallas kernels  14.5 us (17%)
  starting transfers between devices  9.59 us (11%)
    all_to_all x1, waiting for transfers between devices, exchange(): return lax.all_to_all(value, axes, split_axis=0, concat_axis=0, tiled=True)  33 us
    all_to_all x1, blocking collectives, exchange(): return lax.all_to_all(value, axes, split_axis=0, concat_axis=0, tiled=True)  29.3 us
    all_to_all x1, starting transfers between devices, exchange(): return lax.all_to_all(value, axes, split_axis=0, concat_axis=0, tiled=True)  7.3 us
    pallas_call x1, Pallas kernels, convolve_whole(): pl.pallas_call(whole_kernel, out_shape=jax.ShapeDtypeStruct((senders, row...  4.91 us
    pallas_call x1, Pallas kernels, prepare(): pl.pallas_call(prepare_kernel, out_shape=(jax.ShapeDtypeStruct((owners, r...  4.68 us
    pallas_call x1, Pallas kernels, pack(): pl.pallas_call(pack_kernel, out_shape=(jax.ShapeDtypeStruct((owners, heig...  3.67 us
    ppermute x1, starting transfers between devices, from_behind(): lax.ppermute(value, axis, [(source, source + 1) for source in range(count...  2.29 us
  transfers between devices with their start and end apart: 2, of which 1 were waited for; matrix products, arithmetic and copies ran while one was open for 0% of the time, Pallas kernels for 5%

profile of v7, /device:TPU:0, one launch (start us, length us, event | category | flops | bytes accessed | tf_op | source)
XLA Modules:
  0.0 86.6 jit_solution(5273234810039657570)
XLA Ops:
  0.0 3.7 %shard_map.82 = (bf16[32,200,128]{2,1,0:T(8,128)(2,1)}, bf16[8,4096]{1,0:T(8,128)(2,1)}) custom-call(s32[1]{0:T(128)} %bitcast.1.group_ref, bf16[128,4096]{1,0:T(8,128)(2,1)} %query_ref.5, bf16[128,4096]{1,0:T(8,128)(2,1)} %key_ref.1, bf16[128,4096]{1,0:T(8,128)(2,1)} %value_ref.1, bf16[128,4096]{1,0:T(8,128)(2,1)} %filter_ref.1, f32[3,3,4096]{2,1,0:T(4,128)} %taps_ref.7), custom_call_target="tpu_custom_call" | custom-call | flops 6291456 | bytes 4194304 | tf_op jit(solution)/shard_map/pallas_call | solution.py:340
  3.7 0.0 copy-start.8
  3.7 7.3 %all-to-all-start = ((bf16[32,200,128]{2,1,0:T(8,128)(2,1)}), bf16[32,200,128]{2,1,0:T(8,128)(2,1)S(1)}, u32[]{:S(2)}, u32[]{:S(2)}) async-start(bf16[32,200,128]{2,1,0:T(8,128)(2,1)} %get-tuple-element.13.sent_ref), calls=%async_computation | async-start | bytes 3276800 | tf_op jit(solution)/shard_map/all_to_all | solution.py:623
  11.0 0.0 copy-start.4
  11.0 0.0 copy-start.6
  11.0 0.0 copy-start.7
  11.0 0.0 copy-done.8
  11.0 2.3 %collective-permute-start = (bf16[8,4096]{1,0:T(8,128)(2,1)S(1)}, bf16[8,4096]{1,0:T(8,128)(2,1)S(1)}, u32[]{:S(2)}, u32[]{:S(2)}) collective-permute-start(bf16[8,4096]{1,0:T(8,128)(2,1)S(1)} %copy-done.8), channel_id=1, source_target_pairs={{0,1},{1,2},{2,3},{3,4},{4,5},{5,6},{6,7},{7,8},{8,9},{9,10},{10,1... | collective-permute-start | bytes 196616 | tf_op jit(solution)/shard_map/ppermute | solution.py:21
  13.4 4.7 %shard_map.83 = (f32[32,128,128]{2,1,0:T(8,128)}, f32[32,128,128]{2,1,0:T(8,128)}) custom-call(bf16[32,200,128]{2,1,0:T(8,128)(2,1)} %get-tuple-element.13.sent_ref, bf16[128,4096]{1,0:T(8,128)(2,1)} %query_ref.5, f32[3,3,4096]{2,1,0:T(4,128)} %taps_ref.7, f32[1,4096]{1,0:T(1,128)} %bitcast.3), custom_call_target="tpu_custom_call" | custom-call | flops 4194304 | bytes 6291456 | tf_op jit(solution)/shard_map/pallas_call | solution.py:154
  18.0 0.0 collective-permute-done.edge_ref
  18.0 33.0 %all-to-all-done.arrived = bf16[32,200,128]{2,1,0:T(8,128)(2,1)S(1)} async-done(((bf16[32,200,128]{2,1,0:T(8,128)(2,1)}), bf16[32,200,128]{2,1,0:T(8,128)(2,1)S(1)}, u32[]{:S(2)}, u32[]{:S(2)}) %all-to-all-start) | async-done | bytes 1638432 | tf_op jit(solution)/shard_map/all_to_all | solution.py:623
  51.1 0.0 copy-done.4
  51.1 0.0 copy-done.6
  51.1 0.0 copy-done.7
  51.1 0.0 copy-start.1
  51.1 0.0 copy-start.2
  51.1 0.0 copy-start.3
  51.1 4.9 %shard_map.84 = bf16[32,128,128]{2,1,0:T(8,128)(2,1)S(1)} custom-call(s32[1]{0:T(128)} %bitcast.owner_ref, bf16[2,512,256]{2,1,0:T(8,128)(2,1)S(1)} %copy-done.7, bf16[2,512,256]{2,1,0:T(8,128)(2,1)S(1)} %copy-done.6, f32[3,3,4096]{2,1,0:T(4,128)S(1)} %copy-done.4, bf16[32,200,128]{2,1,0:T(8,128)(2,1)S(1)} %all-to-all-done.arrived), custom_call_target="tpu_custom_call" | custom-call | flops 2684354560 | bytes 2686976 | tf_op jit(solution)/shard_map/pallas_call | solution.py:591
  56.0 0.0 copy-start
  56.0 0.0 copy-start.5
  56.1 29.3 %all_to_all.10.conv_ref = bf16[32,128,128]{2,1,0:T(8,128)(2,1)S(1)} all-to-all(bf16[32,128,128]{2,1,0:T(8,128)(2,1)S(1)} %shard_map.84), channel_id=1, replica_groups=mesh['groups'=2,'seq'=16] {'groups','seq'}, dimensions={0} | all-to-all | bytes 2097152 | tf_op jit(solution)/shard_map/all_to_all | solution.py:623
  85.3 0.0 copy-done.1
  85.3 0.0 copy-done.2
  85.3 0.0 copy-done.3
  85.3 0.0 copy-done
  85.3 0.0 copy-done.5
  85.4 1.3 %shard_map.85 = bf16[128,4096]{1,0:T(8,128)(2,1)} custom-call(bf16[32,128,128]{2,1,0:T(8,128)(2,1)S(1)} %all_to_all.10.conv_ref, f32[32,128,128]{2,1,0:T(8,128)S(1)} %copy-done.2, f32[32,128,128]{2,1,0:T(8,128)S(1)} %copy-done.3, bf16[32,200,128]{2,1,0:T(8,128)(2,1)S(1)} %copy-done, bf16[128,4096]{1,0:T(8,128)(2,1)S(1)} %copy-done.1, ...), custom_call_target="tpu_custom_call" | custom-call | flops 1572864 | bytes 6291456 | tf_op jit(solution)/shard_map/pallas_call | solution.py:219
Async XLA Ops:
  3.7 7.4 %copy-start.8 = (bf16[8,4096]{1,0:T(8,128)(2,1)S(1)}, bf16[8,4096]{1,0:T(8,128)(2,1)}, u32[]{:S(2)}) copy-start(bf16[8,4096]{1,0:T(8,128)(2,1)} %get-tuple-element.14) | copy-start | bytes 196612
  3.7 47.4 %all-to-all-start = ((bf16[32,200,128]{2,1,0:T(8,128)(2,1)}), bf16[32,200,128]{2,1,0:T(8,128)(2,1)S(1)}, u32[]{:S(2)}, u32[]{:S(2)}) async-start(bf16[32,200,128]{2,1,0:T(8,128)(2,1)} %get-tuple-element.13.sent_ref), calls=%async_computation | async-start | bytes 3276800 | tf_op jit(solution)/shard_map/all_to_all | solution.py:623
  11.0 40.1 %copy-start.4 = (f32[3,3,4096]{2,1,0:T(4,128)S(1)}, f32[3,3,4096]{2,1,0:T(4,128)}, u32[]{:S(2)}) copy-start(f32[3,3,4096]{2,1,0:T(4,128)} %taps_ref.7) | copy-start | bytes 442372
  11.0 40.1 %copy-start.6 = (bf16[2,512,256]{2,1,0:T(8,128)(2,1)S(1)}, bf16[2,512,256]{2,1,0:T(8,128)(2,1)}, u32[]{:S(2)}) copy-start(bf16[2,512,256]{2,1,0:T(8,128)(2,1)} %constant.16.clone.inverse_ref) | copy-start | bytes 1572868
  11.0 40.1 %copy-start.7 = (bf16[2,512,256]{2,1,0:T(8,128)(2,1)S(1)}, bf16[2,512,256]{2,1,0:T(8,128)(2,1)}, u32[]{:S(2)}) copy-start(bf16[2,512,256]{2,1,0:T(8,128)(2,1)} %constant.15.clone.forward_ref) | copy-start | bytes 1572868
  11.0 7.0 %collective-permute-start = (bf16[8,4096]{1,0:T(8,128)(2,1)S(1)}, bf16[8,4096]{1,0:T(8,128)(2,1)S(1)}, u32[]{:S(2)}, u32[]{:S(2)}) collective-permute-start(bf16[8,4096]{1,0:T(8,128)(2,1)S(1)} %copy-done.8), channel_id=1, source_target_pairs={{0,1},{1,2},{2,3},{3,4},{4,5},{5,6},{6,7},{7,8},{8,9},{9,10},{10,1... | collective-permute-start | bytes 196616 | tf_op jit(solution)/shard_map/ppermute | solution.py:21
  51.1 34.2 %copy-start.1 = (bf16[128,4096]{1,0:T(8,128)(2,1)S(1)}, bf16[128,4096]{1,0:T(8,128)(2,1)}, u32[]{:S(2)}) copy-start(bf16[128,4096]{1,0:T(8,128)(2,1)} %query_ref.5) | copy-start | bytes 3145732
  51.1 34.2 %copy-start.2 = (f32[32,128,128]{2,1,0:T(8,128)S(1)}, f32[32,128,128]{2,1,0:T(8,128)}, u32[]{:S(2)}) copy-start(f32[32,128,128]{2,1,0:T(8,128)} %get-tuple-element.18.short_ref) | copy-start | bytes 6291460
  51.1 34.2 %copy-start.3 = (f32[32,128,128]{2,1,0:T(8,128)S(1)}, f32[32,128,128]{2,1,0:T(8,128)}, u32[]{:S(2)}) copy-start(f32[32,128,128]{2,1,0:T(8,128)} %get-tuple-element.19.direct_ref) | copy-start | bytes 6291460
  56.0 29.3 %copy-start = (bf16[32,200,128]{2,1,0:T(8,128)(2,1)S(1)}, bf16[32,200,128]{2,1,0:T(8,128)(2,1)}, u32[]{:S(2)}) copy-start(bf16[32,200,128]{2,1,0:T(8,128)(2,1)} %get-tuple-element.13.sent_ref) | copy-start | bytes 4915204
  56.0 29.3 %copy-start.5 = (f32[4096]{0:T(1024)S(1)}, f32[4096]{0:T(1024)}, u32[]{:S(2)}) copy-start(f32[4096]{0:T(1024)} %param.13) | copy-start | bytes 49156

commit v8 on v7

--- a/solution.py
+++ b/solution.py
@@ -485,7 +485,6 @@
     owner_ref, forward_ref, inverse_ref, taps_ref, arrived, ready,
     product, filters, data, known, mixed, partly,
 ):
-    del owner_ref
     senders, rows, _ = ready.shape
     places = senders // 2
     share = rows // 2
@@ -494,7 +493,8 @@
     near = block // rows
     tiles = half // SUBLANES // count
     row = lax.broadcasted_iota(jnp.int32, (SUBLANES, LANES), 0)
-    weights = tap_tiles(taps_ref, slice(None))
+    own = pl.multiple_of(owner_ref[0] * LANES, LANES)
+    weights = tap_tiles(taps_ref, pl.ds(own, LANES))
 
     def forward(side, values):
         return transform(forward_ref[side], values)
@@ -587,29 +587,20 @@
     block = forward_table.shape[2]
     length = senders // 2 * rows
     count = length // block
-    taps = short_weight.shape[1]
     return pl.pallas_call(
         whole_kernel,
         out_shape=jax.ShapeDtypeStruct((senders, rows, LANES), jnp.bfloat16),
-        grid_spec=pltpu.PrefetchScalarGridSpec(
-            num_scalar_prefetch=1,
-            grid=(1,),
-            in_specs=[
-                pl.BlockSpec(memory_space=pltpu.VMEM),
-                pl.BlockSpec(memory_space=pltpu.VMEM),
-                pl.BlockSpec((3, taps, LANES), lambda i, owner: (0, 0, owner[0])),
-                pl.BlockSpec(memory_space=pltpu.VMEM),
-            ],
-            out_specs=pl.BlockSpec(memory_space=pltpu.VMEM),
-            scratch_shapes=[
-                pltpu.VMEM((count, block, 2 * LANES), jnp.bfloat16),
-                pltpu.VMEM((count // 2, block, 2 * LANES), jnp.bfloat16),
-                pltpu.VMEM((2, count, block, 2 * LANES), jnp.float32),
-                pltpu.VMEM((2, count, block, LANES), jnp.float32),
-                pltpu.VMEM((2, count, block, 2 * LANES), jnp.float32),
-                pltpu.VMEM((count, block, 2 * LANES), jnp.float32),
-            ],
-        ),
+        in_specs=[pl.BlockSpec(memory_space=pltpu.SMEM)]
+        + [pl.BlockSpec(memory_space=pltpu.VMEM)] * 4,
+        out_specs=pl.BlockSpec(memory_space=pltpu.VMEM),
+        scratch_shapes=[
+            pltpu.VMEM((count, block, 2 * LANES), jnp.bfloat16),
+            pltpu.VMEM((count // 2, block, 2 * LANES), jnp.bfloat16),
+            pltpu.VMEM((2, count, block, 2 * LANES), jnp.float32),
+            pltpu.VMEM((2, count, block, LANES), jnp.float32),
+            pltpu.VMEM((2, count, block, 2 * LANES), jnp.float32),
+            pltpu.VMEM((count, block, 2 * LANES), jnp.float32),
+        ],
         compiler_params=pltpu.CompilerParams(vmem_limit_bytes=32 * MIB),
         cost_estimate=pl.CostEstimate(
             flops=40 * length * block * LANES,

time: 87 us -> 87 us (level)
  no operation moved by 1% of the time
where the time goes in v8:
time: 87 us; the launch traced here: 86.6 us
  waiting for transfers between devices  33 us (38%)
  blocking collectives  29.3 us (34%)
  Pallas kernels  14.5 us (17%)
  starting transfers between devices  9.59 us (11%)
    all_to_all x1, waiting for transfers between devices, exchange(): return lax.all_to_all(value, axes, split_axis=0, concat_axis=0, tiled=True)  33 us
    all_to_all x1, blocking collectives, exchange(): return lax.all_to_all(value, axes, split_axis=0, concat_axis=0, tiled=True)  29.3 us
    all_to_all x1, starting transfers between devices, exchange(): return lax.all_to_all(value, axes, split_axis=0, concat_axis=0, tiled=True)  7.3 us
    pallas_call x1, Pallas kernels, convolve_whole(): pl.pallas_call(whole_kernel, out_shape=jax.ShapeDtypeStruct((senders, row...  4.95 us
    pallas_call x1, Pallas kernels, prepare(): pl.pallas_call(prepare_kernel, out_shape=(jax.ShapeDtypeStruct((owners, r...  4.68 us
    pallas_call x1, Pallas kernels, pack(): pl.pallas_call(pack_kernel, out_shape=(jax.ShapeDtypeStruct((owners, heig...  3.67 us
    ppermute x1, starting transfers between devices, from_behind(): lax.ppermute(value, axis, [(source, source + 1) for source in range(count...  2.29 us
  transfers between devices with their start and end apart: 2, of which 1 were waited for; matrix products, arithmetic and copies ran while one was open for 0% of the time, Pallas kernels for 5%

profile of v8, /device:TPU:0, one launch (start us, length us, event | category | flops | bytes accessed | tf_op | source)
XLA Modules:
  0.0 86.6 jit_solution(4782074222094115242)
XLA Ops:
  0.0 3.7 %shard_map.82 = (bf16[32,200,128]{2,1,0:T(8,128)(2,1)}, bf16[8,4096]{1,0:T(8,128)(2,1)}) custom-call(s32[1]{0:T(128)} %bitcast.1.group_ref, bf16[128,4096]{1,0:T(8,128)(2,1)} %query_ref.5, bf16[128,4096]{1,0:T(8,128)(2,1)} %key_ref.1, bf16[128,4096]{1,0:T(8,128)(2,1)} %value_ref.1, bf16[128,4096]{1,0:T(8,128)(2,1)} %filter_ref.1, f32[3,3,4096]{2,1,0:T(4,128)} %taps_ref.7), custom_call_target="tpu_custom_call" | custom-call | flops 6291456 | bytes 4194304 | tf_op jit(solution)/shard_map/pallas_call | solution.py:340
  3.7 0.0 copy-start.8
  3.7 7.3 %all-to-all-start = ((bf16[32,200,128]{2,1,0:T(8,128)(2,1)}), bf16[32,200,128]{2,1,0:T(8,128)(2,1)S(1)}, u32[]{:S(2)}, u32[]{:S(2)}) async-start(bf16[32,200,128]{2,1,0:T(8,128)(2,1)} %get-tuple-element.13.sent_ref), calls=%async_computation | async-start | bytes 3276800 | tf_op jit(solution)/shard_map/all_to_all | solution.py:614
  11.0 0.0 copy-start.4
  11.0 0.0 copy-start.6
  11.0 0.0 copy-start.7
  11.0 0.0 copy-done.8
  11.0 2.3 %collective-permute-start = (bf16[8,4096]{1,0:T(8,128)(2,1)S(1)}, bf16[8,4096]{1,0:T(8,128)(2,1)S(1)}, u32[]{:S(2)}, u32[]{:S(2)}) collective-permute-start(bf16[8,4096]{1,0:T(8,128)(2,1)S(1)} %copy-done.8), channel_id=1, source_target_pairs={{0,1},{1,2},{2,3},{3,4},{4,5},{5,6},{6,7},{7,8},{8,9},{9,10},{10,1... | collective-permute-start | bytes 196616 | tf_op jit(solution)/shard_map/ppermute | solution.py:21
  13.4 4.7 %shard_map.83 = (f32[32,128,128]{2,1,0:T(8,128)}, f32[32,128,128]{2,1,0:T(8,128)}) custom-call(bf16[32,200,128]{2,1,0:T(8,128)(2,1)} %get-tuple-element.13.sent_ref, bf16[128,4096]{1,0:T(8,128)(2,1)} %query_ref.5, f32[3,3,4096]{2,1,0:T(4,128)} %taps_ref.7, f32[1,4096]{1,0:T(1,128)} %bitcast.3), custom_call_target="tpu_custom_call" | custom-call | flops 4194304 | bytes 6291456 | tf_op jit(solution)/shard_map/pallas_call | solution.py:154
  18.0 0.0 collective-permute-done.edge_ref
  18.0 33.0 %all-to-all-done.arrived = bf16[32,200,128]{2,1,0:T(8,128)(2,1)S(1)} async-done(((bf16[32,200,128]{2,1,0:T(8,128)(2,1)}), bf16[32,200,128]{2,1,0:T(8,128)(2,1)S(1)}, u32[]{:S(2)}, u32[]{:S(2)}) %all-to-all-start) | async-done | bytes 1638432 | tf_op jit(solution)/shard_map/all_to_all | solution.py:614
  51.1 0.0 copy-done.4
  51.1 0.0 copy-done.6
  51.1 0.0 copy-done.7
  51.1 0.0 copy-start.1
  51.1 0.0 copy-start.2
  51.1 0.0 copy-start.3
  51.1 4.9 %shard_map.84 = bf16[32,128,128]{2,1,0:T(8,128)(2,1)S(1)} custom-call(s32[1]{0:T(128)} %bitcast.owner_ref, bf16[2,512,256]{2,1,0:T(8,128)(2,1)S(1)} %copy-done.7, bf16[2,512,256]{2,1,0:T(8,128)(2,1)S(1)} %copy-done.6, f32[3,3,4096]{2,1,0:T(4,128)S(1)} %copy-done.4, bf16[32,200,128]{2,1,0:T(8,128)(2,1)S(1)} %all-to-all-done.arrived), custom_call_target="tpu_custom_call" | custom-call | flops 2684354560 | bytes 2686976 | tf_op jit(solution)/shard_map/pallas_call | solution.py:590
  56.1 0.0 copy-start
  56.1 0.0 copy-start.5
  56.1 29.3 %all_to_all.10.conv_ref = bf16[32,128,128]{2,1,0:T(8,128)(2,1)S(1)} all-to-all(bf16[32,128,128]{2,1,0:T(8,128)(2,1)S(1)} %shard_map.84), channel_id=1, replica_groups=mesh['groups'=2,'seq'=16] {'groups','seq'}, dimensions={0} | all-to-all | bytes 2097152 | tf_op jit(solution)/shard_map/all_to_all | solution.py:614
  85.4 0.0 copy-done.1
  85.4 0.0 copy-done.2
  85.4 0.0 copy-done.3
  85.4 0.0 copy-done
  85.4 0.0 copy-done.5
  85.4 1.3 %shard_map.85 = bf16[128,4096]{1,0:T(8,128)(2,1)} custom-call(bf16[32,128,128]{2,1,0:T(8,128)(2,1)S(1)} %all_to_all.10.conv_ref, f32[32,128,128]{2,1,0:T(8,128)S(1)} %copy-done.2, f32[32,128,128]{2,1,0:T(8,128)S(1)} %copy-done.3, bf16[32,200,128]{2,1,0:T(8,128)(2,1)S(1)} %copy-done, bf16[128,4096]{1,0:T(8,128)(2,1)S(1)} %copy-done.1, ...), custom_call_target="tpu_custom_call" | custom-call | flops 1572864 | bytes 6291456 | tf_op jit(solution)/shard_map/pallas_call | solution.py:219
Async XLA Ops:
  3.7 7.4 %copy-start.8 = (bf16[8,4096]{1,0:T(8,128)(2,1)S(1)}, bf16[8,4096]{1,0:T(8,128)(2,1)}, u32[]{:S(2)}) copy-start(bf16[8,4096]{1,0:T(8,128)(2,1)} %get-tuple-element.14) | copy-start | bytes 196612
  3.7 47.4 %all-to-all-start = ((bf16[32,200,128]{2,1,0:T(8,128)(2,1)}), bf16[32,200,128]{2,1,0:T(8,128)(2,1)S(1)}, u32[]{:S(2)}, u32[]{:S(2)}) async-start(bf16[32,200,128]{2,1,0:T(8,128)(2,1)} %get-tuple-element.13.sent_ref), calls=%async_computation | async-start | bytes 3276800 | tf_op jit(solution)/shard_map/all_to_all | solution.py:614
  11.0 40.1 %copy-start.4 = (f32[3,3,4096]{2,1,0:T(4,128)S(1)}, f32[3,3,4096]{2,1,0:T(4,128)}, u32[]{:S(2)}) copy-start(f32[3,3,4096]{2,1,0:T(4,128)} %taps_ref.7) | copy-start | bytes 442372
  11.0 40.1 %copy-start.6 = (bf16[2,512,256]{2,1,0:T(8,128)(2,1)S(1)}, bf16[2,512,256]{2,1,0:T(8,128)(2,1)}, u32[]{:S(2)}) copy-start(bf16[2,512,256]{2,1,0:T(8,128)(2,1)} %constant.16.clone.inverse_ref) | copy-start | bytes 1572868
  11.0 40.1 %copy-start.7 = (bf16[2,512,256]{2,1,0:T(8,128)(2,1)S(1)}, bf16[2,512,256]{2,1,0:T(8,128)(2,1)}, u32[]{:S(2)}) copy-start(bf16[2,512,256]{2,1,0:T(8,128)(2,1)} %constant.15.clone.forward_ref) | copy-start | bytes 1572868
  11.0 7.0 %collective-permute-start = (bf16[8,4096]{1,0:T(8,128)(2,1)S(1)}, bf16[8,4096]{1,0:T(8,128)(2,1)S(1)}, u32[]{:S(2)}, u32[]{:S(2)}) collective-permute-start(bf16[8,4096]{1,0:T(8,128)(2,1)S(1)} %copy-done.8), channel_id=1, source_target_pairs={{0,1},{1,2},{2,3},{3,4},{4,5},{5,6},{6,7},{7,8},{8,9},{9,10},{10,1... | collective-permute-start | bytes 196616 | tf_op jit(solution)/shard_map/ppermute | solution.py:21
  51.1 34.3 %copy-start.1 = (bf16[128,4096]{1,0:T(8,128)(2,1)S(1)}, bf16[128,4096]{1,0:T(8,128)(2,1)}, u32[]{:S(2)}) copy-start(bf16[128,4096]{1,0:T(8,128)(2,1)} %query_ref.5) | copy-start | bytes 3145732
  51.1 34.3 %copy-start.2 = (f32[32,128,128]{2,1,0:T(8,128)S(1)}, f32[32,128,128]{2,1,0:T(8,128)}, u32[]{:S(2)}) copy-start(f32[32,128,128]{2,1,0:T(8,128)} %get-tuple-element.18.short_ref) | copy-start | bytes 6291460
  51.1 34.3 %copy-start.3 = (f32[32,128,128]{2,1,0:T(8,128)S(1)}, f32[32,128,128]{2,1,0:T(8,128)}, u32[]{:S(2)}) copy-start(f32[32,128,128]{2,1,0:T(8,128)} %get-tuple-element.19.direct_ref) | copy-start | bytes 6291460
  56.1 29.3 %copy-start = (bf16[32,200,128]{2,1,0:T(8,128)(2,1)S(1)}, bf16[32,200,128]{2,1,0:T(8,128)(2,1)}, u32[]{:S(2)}) copy-start(bf16[32,200,128]{2,1,0:T(8,128)(2,1)} %get-tuple-element.13.sent_ref) | copy-start | bytes 4915204
  56.1 29.3 %copy-start.5 = (f32[4096]{0:T(1024)S(1)}, f32[4096]{0:T(1024)}, u32[]{:S(2)}) copy-start(f32[4096]{0:T(1024)} %param.13) | copy-start | bytes 49156

commit v9 on v7

--- a/solution.py
+++ b/solution.py
@@ -169,7 +169,7 @@
 
 
 def finish_kernel(
-    conv_ref, short_ref, direct_ref, sent_ref, query_ref, edge_ref, taps_ref, gain_ref, out_ref,
+    places, conv_ref, short_ref, direct_ref, sent_ref, query_ref, edge_ref, taps_ref, gain_ref, out_ref,
     ready, sems,
 ):
     rows, channels = ready.shape
@@ -201,7 +201,8 @@
             two = jnp.where(row < 2, pltpu.roll(behind, 6, 0), pltpu.roll(top, 2, 0))
             top = weights[0:1] * top + weights[1:2] * one + weights[2:3] * two
 
-            convolved = conv_ref[owner].astype(jnp.float32)
+            source = 2 * lax.rem(owner, places) + lax.div(owner, places)
+            convolved = conv_ref[source].astype(jnp.float32)
             top = top * convolved[:SUBLANES] + top * (gain_ref[:, lanes] * product)
             result = short_ref[owner] * convolved + direct_ref[owner]
             result = jnp.concatenate([top, result[SUBLANES:]], axis=0)
@@ -217,7 +218,7 @@
     chunks = max(1, channels // 512)
     here = pl.BlockSpec(memory_space=pltpu.VMEM)
     return pl.pallas_call(
-        finish_kernel,
+        functools.partial(finish_kernel, sent.shape[0] // 2),
         out_shape=jax.ShapeDtypeStruct((rows, channels), jnp.bfloat16),
         in_specs=[here] * 8,
         out_specs=pl.BlockSpec(memory_space=pltpu.HBM),
@@ -577,7 +578,7 @@
         result = (partly[step] + backward(1, step)).astype(ready.dtype)
         for part in range(2):
             for offset in range(near):
-                ready[part * places + step * near + offset] = result[
+                ready[2 * (step * near + offset) + part] = result[
                     offset * rows : (offset + 1) * rows, part * LANES : (part + 1) * LANES
                 ]
 
@@ -658,7 +659,7 @@
         convolved = convolve_whole(
             received, short_weight, owner, rows, forward_table, inverse_table
         )
-        convolved = exchange(convolved, ("groups", "seq"))
+        convolved = exchange(convolved, ("seq", "groups"))
         return finish(
             convolved, prepared, sent, query_in, edges, short_weight, skip_gain
         )

time: 87 us -> 86.2 us (level)
  blocking collectives: 29.3 us -> 28.3 us
    all_to_all x1, blocking collectives: 29.3 us -> 28.3 us  [exchange(): return lax.all_to_all(value, axes, split_axis=0, concat_axis=0, tiled=True)]
where the time goes in v9:
time: 86.2 us; the launch traced here: 85.8 us
  waiting for transfers between devices  33 us (38%)
  blocking collectives  28.3 us (33%)
  Pallas kernels  14.7 us (17%)
  starting transfers between devices  9.59 us (11%)
    all_to_all x1, waiting for transfers between devices, exchange(): return lax.all_to_all(value, axes, split_axis=0, concat_axis=0, tiled=True)  33 us
    all_to_all x1, blocking collectives, exchange(): return lax.all_to_all(value, axes, split_axis=0, concat_axis=0, tiled=True)  28.3 us
    all_to_all x1, starting transfers between devices, exchange(): return lax.all_to_all(value, axes, split_axis=0, concat_axis=0, tiled=True)  7.3 us
    pallas_call x1, Pallas kernels, convolve_whole(): pl.pallas_call(whole_kernel, out_shape=jax.ShapeDtypeStruct((senders, row...  4.91 us
    pallas_call x1, Pallas kernels, prepare(): pl.pallas_call(prepare_kernel, out_shape=(jax.ShapeDtypeStruct((owners, r...  4.68 us
    pallas_call x1, Pallas kernels, pack(): pl.pallas_call(pack_kernel, out_shape=(jax.ShapeDtypeStruct((owners, heig...  3.67 us
    ppermute x1, starting transfers between devices, from_behind(): lax.ppermute(value, axis, [(source, source + 1) for source in range(count...  2.29 us
  transfers between devices with their start and end apart: 2, of which 1 were waited for; matrix products, arithmetic and copies ran while one was open for 0% of the time, Pallas kernels for 5%

profile of v9, /device:TPU:0, one launch (start us, length us, event | category | flops | bytes accessed | tf_op | source)
XLA Modules:
  0.0 85.8 jit_solution(4401234902430243676)
XLA Ops:
  0.0 3.7 %shard_map.82 = (bf16[32,200,128]{2,1,0:T(8,128)(2,1)}, bf16[8,4096]{1,0:T(8,128)(2,1)}) custom-call(s32[1]{0:T(128)} %bitcast.1.group_ref, bf16[128,4096]{1,0:T(8,128)(2,1)} %query_ref.5, bf16[128,4096]{1,0:T(8,128)(2,1)} %key_ref.1, bf16[128,4096]{1,0:T(8,128)(2,1)} %value_ref.1, bf16[128,4096]{1,0:T(8,128)(2,1)} %filter_ref.1, f32[3,3,4096]{2,1,0:T(4,128)} %taps_ref.7), custom_call_target="tpu_custom_call" | custom-call | flops 6291456 | bytes 4194304 | tf_op jit(solution)/shard_map/pallas_call | solution.py:341
  3.7 0.0 copy-start.8
  3.7 7.3 %all-to-all-start = ((bf16[32,200,128]{2,1,0:T(8,128)(2,1)}), bf16[32,200,128]{2,1,0:T(8,128)(2,1)S(1)}, u32[]{:S(2)}, u32[]{:S(2)}) async-start(bf16[32,200,128]{2,1,0:T(8,128)(2,1)} %get-tuple-element.13.sent_ref), calls=%async_computation | async-start | bytes 3276800 | tf_op jit(solution)/shard_map/all_to_all | solution.py:624
  11.0 0.0 copy-start.4
  11.0 0.0 copy-start.6
  11.0 0.0 copy-start.7
  11.0 0.0 copy-done.8
  11.0 2.3 %collective-permute-start = (bf16[8,4096]{1,0:T(8,128)(2,1)S(1)}, bf16[8,4096]{1,0:T(8,128)(2,1)S(1)}, u32[]{:S(2)}, u32[]{:S(2)}) collective-permute-start(bf16[8,4096]{1,0:T(8,128)(2,1)S(1)} %copy-done.8), channel_id=1, source_target_pairs={{0,1},{1,2},{2,3},{3,4},{4,5},{5,6},{6,7},{7,8},{8,9},{9,10},{10,1... | collective-permute-start | bytes 196616 | tf_op jit(solution)/shard_map/ppermute | solution.py:21
  13.4 4.7 %shard_map.83 = (f32[32,128,128]{2,1,0:T(8,128)}, f32[32,128,128]{2,1,0:T(8,128)}) custom-call(bf16[32,200,128]{2,1,0:T(8,128)(2,1)} %get-tuple-element.13.sent_ref, bf16[128,4096]{1,0:T(8,128)(2,1)} %query_ref.5, f32[3,3,4096]{2,1,0:T(4,128)} %taps_ref.7, f32[1,4096]{1,0:T(1,128)} %bitcast.3), custom_call_target="tpu_custom_call" | custom-call | flops 4194304 | bytes 6291456 | tf_op jit(solution)/shard_map/pallas_call | solution.py:154
  18.0 0.0 collective-permute-done.edge_ref
  18.0 33.0 %all-to-all-done.arrived = bf16[32,200,128]{2,1,0:T(8,128)(2,1)S(1)} async-done(((bf16[32,200,128]{2,1,0:T(8,128)(2,1)}), bf16[32,200,128]{2,1,0:T(8,128)(2,1)S(1)}, u32[]{:S(2)}, u32[]{:S(2)}) %all-to-all-start) | async-done | bytes 1638432 | tf_op jit(solution)/shard_map/all_to_all | solution.py:624
  51.1 0.0 copy-done.4
  51.1 0.0 copy-done.6
  51.1 0.0 copy-done.7
  51.1 0.0 copy-start.1
  51.1 0.0 copy-start.2
  51.1 0.0 copy-start.3
  51.1 4.9 %shard_map.84 = bf16[32,128,128]{2,1,0:T(8,128)(2,1)S(1)} custom-call(s32[1]{0:T(128)} %bitcast.owner_ref, bf16[2,512,256]{2,1,0:T(8,128)(2,1)S(1)} %copy-done.7, bf16[2,512,256]{2,1,0:T(8,128)(2,1)S(1)} %copy-done.6, f32[3,3,4096]{2,1,0:T(4,128)S(1)} %copy-done.4, bf16[32,200,128]{2,1,0:T(8,128)(2,1)S(1)} %all-to-all-done.arrived), custom_call_target="tpu_custom_call" | custom-call | flops 2684354560 | bytes 2686976 | tf_op jit(solution)/shard_map/pallas_call | solution.py:592
  56.0 0.0 copy-start
  56.0 0.0 copy-start.5
  56.1 28.3 %all_to_all.10.conv_ref = bf16[32,128,128]{2,1,0:T(8,128)(2,1)S(1)} all-to-all(bf16[32,128,128]{2,1,0:T(8,128)(2,1)S(1)} %shard_map.84), channel_id=1, replica_groups=mesh['groups'=2,'seq'=16] {'seq','groups'}, dimensions={0} | all-to-all | bytes 2097152 | tf_op jit(solution)/shard_map/all_to_all | solution.py:624
  84.4 0.0 copy-done.1
  84.4 0.0 copy-done.2
  84.4 0.0 copy-done.3
  84.4 0.0 copy-done
  84.4 0.0 copy-done.5
  84.4 1.4 %shard_map.85 = bf16[128,4096]{1,0:T(8,128)(2,1)} custom-call(bf16[32,128,128]{2,1,0:T(8,128)(2,1)S(1)} %all_to_all.10.conv_ref, f32[32,128,128]{2,1,0:T(8,128)S(1)} %copy-done.2, f32[32,128,128]{2,1,0:T(8,128)S(1)} %copy-done.3, bf16[32,200,128]{2,1,0:T(8,128)(2,1)S(1)} %copy-done, bf16[128,4096]{1,0:T(8,128)(2,1)S(1)} %copy-done.1, ...), custom_call_target="tpu_custom_call" | custom-call | flops 1572864 | bytes 6291456 | tf_op jit(solution)/shard_map/pallas_call | solution.py:220
Async XLA Ops:
  3.7 7.4 %copy-start.8 = (bf16[8,4096]{1,0:T(8,128)(2,1)S(1)}, bf16[8,4096]{1,0:T(8,128)(2,1)}, u32[]{:S(2)}) copy-start(bf16[8,4096]{1,0:T(8,128)(2,1)} %get-tuple-element.14) | copy-start | bytes 196612
  3.7 47.4 %all-to-all-start = ((bf16[32,200,128]{2,1,0:T(8,128)(2,1)}), bf16[32,200,128]{2,1,0:T(8,128)(2,1)S(1)}, u32[]{:S(2)}, u32[]{:S(2)}) async-start(bf16[32,200,128]{2,1,0:T(8,128)(2,1)} %get-tuple-element.13.sent_ref), calls=%async_computation | async-start | bytes 3276800 | tf_op jit(solution)/shard_map/all_to_all | solution.py:624
  11.0 40.1 %copy-start.4 = (f32[3,3,4096]{2,1,0:T(4,128)S(1)}, f32[3,3,4096]{2,1,0:T(4,128)}, u32[]{:S(2)}) copy-start(f32[3,3,4096]{2,1,0:T(4,128)} %taps_ref.7) | copy-start | bytes 442372
  11.0 40.1 %copy-start.6 = (bf16[2,512,256]{2,1,0:T(8,128)(2,1)S(1)}, bf16[2,512,256]{2,1,0:T(8,128)(2,1)}, u32[]{:S(2)}) copy-start(bf16[2,512,256]{2,1,0:T(8,128)(2,1)} %constant.16.clone.inverse_ref) | copy-start | bytes 1572868
  11.0 40.1 %copy-start.7 = (bf16[2,512,256]{2,1,0:T(8,128)(2,1)S(1)}, bf16[2,512,256]{2,1,0:T(8,128)(2,1)}, u32[]{:S(2)}) copy-start(bf16[2,512,256]{2,1,0:T(8,128)(2,1)} %constant.15.clone.forward_ref) | copy-start | bytes 1572868
  11.0 7.0 %collective-permute-start = (bf16[8,4096]{1,0:T(8,128)(2,1)S(1)}, bf16[8,4096]{1,0:T(8,128)(2,1)S(1)}, u32[]{:S(2)}, u32[]{:S(2)}) collective-permute-start(bf16[8,4096]{1,0:T(8,128)(2,1)S(1)} %copy-done.8), channel_id=1, source_target_pairs={{0,1},{1,2},{2,3},{3,4},{4,5},{5,6},{6,7},{7,8},{8,9},{9,10},{10,1... | collective-permute-start | bytes 196616 | tf_op jit(solution)/shard_map/ppermute | solution.py:21
  51.1 33.3 %copy-start.1 = (bf16[128,4096]{1,0:T(8,128)(2,1)S(1)}, bf16[128,4096]{1,0:T(8,128)(2,1)}, u32[]{:S(2)}) copy-start(bf16[128,4096]{1,0:T(8,128)(2,1)} %query_ref.5) | copy-start | bytes 3145732
  51.1 33.3 %copy-start.2 = (f32[32,128,128]{2,1,0:T(8,128)S(1)}, f32[32,128,128]{2,1,0:T(8,128)}, u32[]{:S(2)}) copy-start(f32[32,128,128]{2,1,0:T(8,128)} %get-tuple-element.18.short_ref) | copy-start | bytes 6291460
  51.1 33.3 %copy-start.3 = (f32[32,128,128]{2,1,0:T(8,128)S(1)}, f32[32,128,128]{2,1,0:T(8,128)}, u32[]{:S(2)}) copy-start(f32[32,128,128]{2,1,0:T(8,128)} %get-tuple-element.19.direct_ref) | copy-start | bytes 6291460
  56.0 28.4 %copy-start = (bf16[32,200,128]{2,1,0:T(8,128)(2,1)S(1)}, bf16[32,200,128]{2,1,0:T(8,128)(2,1)}, u32[]{:S(2)}) copy-start(bf16[32,200,128]{2,1,0:T(8,128)(2,1)} %get-tuple-element.13.sent_ref) | copy-start | bytes 4915204
  56.0 28.4 %copy-start.5 = (f32[4096]{0:T(1024)S(1)}, f32[4096]{0:T(1024)}, u32[]{:S(2)}) copy-start(f32[4096]{0:T(1024)} %param.13) | copy-start | bytes 49156

commit v10 on v9

--- a/solution.py
+++ b/solution.py
@@ -201,7 +201,7 @@
             two = jnp.where(row < 2, pltpu.roll(behind, 6, 0), pltpu.roll(top, 2, 0))
             top = weights[0:1] * top + weights[1:2] * one + weights[2:3] * two
 
-            source = 2 * lax.rem(owner, places) + lax.div(owner, places)
+            source = 2 * owner - jnp.where(owner >= places, 2 * places - 1, 0)
             convolved = conv_ref[source].astype(jnp.float32)
             top = top * convolved[:SUBLANES] + top * (gain_ref[:, lanes] * product)
             result = short_ref[owner] * convolved + direct_ref[owner]

time: 86.2 us -> 86.2 us (level)
  no operation moved by 1% of the time
where the time goes in v10:
time: 86.2 us; the launch traced here: 85.8 us
  waiting for transfers between devices  33 us (38%)
  blocking collectives  28.3 us (33%)
  Pallas kernels  14.6 us (17%)
  starting transfers between devices  9.59 us (11%)
    all_to_all x1, waiting for transfers between devices, exchange(): return lax.all_to_all(value, axes, split_axis=0, concat_axis=0, tiled=True)  33 us
    all_to_all x1, blocking collectives, exchange(): return lax.all_to_all(value, axes, split_axis=0, concat_axis=0, tiled=True)  28.3 us
    all_to_all x1, starting transfers between devices, exchange(): return lax.all_to_all(value, axes, split_axis=0, concat_axis=0, tiled=True)  7.3 us
    pallas_call x1, Pallas kernels, convolve_whole(): pl.pallas_call(whole_kernel, out_shape=jax.ShapeDtypeStruct((senders, row...  4.91 us
    pallas_call x1, Pallas kernels, prepare(): pl.pallas_call(prepare_kernel, out_shape=(jax.ShapeDtypeStruct((owners, r...  4.68 us
    pallas_call x1, Pallas kernels, pack(): pl.pallas_call(pack_kernel, out_shape=(jax.ShapeDtypeStruct((owners, heig...  3.67 us
    ppermute x1, starting transfers between devices, from_behind(): lax.ppermute(value, axis, [(source, source + 1) for source in range(count...  2.29 us
  transfers between devices with their start and end apart: 2, of which 1 were waited for; matrix products, arithmetic and copies ran while one was open for 0% of the time, Pallas kernels for 5%

profile of v10, /device:TPU:0, one launch (start us, length us, event | category | flops | bytes accessed | tf_op | source)
XLA Modules:
  0.0 85.8 jit_solution(13964093348684818500)
XLA Ops:
  0.0 3.7 %shard_map.82 = (bf16[32,200,128]{2,1,0:T(8,128)(2,1)}, bf16[8,4096]{1,0:T(8,128)(2,1)}) custom-call(s32[1]{0:T(128)} %bitcast.1.group_ref, bf16[128,4096]{1,0:T(8,128)(2,1)} %query_ref.5, bf16[128,4096]{1,0:T(8,128)(2,1)} %key_ref.1, bf16[128,4096]{1,0:T(8,128)(2,1)} %value_ref.1, bf16[128,4096]{1,0:T(8,128)(2,1)} %filter_ref.1, f32[3,3,4096]{2,1,0:T(4,128)} %taps_ref.7), custom_call_target="tpu_custom_call" | custom-call | flops 6291456 | bytes 4194304 | tf_op jit(solution)/shard_map/pallas_call | solution.py:341
  3.7 0.0 copy-start.8
  3.7 7.3 %all-to-all-start = ((bf16[32,200,128]{2,1,0:T(8,128)(2,1)}), bf16[32,200,128]{2,1,0:T(8,128)(2,1)S(1)}, u32[]{:S(2)}, u32[]{:S(2)}) async-start(bf16[32,200,128]{2,1,0:T(8,128)(2,1)} %get-tuple-element.13.sent_ref), calls=%async_computation | async-start | bytes 3276800 | tf_op jit(solution)/shard_map/all_to_all | solution.py:624
  11.0 0.0 copy-start.4
  11.0 0.0 copy-start.6
  11.0 0.0 copy-start.7
  11.0 0.0 copy-done.8
  11.0 2.3 %collective-permute-start = (bf16[8,4096]{1,0:T(8,128)(2,1)S(1)}, bf16[8,4096]{1,0:T(8,128)(2,1)S(1)}, u32[]{:S(2)}, u32[]{:S(2)}) collective-permute-start(bf16[8,4096]{1,0:T(8,128)(2,1)S(1)} %copy-done.8), channel_id=1, source_target_pairs={{0,1},{1,2},{2,3},{3,4},{4,5},{5,6},{6,7},{7,8},{8,9},{9,10},{10,1... | collective-permute-start | bytes 196616 | tf_op jit(solution)/shard_map/ppermute | solution.py:21
  13.4 4.7 %shard_map.83 = (f32[32,128,128]{2,1,0:T(8,128)}, f32[32,128,128]{2,1,0:T(8,128)}) custom-call(bf16[32,200,128]{2,1,0:T(8,128)(2,1)} %get-tuple-element.13.sent_ref, bf16[128,4096]{1,0:T(8,128)(2,1)} %query_ref.5, f32[3,3,4096]{2,1,0:T(4,128)} %taps_ref.7, f32[1,4096]{1,0:T(1,128)} %bitcast.3), custom_call_target="tpu_custom_call" | custom-call | flops 4194304 | bytes 6291456 | tf_op jit(solution)/shard_map/pallas_call | solution.py:154
  18.0 0.0 collective-permute-done.edge_ref
  18.0 33.0 %all-to-all-done.arrived = bf16[32,200,128]{2,1,0:T(8,128)(2,1)S(1)} async-done(((bf16[32,200,128]{2,1,0:T(8,128)(2,1)}), bf16[32,200,128]{2,1,0:T(8,128)(2,1)S(1)}, u32[]{:S(2)}, u32[]{:S(2)}) %all-to-all-start) | async-done | bytes 1638432 | tf_op jit(solution)/shard_map/all_to_all | solution.py:624
  51.1 0.0 copy-done.4
  51.1 0.0 copy-done.6
  51.1 0.0 copy-done.7
  51.1 0.0 copy-start.1
  51.1 0.0 copy-start.2
  51.1 0.0 copy-start.3
  51.1 4.9 %shard_map.84 = bf16[32,128,128]{2,1,0:T(8,128)(2,1)S(1)} custom-call(s32[1]{0:T(128)} %bitcast.owner_ref, bf16[2,512,256]{2,1,0:T(8,128)(2,1)S(1)} %copy-done.7, bf16[2,512,256]{2,1,0:T(8,128)(2,1)S(1)} %copy-done.6, f32[3,3,4096]{2,1,0:T(4,128)S(1)} %copy-done.4, bf16[32,200,128]{2,1,0:T(8,128)(2,1)S(1)} %all-to-all-done.arrived), custom_call_target="tpu_custom_call" | custom-call | flops 2684354560 | bytes 2686976 | tf_op jit(solution)/shard_map/pallas_call | solution.py:592
  56.0 0.0 copy-start
  56.0 0.0 copy-start.5
  56.1 28.3 %all_to_all.10.conv_ref = bf16[32,128,128]{2,1,0:T(8,128)(2,1)S(1)} all-to-all(bf16[32,128,128]{2,1,0:T(8,128)(2,1)S(1)} %shard_map.84), channel_id=1, replica_groups=mesh['groups'=2,'seq'=16] {'seq','groups'}, dimensions={0} | all-to-all | bytes 2097152 | tf_op jit(solution)/shard_map/all_to_all | solution.py:624
  84.4 0.0 copy-done.1
  84.4 0.0 copy-done.2
  84.4 0.0 copy-done.3
  84.4 0.0 copy-done
  84.4 0.0 copy-done.5
  84.4 1.4 %shard_map.85 = bf16[128,4096]{1,0:T(8,128)(2,1)} custom-call(bf16[32,128,128]{2,1,0:T(8,128)(2,1)S(1)} %all_to_all.10.conv_ref, f32[32,128,128]{2,1,0:T(8,128)S(1)} %copy-done.2, f32[32,128,128]{2,1,0:T(8,128)S(1)} %copy-done.3, bf16[32,200,128]{2,1,0:T(8,128)(2,1)S(1)} %copy-done, bf16[128,4096]{1,0:T(8,128)(2,1)S(1)} %copy-done.1, ...), custom_call_target="tpu_custom_call" | custom-call | flops 1572864 | bytes 6291456 | tf_op jit(solution)/shard_map/pallas_call | solution.py:220
Async XLA Ops:
  3.7 7.4 %copy-start.8 = (bf16[8,4096]{1,0:T(8,128)(2,1)S(1)}, bf16[8,4096]{1,0:T(8,128)(2,1)}, u32[]{:S(2)}) copy-start(bf16[8,4096]{1,0:T(8,128)(2,1)} %get-tuple-element.14) | copy-start | bytes 196612
  3.7 47.4 %all-to-all-start = ((bf16[32,200,128]{2,1,0:T(8,128)(2,1)}), bf16[32,200,128]{2,1,0:T(8,128)(2,1)S(1)}, u32[]{:S(2)}, u32[]{:S(2)}) async-start(bf16[32,200,128]{2,1,0:T(8,128)(2,1)} %get-tuple-element.13.sent_ref), calls=%async_computation | async-start | bytes 3276800 | tf_op jit(solution)/shard_map/all_to_all | solution.py:624
  11.0 40.1 %copy-start.4 = (f32[3,3,4096]{2,1,0:T(4,128)S(1)}, f32[3,3,4096]{2,1,0:T(4,128)}, u32[]{:S(2)}) copy-start(f32[3,3,4096]{2,1,0:T(4,128)} %taps_ref.7) | copy-start | bytes 442372
  11.0 40.1 %copy-start.6 = (bf16[2,512,256]{2,1,0:T(8,128)(2,1)S(1)}, bf16[2,512,256]{2,1,0:T(8,128)(2,1)}, u32[]{:S(2)}) copy-start(bf16[2,512,256]{2,1,0:T(8,128)(2,1)} %constant.16.clone.inverse_ref) | copy-start | bytes 1572868
  11.0 40.1 %copy-start.7 = (bf16[2,512,256]{2,1,0:T(8,128)(2,1)S(1)}, bf16[2,512,256]{2,1,0:T(8,128)(2,1)}, u32[]{:S(2)}) copy-start(bf16[2,512,256]{2,1,0:T(8,128)(2,1)} %constant.15.clone.forward_ref) | copy-start | bytes 1572868
  11.0 7.0 %collective-permute-start = (bf16[8,4096]{1,0:T(8,128)(2,1)S(1)}, bf16[8,4096]{1,0:T(8,128)(2,1)S(1)}, u32[]{:S(2)}, u32[]{:S(2)}) collective-permute-start(bf16[8,4096]{1,0:T(8,128)(2,1)S(1)} %copy-done.8), channel_id=1, source_target_pairs={{0,1},{1,2},{2,3},{3,4},{4,5},{5,6},{6,7},{7,8},{8,9},{9,10},{10,1... | collective-permute-start | bytes 196616 | tf_op jit(solution)/shard_map/ppermute | solution.py:21
  51.1 33.3 %copy-start.1 = (bf16[128,4096]{1,0:T(8,128)(2,1)S(1)}, bf16[128,4096]{1,0:T(8,128)(2,1)}, u32[]{:S(2)}) copy-start(bf16[128,4096]{1,0:T(8,128)(2,1)} %query_ref.5) | copy-start | bytes 3145732
  51.1 33.3 %copy-start.2 = (f32[32,128,128]{2,1,0:T(8,128)S(1)}, f32[32,128,128]{2,1,0:T(8,128)}, u32[]{:S(2)}) copy-start(f32[32,128,128]{2,1,0:T(8,128)} %get-tuple-element.18.short_ref) | copy-start | bytes 6291460
  51.1 33.3 %copy-start.3 = (f32[32,128,128]{2,1,0:T(8,128)S(1)}, f32[32,128,128]{2,1,0:T(8,128)}, u32[]{:S(2)}) copy-start(f32[32,128,128]{2,1,0:T(8,128)} %get-tuple-element.19.direct_ref) | copy-start | bytes 6291460
  56.0 28.4 %copy-start = (bf16[32,200,128]{2,1,0:T(8,128)(2,1)S(1)}, bf16[32,200,128]{2,1,0:T(8,128)(2,1)}, u32[]{:S(2)}) copy-start(bf16[32,200,128]{2,1,0:T(8,128)(2,1)} %get-tuple-element.13.sent_ref) | copy-start | bytes 4915204
  56.0 28.4 %copy-start.5 = (f32[4096]{0:T(1024)S(1)}, f32[4096]{0:T(1024)}, u32[]{:S(2)}) copy-start(f32[4096]{0:T(1024)} %param.13) | copy-start | bytes 49156

commit v11 on v10

--- a/solution.py
+++ b/solution.py
@@ -289,7 +289,7 @@
         copy.start()
     for chunk in range(chunks):
         for copy in arrivals(chunk):
-            copy.start(priority=1)
+            copy.start(priority=1 if chunk else 0)
     for copy in whole:
         copy.wait()
     row = lax.broadcasted_iota(jnp.int32, (SUBLANES, LANES), 0)

time: 86.2 us -> 86.1 us (level)
  no operation moved by 1% of the time
where the time goes in v11:
time: 86.1 us; the launch traced here: 85.8 us
  waiting for transfers between devices  33 us (38%)
  blocking collectives  28.3 us (33%)
  Pallas kernels  14.6 us (17%)
  starting transfers between devices  9.59 us (11%)
    all_to_all x1, waiting for transfers between devices, exchange(): return lax.all_to_all(value, axes, split_axis=0, concat_axis=0, tiled=True)  33 us
    all_to_all x1, blocking collectives, exchange(): return lax.all_to_all(value, axes, split_axis=0, concat_axis=0, tiled=True)  28.3 us
    all_to_all x1, starting transfers between devices, exchange(): return lax.all_to_all(value, axes, split_axis=0, concat_axis=0, tiled=True)  7.3 us
    pallas_call x1, Pallas kernels, convolve_whole(): pl.pallas_call(whole_kernel, out_shape=jax.ShapeDtypeStruct((senders, row...  4.91 us
    pallas_call x1, Pallas kernels, prepare(): pl.pallas_call(prepare_kernel, out_shape=(jax.ShapeDtypeStruct((owners, r...  4.68 us
    pallas_call x1, Pallas kernels, pack(): pl.pallas_call(pack_kernel, out_shape=(jax.ShapeDtypeStruct((owners, heig...  3.62 us
    ppermute x1, starting transfers between devices, from_behind(): lax.ppermute(value, axis, [(source, source + 1) for source in range(count...  2.29 us
  transfers between devices with their start and end apart: 2, of which 1 were waited for; matrix products, arithmetic and copies ran while one was open for 0% of the time, Pallas kernels for 5%

profile of v11, /device:TPU:0, one launch (start us, length us, event | category | flops | bytes accessed | tf_op | source)
XLA Modules:
  0.0 85.8 jit_solution(1151740427284264419)
XLA Ops:
  0.0 3.6 %shard_map.82 = (bf16[32,200,128]{2,1,0:T(8,128)(2,1)}, bf16[8,4096]{1,0:T(8,128)(2,1)}) custom-call(s32[1]{0:T(128)} %bitcast.1.group_ref, bf16[128,4096]{1,0:T(8,128)(2,1)} %query_ref.5, bf16[128,4096]{1,0:T(8,128)(2,1)} %key_ref.1, bf16[128,4096]{1,0:T(8,128)(2,1)} %value_ref.1, bf16[128,4096]{1,0:T(8,128)(2,1)} %filter_ref.1, f32[3,3,4096]{2,1,0:T(4,128)} %taps_ref.7), custom_call_target="tpu_custom_call" | custom-call | flops 6291456 | bytes 4194304 | tf_op jit(solution)/shard_map/pallas_call | solution.py:341
  3.6 0.0 copy-start.8
  3.6 7.3 %all-to-all-start = ((bf16[32,200,128]{2,1,0:T(8,128)(2,1)}), bf16[32,200,128]{2,1,0:T(8,128)(2,1)S(1)}, u32[]{:S(2)}, u32[]{:S(2)}) async-start(bf16[32,200,128]{2,1,0:T(8,128)(2,1)} %get-tuple-element.13.sent_ref), calls=%async_computation | async-start | bytes 3276800 | tf_op jit(solution)/shard_map/all_to_all | solution.py:624
  10.9 0.0 copy-start.4
  11.0 0.0 copy-start.6
  11.0 0.0 copy-start.7
  11.0 0.0 copy-done.8
  11.0 2.3 %collective-permute-start = (bf16[8,4096]{1,0:T(8,128)(2,1)S(1)}, bf16[8,4096]{1,0:T(8,128)(2,1)S(1)}, u32[]{:S(2)}, u32[]{:S(2)}) collective-permute-start(bf16[8,4096]{1,0:T(8,128)(2,1)S(1)} %copy-done.8), channel_id=1, source_target_pairs={{0,1},{1,2},{2,3},{3,4},{4,5},{5,6},{6,7},{7,8},{8,9},{9,10},{10,1... | collective-permute-start | bytes 196616 | tf_op jit(solution)/shard_map/ppermute | solution.py:21
  13.3 4.7 %shard_map.83 = (f32[32,128,128]{2,1,0:T(8,128)}, f32[32,128,128]{2,1,0:T(8,128)}) custom-call(bf16[32,200,128]{2,1,0:T(8,128)(2,1)} %get-tuple-element.13.sent_ref, bf16[128,4096]{1,0:T(8,128)(2,1)} %query_ref.5, f32[3,3,4096]{2,1,0:T(4,128)} %taps_ref.7, f32[1,4096]{1,0:T(1,128)} %bitcast.3), custom_call_target="tpu_custom_call" | custom-call | flops 4194304 | bytes 6291456 | tf_op jit(solution)/shard_map/pallas_call | solution.py:154
  18.0 0.0 collective-permute-done.edge_ref
  18.0 33.0 %all-to-all-done.arrived = bf16[32,200,128]{2,1,0:T(8,128)(2,1)S(1)} async-done(((bf16[32,200,128]{2,1,0:T(8,128)(2,1)}), bf16[32,200,128]{2,1,0:T(8,128)(2,1)S(1)}, u32[]{:S(2)}, u32[]{:S(2)}) %all-to-all-start) | async-done | bytes 1638432 | tf_op jit(solution)/shard_map/all_to_all | solution.py:624
  51.0 0.0 copy-done.4
  51.0 0.0 copy-done.6
  51.0 0.0 copy-done.7
  51.0 0.0 copy-start.1
  51.0 0.0 copy-start.2
  51.1 0.0 copy-start.3
  51.1 4.9 %shard_map.84 = bf16[32,128,128]{2,1,0:T(8,128)(2,1)S(1)} custom-call(s32[1]{0:T(128)} %bitcast.owner_ref, bf16[2,512,256]{2,1,0:T(8,128)(2,1)S(1)} %copy-done.7, bf16[2,512,256]{2,1,0:T(8,128)(2,1)S(1)} %copy-done.6, f32[3,3,4096]{2,1,0:T(4,128)S(1)} %copy-done.4, bf16[32,200,128]{2,1,0:T(8,128)(2,1)S(1)} %all-to-all-done.arrived), custom_call_target="tpu_custom_call" | custom-call | flops 2684354560 | bytes 2686976 | tf_op jit(solution)/shard_map/pallas_call | solution.py:592
  56.0 0.0 copy-start
  56.0 0.0 copy-start.5
  56.0 28.3 %all_to_all.10.conv_ref = bf16[32,128,128]{2,1,0:T(8,128)(2,1)S(1)} all-to-all(bf16[32,128,128]{2,1,0:T(8,128)(2,1)S(1)} %shard_map.84), channel_id=1, replica_groups=mesh['groups'=2,'seq'=16] {'seq','groups'}, dimensions={0} | all-to-all | bytes 2097152 | tf_op jit(solution)/shard_map/all_to_all | solution.py:624
  84.3 0.0 copy-done.1
  84.3 0.0 copy-done.2
  84.3 0.0 copy-done.3
  84.3 0.0 copy-done
  84.4 0.0 copy-done.5
  84.4 1.4 %shard_map.85 = bf16[128,4096]{1,0:T(8,128)(2,1)} custom-call(bf16[32,128,128]{2,1,0:T(8,128)(2,1)S(1)} %all_to_all.10.conv_ref, f32[32,128,128]{2,1,0:T(8,128)S(1)} %copy-done.2, f32[32,128,128]{2,1,0:T(8,128)S(1)} %copy-done.3, bf16[32,200,128]{2,1,0:T(8,128)(2,1)S(1)} %copy-done, bf16[128,4096]{1,0:T(8,128)(2,1)S(1)} %copy-done.1, ...), custom_call_target="tpu_custom_call" | custom-call | flops 1572864 | bytes 6291456 | tf_op jit(solution)/shard_map/pallas_call | solution.py:220
Async XLA Ops:
  3.6 7.4 %copy-start.8 = (bf16[8,4096]{1,0:T(8,128)(2,1)S(1)}, bf16[8,4096]{1,0:T(8,128)(2,1)}, u32[]{:S(2)}) copy-start(bf16[8,4096]{1,0:T(8,128)(2,1)} %get-tuple-element.14) | copy-start | bytes 196612
  3.6 47.4 %all-to-all-start = ((bf16[32,200,128]{2,1,0:T(8,128)(2,1)}), bf16[32,200,128]{2,1,0:T(8,128)(2,1)S(1)}, u32[]{:S(2)}, u32[]{:S(2)}) async-start(bf16[32,200,128]{2,1,0:T(8,128)(2,1)} %get-tuple-element.13.sent_ref), calls=%async_computation | async-start | bytes 3276800 | tf_op jit(solution)/shard_map/all_to_all | solution.py:624
  10.9 40.1 %copy-start.4 = (f32[3,3,4096]{2,1,0:T(4,128)S(1)}, f32[3,3,4096]{2,1,0:T(4,128)}, u32[]{:S(2)}) copy-start(f32[3,3,4096]{2,1,0:T(4,128)} %taps_ref.7) | copy-start | bytes 442372
  11.0 40.1 %copy-start.6 = (bf16[2,512,256]{2,1,0:T(8,128)(2,1)S(1)}, bf16[2,512,256]{2,1,0:T(8,128)(2,1)}, u32[]{:S(2)}) copy-start(bf16[2,512,256]{2,1,0:T(8,128)(2,1)} %constant.16.clone.inverse_ref) | copy-start | bytes 1572868
  11.0 40.1 %copy-start.7 = (bf16[2,512,256]{2,1,0:T(8,128)(2,1)S(1)}, bf16[2,512,256]{2,1,0:T(8,128)(2,1)}, u32[]{:S(2)}) copy-start(bf16[2,512,256]{2,1,0:T(8,128)(2,1)} %constant.15.clone.forward_ref) | copy-start | bytes 1572868
  11.0 7.0 %collective-permute-start = (bf16[8,4096]{1,0:T(8,128)(2,1)S(1)}, bf16[8,4096]{1,0:T(8,128)(2,1)S(1)}, u32[]{:S(2)}, u32[]{:S(2)}) collective-permute-start(bf16[8,4096]{1,0:T(8,128)(2,1)S(1)} %copy-done.8), channel_id=1, source_target_pairs={{0,1},{1,2},{2,3},{3,4},{4,5},{5,6},{6,7},{7,8},{8,9},{9,10},{10,1... | collective-permute-start | bytes 196616 | tf_op jit(solution)/shard_map/ppermute | solution.py:21
  51.0 33.3 %copy-start.1 = (bf16[128,4096]{1,0:T(8,128)(2,1)S(1)}, bf16[128,4096]{1,0:T(8,128)(2,1)}, u32[]{:S(2)}) copy-start(bf16[128,4096]{1,0:T(8,128)(2,1)} %query_ref.5) | copy-start | bytes 3145732
  51.0 33.3 %copy-start.2 = (f32[32,128,128]{2,1,0:T(8,128)S(1)}, f32[32,128,128]{2,1,0:T(8,128)}, u32[]{:S(2)}) copy-start(f32[32,128,128]{2,1,0:T(8,128)} %get-tuple-element.18.short_ref) | copy-start | bytes 6291460
  51.1 33.3 %copy-start.3 = (f32[32,128,128]{2,1,0:T(8,128)S(1)}, f32[32,128,128]{2,1,0:T(8,128)}, u32[]{:S(2)}) copy-start(f32[32,128,128]{2,1,0:T(8,128)} %get-tuple-element.19.direct_ref) | copy-start | bytes 6291460
  56.0 28.4 %copy-start = (bf16[32,200,128]{2,1,0:T(8,128)(2,1)S(1)}, bf16[32,200,128]{2,1,0:T(8,128)(2,1)}, u32[]{:S(2)}) copy-start(bf16[32,200,128]{2,1,0:T(8,128)(2,1)} %get-tuple-element.13.sent_ref) | copy-start | bytes 4915204
  56.0 28.4 %copy-start.5 = (f32[4096]{0:T(1024)S(1)}, f32[4096]{0:T(1024)}, u32[]{:S(2)}) copy-start(f32[4096]{0:T(1024)} %param.13) | copy-start | bytes 49156
